TPU v7x, 256 devices: a whole 4x4x8 slice. The times are simulated.
256 devices in a mesh: space: 64 (over x, z, core), chan: 4 (over y).
Axes of the slice: x: 4, y: 4, z: 8, core: 2. Of those that a mesh axis runs over, the one named last changes fastest.
Arguments:
- features: bfloat16 [8192, 512], P('space', 'chan'), may hold values from -6 to 6
- mask: int32 [8192], P('space'), may hold values 0 or 1
- rulebook: int32 [128, 27], P('space'), may hold values from -1 to 127, as said below
- weight_first: bfloat16 [512, 27, 512], P('space', None, 'chan'), may hold values from -0.0546875 to 0.0546875
- weight_second: bfloat16 [512, 27, 512], P('space', None, 'chan'), may hold values from -0.0546875 to 0.0546875
- cotangent: bfloat16 [8192, 512], P('space', 'chan'), may hold values from -6 to 6
Outputs:
- output: bfloat16 [8192, 512], P('space', 'chan')
- features_grad: bfloat16 [8192, 512], P('space', 'chan')
- weight_first_grad: float32 [512, 27, 512], P('space', None, 'chan')
- weight_second_grad: float32 [512, 27, 512], P('space', None, 'chan')
Inputs may be any that keep to these rules, and one draw needn't show every extreme that they name: `rulebook`: entry [b, c] is the brick that feeds brick b through brick offset c, or -1 for none; entry 13 is b itself. A brick of another device belongs to a device s one or two indices away; if it feeds the device s + 1, s + 2, s - 1 or s - 2 (k = 0, 1, 2, 3 respectively), it is brick s * 2 + ((k + h) mod 2) for some h below 1.
All inputs are finite; a program needn't handle non-finite values. No bound on the sum of `mask` on one device may be relied on, other than what follows from the above.
Results may differ from a plain program's by a relative error of at most 0.005.
Values may be sent and summed in bfloat16 or wider, within the bound.
No kernel may reach another device: no remote copies, remote signals or barrier semaphores. Data moves between devices by JAX's collectives and lax.ppermute only.
A program may use at most 128 MiB of HBM per device.

v0:
```python
import jax
import jax.numpy as jnp
import numpy as np
from jax import lax
from jax.sharding import PartitionSpec as P

HB = 1


direction_steps = (1, 2, -1, -2)


def passed_along(value, axis, by):
    devices = lax.axis_size(axis)
    pairs = [(i, i + by) for i in range(devices) if 0 <= i + by < devices]
    return lax.ppermute(value, axis, pairs)


def offset_tables():
    brick_table = np.zeros((27, 64), np.int32)
    cell_table = np.zeros((27, 64), np.int32)
    for offset in range(27):
        moves = (offset // 9 - 1, offset // 3 % 3 - 1, offset % 3 - 1)
        for voxel in range(64):
            cells = (voxel // 16, voxel // 4 % 4, voxel % 4)
            target = [cells[axis_number] + moves[axis_number] for axis_number in range(3)]
            brick_table[offset, voxel] = (
                (target[0] // 4 + 1) * 9 + (target[1] // 4 + 1) * 3 + (target[2] // 4 + 1)
            )
            cell_table[offset, voxel] = target[0] % 4 * 16 + target[1] % 4 * 4 + target[2] % 4
    return (brick_table, cell_table)


def on_device(features, mask, rulebook, weight_first, weight_second, cotangent):
    brick_table, cell_table = offset_tables()
    bricks = rulebook.shape[0]
    spread = HB
    row_count = features.shape[0]
    halo_rows = 4 * spread * 64
    device_index = lax.axis_index("space")
    owner_device = rulebook // bricks
    within = rulebook % bricks
    sources = device_index - jnp.array(direction_steps, jnp.int32)
    lent_table = (
        jnp.arange(4, dtype=jnp.int32)[:, None] * spread
        + jnp.arange(spread, dtype=jnp.int32)[None, :]
    ) % bricks
    matches = (owner_device[:, :, None, None] == sources[None, None, :, None]) & (
        within[:, :, None, None] == lent_table[None, None]
    )
    numbers = bricks + jnp.arange(4 * spread, dtype=jnp.int32).reshape(4, spread)
    remote = jnp.sum(jnp.where(matches, numbers, 0), axis=(2, 3))
    slot_index = jnp.where(
        rulebook < 0, bricks + 4 * spread, jnp.where(owner_device == device_index, within, remote)
    )
    lookup = slot_index[:, brick_table] * 64 + cell_table[None]
    lookup = jnp.transpose(lookup, (1, 0, 2)).reshape(27, row_count).astype(jnp.int32)
    active = mask.astype(jnp.float32)[:, None]
    masked = (features.astype(jnp.float32) * active).astype(jnp.bfloat16)

    def outgoing(source, position):
        shaped = source.reshape(bricks, 64, source.shape[1])
        return jnp.take(shaped, lent_table[position], axis=0).reshape(spread * 64, source.shape[1])

    def extend(source):
        gathered = lax.all_gather(source, "chan", axis=1, tiled=True)
        blocks = [gathered]
        for position, offset in enumerate(direction_steps):
            blocks.append(passed_along(outgoing(gathered, position), "space", offset))
        blocks.append(jnp.zeros((64, gathered.shape[1]), jnp.bfloat16))
        return jnp.concatenate(blocks, 0)

    def lend_back(own_rows, returned, position):
        shaped = own_rows.reshape(bricks, 64, own_rows.shape[1])
        shaped = shaped.at[lent_table[position]].add(
            returned.reshape(spread, 64, own_rows.shape[1])
        )
        return shaped.reshape(row_count, own_rows.shape[1])

    def settle(running):
        summed = lax.psum_scatter(
            running[: row_count + halo_rows], "chan", scatter_dimension=1, tiled=True
        )
        own_rows = summed[:row_count]
        for position, offset in enumerate(direction_steps):
            block_start = row_count + position * spread * 64
            returned = passed_along(
                summed[block_start : block_start + spread * 64], "space", -offset
            )
            own_rows = lend_back(own_rows, returned, position)
        return own_rows

    def weight_term(extended, gradient):

        def advance(offset):
            picked = jnp.take(extended, lookup[offset], axis=0)
            return lax.dot_general(
                picked, gradient, (((0,), (0,)), ((), ())), preferred_element_type=jnp.float32
            )

        stacked = lax.map(advance, jnp.arange(27, dtype=jnp.int32))
        return jnp.transpose(stacked, (1, 0, 2))

    ext_in = extend(masked)
    table_rows = ext_in.shape[0]
    width = ext_in.shape[1]
    initial = jnp.zeros((row_count, weight_first.shape[2]), jnp.float32)
    segment = lax.all_gather(weight_first, "space", axis=0, tiled=True)
    columns = ext_in

    def advance(offset, running):
        picked = jnp.take(columns, lookup[offset], axis=0)
        kernel = lax.dynamic_index_in_dim(segment, offset, 1, keepdims=False)
        return running + jnp.dot(picked, kernel, preferred_element_type=jnp.float32)

    first_act = active * lax.fori_loop(0, 27, advance, initial)
    hidden = jax.nn.silu(first_act).astype(jnp.bfloat16)
    ext_hidden = extend(hidden)
    second_whole = lax.all_gather(weight_second, "space", axis=0, tiled=True)

    def forward_step(offset, running):
        picked = jnp.take(ext_hidden, lookup[offset], axis=0)
        kernel = lax.dynamic_index_in_dim(second_whole, offset, 1, keepdims=False)
        return running + jnp.dot(picked, kernel, preferred_element_type=jnp.float32)

    second_act = active * lax.fori_loop(
        0, 27, forward_step, jnp.zeros((row_count, second_whole.shape[2]), jnp.float32)
    )
    output = second_act.astype(jnp.bfloat16)
    grad_second = (cotangent.astype(jnp.float32) * active).astype(jnp.bfloat16)
    weight_second_grad = lax.psum_scatter(
        weight_term(ext_hidden, grad_second), "space", scatter_dimension=0, tiled=True
    )

    def backward_step(offset, running):
        kernel = lax.dynamic_index_in_dim(second_whole, offset, 1, keepdims=False)
        contrib = lax.dot_general(
            grad_second, kernel, (((1,), (1,)), ((), ())), preferred_element_type=jnp.float32
        )
        return running.at[lookup[offset]].add(contrib)

    hidden_grad = settle(
        lax.fori_loop(0, 27, backward_step, jnp.zeros((table_rows, width), jnp.float32))
    )
    sigmoid_first = jax.nn.sigmoid(first_act)
    grad_first = (
        active * hidden_grad * sigmoid_first * (1.0 + first_act * (1.0 - sigmoid_first))
    ).astype(jnp.bfloat16)
    weight_first_grad = lax.psum_scatter(
        weight_term(ext_in, grad_first), "space", scatter_dimension=0, tiled=True
    )

    def add_back(running, segment):
        columns = running

        def advance(offset, current):
            kernel = lax.dynamic_index_in_dim(segment, offset, 1, keepdims=False)
            contrib = lax.dot_general(
                grad_first, kernel, (((1,), (1,)), ((), ())), preferred_element_type=jnp.float32
            )
            return current.at[lookup[offset]].add(contrib)

        columns = lax.fori_loop(0, 27, advance, columns)
        return columns

    running = add_back(
        jnp.zeros((table_rows, width), jnp.float32),
        lax.all_gather(weight_first, "space", axis=0, tiled=True),
    )
    features_grad = (active * settle(running)).astype(jnp.bfloat16)
    return (output, features_grad, weight_first_grad, weight_second_grad)


def solution(mesh):
    placed = (
        P("space", "chan"),
        P("space"),
        P("space", None),
        P("space", None, "chan"),
        P("space", None, "chan"),
        P("space", "chan"),
    )
    return jax.shard_map(
        on_device,
        mesh=mesh,
        in_specs=placed,
        out_specs=(
            P("space", "chan"),
            P("space", "chan"),
            P("space", None, "chan"),
            P("space", None, "chan"),
        ),
        check_vma=False,
    )
```

profile of v0, /device:TPU:6, one launch (start us, length us, event | category | flops | bytes accessed | tf_op | source)
XLA Modules:
  0.0 874.7 jit_solution(18097774328851206864)
XLA Ops:
  10.5 3.3 gather_fusion.4
  16.8 72.0 %all-gather.5.cloned.1.call-done = bf16[512,27,128]{2,0,1:T(8,128)(2,1)} async-done(((bf16[8,27,128]{2,0,1:T(8,128)(2,1)}), bf16[512,27,128]{2,0,1:T(8,128)(2,1)}) %all-gather.5.cloned.1.call-update) | async-done | bytes 3538960 | tf_op jit(solution)/shard_map/all_gather | solution.py:119
  88.9 80.3 %while.83 = (s32[]{:T(128)}, f32[448,512]{1,0:T(8,128)S(1)}, s32[27,128]{1,0:T(8,128)S(1)}, bf16[512,27,128]{2,0,1:T(8,128)(2,1)}, bf16[128,128]{1,0:T(8,128)(2,1)S(1)}, /*index=5*/s32[]{:T(128)}) while((s32[]{:T(128)}, f32[448,512]{1,0:T(8,128)S(1)}, s32[27,128]{1,0:T(8,128)S(1)}, bf16[512,27,128]{2,0,1:T(8,128)(2,1)}, ...), condition=%wide.region_7.10_spmd, body=%wide.region_5.9_spmd.sunk | while | flops 16843136 | bytes 1738325 | solution.py:143
  90.2 1.7 scatter_fusion
  93.2 1.7 scatter_fusion
  96.1 1.7 scatter_fusion
  102.1 1.7 scatter_fusion
  108.0 1.7 scatter_fusion
  111.0 1.7 scatter_fusion
  114.0 1.7 scatter_fusion
  116.9 1.7 scatter_fusion
  122.9 1.7 scatter_fusion
  128.8 1.7 scatter_fusion
  131.8 1.7 scatter_fusion
  137.8 1.7 scatter_fusion
  143.7 1.7 scatter_fusion
  146.7 1.7 scatter_fusion
  149.6 1.7 scatter_fusion
  152.6 1.7 scatter_fusion
  158.6 1.7 scatter_fusion
  164.5 1.7 scatter_fusion
  167.5 1.7 scatter_fusion
  179.3 12.1 %all_gather.13 = bf16[128,512]{1,0:T(8,128)(2,1)S(1)} all-gather(bf16[128,128]{1,0:T(8,128)(2,1)S(1)} %get-tuple-element.700), channel_id=1, replica_groups=mesh['space'=64,'chan'=4] {'chan'}, dimensions={1}, use_global_device_ids=true | all-gather | bytes 163840 | tf_op jit(solution)/shard_map/all_gather | solution.py:66
  191.4 1.9 collective-permute-start
  193.4 3.3 collective-permute-start.1
  196.7 5.5 collective-permute-start.2
  202.2 2.5 collective-permute-start.3
  205.6 2.7 collective-permute-done.3
  209.2 2.9 collective-permute-start.8
  212.1 60.8 %all-gather.3.cloned.1.call-done = bf16[512,27,128]{2,0,1:T(8,128)(2,1)} async-done(((bf16[8,27,128]{2,0,1:T(8,128)(2,1)}), bf16[512,27,128]{2,0,1:T(8,128)(2,1)}) %all-gather.3.cloned.1.call-update) | async-done | bytes 3538960 | tf_op jit(solution)/shard_map/all_gather | solution.py:108
  272.9 55.7 %while.87 = (s32[]{:T(128)}, f32[128,128]{1,0:T(8,128)S(1)}, s32[27,128]{1,0:T(8,128)S(1)}, bf16[448,512]{1,0:T(8,128)(2,1)S(1)}, bf16[512,27,128]{2,0,1:T(8,128)(2,1)}, /*index=5*/s32[]{:T(128)}, s32[]{:T(128)}) while((s32[]{:T(128)}, f32[128,128]{1,0:T(8,128)S(1)}, s32[27,128]{1,0:T(8,128)S(1)}, bf16[448,512]{1,0:T(8,128)(2,1)S(1)}, ...), condition=%wide.region_2.5_spmd.clone, body=%wide.region_1.4_spmd.clone.sunk | while | flops 16877316 | bytes 661863 | solution.py:116
  328.7 4.8 collective-permute-start.9
  333.5 1.9 collective-permute-start.10
  335.4 1.9 collective-permute-start.11
  338.7 2.2 collective-permute-done.10
  341.5 1.8 collective-permute-done.11
  344.2 80.3 %while.84 = (s32[]{:T(128)}, f32[448,512]{1,0:T(8,128)S(1)}, s32[27,128]{1,0:T(8,128)S(1)}, bf16[512,27,128]{2,0,1:T(8,128)(2,1)}, bf16[128,128]{1,0:T(8,128)(2,1)S(1)}, /*index=5*/s32[]{:T(128)}) while((s32[]{:T(128)}, f32[448,512]{1,0:T(8,128)S(1)}, s32[27,128]{1,0:T(8,128)S(1)}, bf16[512,27,128]{2,0,1:T(8,128)(2,1)}, ...), condition=%wide.region_15.18_spmd, body=%wide.region_13.17_spmd.sunk | while | flops 16843136 | bytes 1738325 | solution.py:163
  348.4 1.7 scatter_fusion.1
  354.3 1.7 scatter_fusion.1
  357.3 1.7 scatter_fusion.1
  363.3 1.7 scatter_fusion.1
  369.2 1.7 scatter_fusion.1
  372.2 1.7 scatter_fusion.1
  375.1 1.7 scatter_fusion.1
  378.1 1.7 scatter_fusion.1
  384.1 1.7 scatter_fusion.1
  390.0 1.7 scatter_fusion.1
  393.0 1.7 scatter_fusion.1
  425.5 11.7 %all_gather.15 = bf16[128,512]{1,0:T(8,128)(2,1)S(1)} all-gather(bf16[128,128]{1,0:T(8,128)(2,1)S(1)} %get-tuple-element.688), channel_id=1, replica_groups=mesh['space'=64,'chan'=4] {'chan'}, dimensions={1}, use_global_device_ids=true | all-gather | bytes 163840 | tf_op jit(solution)/shard_map/all_gather | solution.py:66
  437.2 1.9 collective-permute-start.4
  439.2 1.9 collective-permute-start.5
  441.1 5.8 collective-permute-start.6
  446.8 3.6 collective-permute-start.7
  450.5 3.7 broadcast.332.clone
  454.2 119.1 %while.85 = (s32[]{:T(128)}, f32[27,512,128]{2,1,0:T(8,128)}, s32[27]{0:T(128)S(1)}, s32[27,128]{1,0:T(8,128)S(1)}, bf16[448,512]{1,0:T(8,128)(2,1)S(1)}, /*inde...) while((s32[]{:T(128)}, f32[27,512,128]{2,1,0:T(8,128)}, s32[27]{0:T(128)S(1)}, ...), condition=%wide.region_18.21_spmd, body=%wide.region_17.20_spmd.sunk | while | flops 16844548 | bytes 694683 | solution.py:101
  573.5 3.7 broadcast.332.clone.1
  577.2 119.1 %while.86 = (s32[]{:T(128)}, f32[27,512,128]{2,1,0:T(8,128)}, s32[27]{0:T(128)S(1)}, s32[27,128]{1,0:T(8,128)S(1)}, bf16[448,512]{1,0:T(8,128)(2,1)S(1)}, /*inde...) while((s32[]{:T(128)}, f32[27,512,128]{2,1,0:T(8,128)}, s32[27]{0:T(128)S(1)}, ...), condition=%wide.region_21.24_spmd, body=%wide.region_20.23_spmd.sunk | while | flops 16844548 | bytes 694683 | solution.py:101
  697.2 1.9 collective-permute-start.12
  699.1 55.8 %while.88 = (s32[]{:T(128)}, f32[128,128]{1,0:T(8,128)S(1)}, s32[27,128]{1,0:T(8,128)S(1)}, bf16[448,512]{1,0:T(8,128)(2,1)S(1)}, bf16[512,27,128]{2,0,1:T(8,128)(2,1)}, /*index=5*/s32[]{:T(128)}, s32[]{:T(128)}) while((s32[]{:T(128)}, f32[128,128]{1,0:T(8,128)S(1)}, s32[27,128]{1,0:T(8,128)S(1)}, bf16[448,512]{1,0:T(8,128)(2,1)S(1)}, ...), condition=%wide.region_4.7_spmd.clone, body=%wide.region_3.6_spmd.clone.sunk | while | flops 16877316 | bytes 661863 | solution.py:126
  754.9 1.9 collective-permute-start.13
  756.9 2.5 collective-permute-start.14
  759.4 3.6 collective-permute-start.15
  765.1 2.2 collective-permute-done.15
  768.6 99.3 %reduce-scatter.11.cloned.1.call-done = f32[8,27,128]{2,0,1:T(8,128)} async-done(((f32[512,27,128]{2,0,1:T(8,128)}), f32[8,27,128]{2,0,1:T(8,128)}) %reduce-scatter.11.cloned.1.call-update) | async-done | bytes 110608 | tf_op jit(solution)/shard_map/reduce_scatter | solution.py:131
  (758 shorter events, 367.1 us)
Async XLA Ops:
  7.2 81.6 %all-gather.5.cloned.1.call-start = ((), (), s32[]{:S(2)}) async-start(), calls=%async_computation.5 | async-start | bytes 3594240 | tf_op jit(solution)/shard_map/all_gather | solution.py:119
  7.9 200.5 %reduce-scatter.5.cloned.1.call-start = ((), (), s32[]{:S(2)}) async-start(), calls=%async_computation.6 | async-start | bytes 983040 | tf_op jit(solution)/shard_map/reduce_scatter | solution.py:81
  88.9 115.8 %copy-start = (s32[3]{0:T(128)S(1)}, s32[3]{0:T(128)}, u32[]{:S(2)}) copy-start(s32[3]{0:T(128)} %constant.387.clone.1) | copy-start | bytes 40
  170.2 102.8 %all-gather.3.cloned.1.call-start = ((), (), s32[]{:S(2)}) async-start(), calls=%async_computation.4 | async-start | bytes 3594240 | tf_op jit(solution)/shard_map/all_gather | solution.py:108
  170.9 525.4 %reduce-scatter.7.cloned.1.call-start = ((), (), s32[]{:S(2)}) async-start(), calls=%async_computation.7 | async-start | bytes 983040 | tf_op jit(solution)/shard_map/reduce_scatter | solution.py:81
  191.4 14.1 %collective-permute-start = (bf16[64,512]{1,0:T(8,128)(2,1)S(1)}, bf16[64,512]{1,0:T(8,128)(2,1)S(1)}, u32[]{:S(2)}, u32[]{:S(2)}) collective-permute-start(bf16[64,512]{1,0:T(8,128)(2,1)S(1)} %get-tuple-element.686), channel_id=1, source_target_pairs={{0,4},{4,8},{8,12},{12,16},{16,20},{20,24},{24,28},{28,32},{32,36}... | collective-permute-start | bytes 196616 | tf_op jit(solution)/shard_map/ppermute | solution.py:16
  193.4 12.2 %collective-permute-start.1 = (bf16[64,512]{1,0:T(8,128)(2,1)S(1)}, bf16[64,512]{1,0:T(8,128)(2,1)S(1)}, u32[]{:S(2)}, u32[]{:S(2)}) collective-permute-start(bf16[64,512]{1,0:T(8,128)(2,1)S(1)} %get-tuple-element.685), channel_id=1, source_target_pairs={{0,8},{4,12},{8,16},{12,20},{16,24},{20,28},{24,32},{28,36},{32,40... | collective-permute-start | bytes 196616 | tf_op jit(solution)/shard_map/ppermute | solution.py:16
  196.7 8.9 %collective-permute-start.2 = (bf16[64,512]{1,0:T(8,128)(2,1)S(1)}, bf16[64,512]{1,0:T(8,128)(2,1)S(1)}, u32[]{:S(2)}, u32[]{:S(2)}) collective-permute-start(bf16[64,512]{1,0:T(8,128)(2,1)S(1)} %get-tuple-element.684), channel_id=1, source_target_pairs={{4,0},{8,4},{12,8},{16,12},{20,16},{24,20},{28,24},{32,28},{36,32}... | collective-permute-start | bytes 196616 | tf_op jit(solution)/shard_map/ppermute | solution.py:16
  202.2 6.2 collective-permute-start.3
  208.4 129.0 %slice-start.1 = ((f32[384,128]{1,0:T(8,128)}), f32[128,128]{1,0:T(8,128)S(1)}, s32[]{:S(2)}) async-start(f32[384,128]{1,0:T(8,128)} %reduce-scatter.5.cloned.1.call-done), calls=%async_computation.11 | async-start | bytes 131072 | tf_op jit(solution)/shard_map/slice | solution.py:84
  209.2 128.1 %collective-permute-start.8 = (f32[64,128]{1,0:T(8,128)S(1)}, f32[64,128]{1,0:T(8,128)S(1)}, u32[]{:S(2)}, u32[]{:S(2)}) collective-permute-start(f32[64,128]{1,0:T(8,128)S(1)} %get-tuple-element.678), channel_id=1, source_target_pairs={{4,0},{8,4},{12,8},{16,12},{20,16},{24,20},{28,24},{32,28},{36,32}... | collective-permute-start | bytes 98312 | tf_op jit(solution)/shard_map/ppermute | solution.py:16
  328.7 9.3 %collective-permute-start.9 = (f32[64,128]{1,0:T(8,128)S(1)}, f32[64,128]{1,0:T(8,128)S(1)}, u32[]{:S(2)}, u32[]{:S(2)}) collective-permute-start(f32[64,128]{1,0:T(8,128)S(1)} %get-tuple-element.677), channel_id=1, source_target_pairs={{8,0},{12,4},{16,8},{20,12},{24,16},{28,20},{32,24},{36,28},{40,32... | collective-permute-start | bytes 98312 | tf_op jit(solution)/shard_map/ppermute | solution.py:16
  333.5 7.3 collective-permute-start.10
  335.4 7.9 collective-permute-start.11
  425.4 343.2 %reduce-scatter.9.cloned.1.call-start = ((), (), s32[]{:S(2)}) async-start(), calls=%async_computation.8 | async-start | bytes 7188480 | tf_op jit(solution)/shard_map/reduce_scatter | solution.py:149
  437.2 136.2 %collective-permute-start.4 = (bf16[64,512]{1,0:T(8,128)(2,1)S(1)}, bf16[64,512]{1,0:T(8,128)(2,1)S(1)}, u32[]{:S(2)}, u32[]{:S(2)}) collective-permute-start(bf16[64,512]{1,0:T(8,128)(2,1)S(1)} %get-tuple-element.682), channel_id=1, source_target_pairs={{0,4},{4,8},{8,12},{12,16},{16,20},{20,24},{24,28},{28,32},{32,36}... | collective-permute-start | bytes 196616 | tf_op jit(solution)/shard_map/ppermute | solution.py:16
  439.2 134.3 %collective-permute-start.5 = (bf16[64,512]{1,0:T(8,128)(2,1)S(1)}, bf16[64,512]{1,0:T(8,128)(2,1)S(1)}, u32[]{:S(2)}, u32[]{:S(2)}) collective-permute-start(bf16[64,512]{1,0:T(8,128)(2,1)S(1)} %get-tuple-element.681), channel_id=1, source_target_pairs={{0,8},{4,12},{8,16},{12,20},{16,24},{20,28},{24,32},{28,36},{32,40... | collective-permute-start | bytes 196616 | tf_op jit(solution)/shard_map/ppermute | solution.py:16
  441.1 132.4 %collective-permute-start.6 = (bf16[64,512]{1,0:T(8,128)(2,1)S(1)}, bf16[64,512]{1,0:T(8,128)(2,1)S(1)}, u32[]{:S(2)}, u32[]{:S(2)}) collective-permute-start(bf16[64,512]{1,0:T(8,128)(2,1)S(1)} %get-tuple-element.680), channel_id=1, source_target_pairs={{4,0},{8,4},{12,8},{16,12},{20,16},{24,20},{28,24},{32,28},{36,32}... | collective-permute-start | bytes 196616 | tf_op jit(solution)/shard_map/ppermute | solution.py:16
  446.8 126.6 %collective-permute-start.7 = (bf16[64,512]{1,0:T(8,128)(2,1)S(1)}, bf16[64,512]{1,0:T(8,128)(2,1)S(1)}, u32[]{:S(2)}, u32[]{:S(2)}) collective-permute-start(bf16[64,512]{1,0:T(8,128)(2,1)S(1)} %get-tuple-element.679), channel_id=1, source_target_pairs={{8,0},{12,4},{16,8},{20,12},{24,16},{28,20},{32,24},{36,28},{40,32... | collective-permute-start | bytes 196616 | tf_op jit(solution)/shard_map/ppermute | solution.py:16
  573.3 294.6 %reduce-scatter.11.cloned.1.call-start = ((), (), s32[]{:S(2)}) async-start(), calls=%async_computation.9 | async-start | bytes 7188480 | tf_op jit(solution)/shard_map/reduce_scatter | solution.py:131
  696.3 66.7 %slice-start = ((f32[384,128]{1,0:T(8,128)}), f32[128,128]{1,0:T(8,128)S(1)}, s32[]{:S(2)}) async-start(f32[384,128]{1,0:T(8,128)} %reduce-scatter.7.cloned.1.call-done), calls=%async_computation.10 | async-start | bytes 131072 | tf_op jit(solution)/shard_map/slice | solution.py:84
  697.2 65.8 %collective-permute-start.12 = (f32[64,128]{1,0:T(8,128)S(1)}, f32[64,128]{1,0:T(8,128)S(1)}, u32[]{:S(2)}, u32[]{:S(2)}) collective-permute-start(f32[64,128]{1,0:T(8,128)S(1)} %get-tuple-element.674), channel_id=1, source_target_pairs={{4,0},{8,4},{12,8},{16,12},{20,16},{24,20},{28,24},{32,28},{36,32}... | collective-permute-start | bytes 98312 | tf_op jit(solution)/shard_map/ppermute | solution.py:16
  754.9 8.7 collective-permute-start.13
  756.9 7.5 collective-permute-start.14
  759.4 7.9 collective-permute-start.15
Sparse Core Ops, SparseCore 0:
  10.6 78.2 all-gather.4
  170.3 24.6 reduce-scatter.4
  197.5 75.3 all-gather.2
  425.5 22.1 reduce-scatter.6
  573.5 142.7 reduce-scatter.8
  721.0 146.8 reduce-scatter.10
where the time goes:
time: 880 us; the launch traced here: 875 us
  waiting for transfers between devices  242 us (28%)
  matrix products  175 us (20%)
  local copies, waits for them, and re-layouts  147 us (17%)
  loops' own time  111 us (13%)
  other arithmetic  106 us (12%)
  starting transfers between devices  48.2 us (5%)
  blocking collectives  23.9 us (3%)
  between operations  22.5 us (3%)
    another operation x2, loops' own time, weight_term(): stacked = lax.map(advance, jnp.arange(27, dtype=jnp.int32))  106 us
    reduce_scatter x1, waiting for transfers between devices, on_device(): lax.psum_scatter(weight_term(ext_hidden, grad_second), 'space', scatter_d...  99.3 us
    all_gather x1, waiting for transfers between devices, on_device(): second_whole = lax.all_gather(weight_second, 'space', axis=0, tiled=True)  72 us
    all_gather x1, waiting for transfers between devices, on_device(): segment = lax.all_gather(weight_first, 'space', axis=0, tiled=True)  60.8 us
    dot_general x54, matrix products, advance(): lax.dot_general(picked, gradient, (((0,), (0,)), ((), ())), preferred_ele...  53.9 us
    ppermute x16, starting transfers between devices, passed_along(): return lax.ppermute(value, axis, pairs)  48 us
    scatter-add x27, other arithmetic, backward_step(): return running.at[lookup[offset]].add(contrib)  45.9 us
    scatter-add x27, other arithmetic, advance(): return current.at[lookup[offset]].add(contrib)  45.9 us
  transfers between devices with their start and end apart: 22, of which 7 were waited for; matrix products, arithmetic and copies ran while one was open for 30% of the time, Pallas kernels for 0%

commit v1 on v0

v1 whole, which is shorter than its diff:
```python
import jax
import jax.numpy as jnp
import numpy as np
from jax import lax
from jax.experimental import pallas as pl
from jax.experimental.pallas import tpu as pltpu
from jax.sharding import Mesh
from jax.sharding import PartitionSpec as P

STEPS = (1, 2, -1, -2)
SPACE = ("x", "z", "core")
CELLS = 224
BF = jnp.bfloat16
F32 = jnp.float32


def tables():
    pick = np.zeros((CELLS, 32), np.float32)
    pick_back = np.zeros((CELLS, 32), np.float32)
    local = np.zeros((CELLS, 128), np.float32)
    for row in range(216):
        cell = (row // 36, row // 6 % 6, row % 6)
        side = [(v == 5) - (v == 0) for v in cell]
        at = [(v - 1) % 4 for v in cell]
        pick[row, 9 * (side[0] + 1) + 3 * (side[1] + 1) + side[2] + 1] = 1
        pick_back[row, 9 * (1 - side[0]) + 3 * (1 - side[1]) + 1 - side[2]] = 1
        voxel = at[0] * 16 + at[1] * 4 + at[2]
        local[row, voxel] = 1
        local[row, 64 + voxel] = 1
    spread = np.zeros((9, 6, 4, 4, CELLS), np.float32)
    for move in range(9):
        for i in range(6):
            for j in range(4):
                for k in range(4):
                    spread[move, i, j, k, i * 36 + (j + move // 3) * 6 + k + move % 3] = 1
    lanes = np.zeros((128, 2048), np.float32)
    for brick in range(2):
        for column in range(384):
            lanes[brick * 6 + column // 64, brick * 384 + column] = 1
        for column in range(640):
            lanes[12 + brick * 10 + column // 64, 768 + brick * 640 + column] = 1
    lane = np.arange(128)
    device = np.where((lane >= 12) & (lane < 32), (lane - 12) % 10 // 2, 0)
    sources = np.zeros((16, 128), np.float32)
    sources[device, lane] = 1
    as_bf = lambda value: jnp.asarray(value, BF)
    return (
        as_bf(pick),
        as_bf(pick_back),
        jnp.asarray(local),
        as_bf(spread.reshape(864, CELLS)),
        as_bf(lanes),
        as_bf(sources),
    )


def dot(a, b):
    return jnp.dot(a, b, preferred_element_type=F32)


def fill(out, base, matches, rows, pick, local, spread):
    count = rows.shape[0]
    padded = []
    for brick in range(2):
        chosen = dot(pick, matches[:, brick * count : (brick + 1) * count])
        select = (chosen * jnp.concatenate([local] * (count // 128), axis=1)).astype(BF)
        padded.append(dot(select, rows).astype(BF))
    wide = dot(spread, jnp.concatenate(padded, axis=1)).astype(BF)
    for brick in range(2):
        out[base + brick] = wide[:, brick * 128 : (brick + 1) * 128].reshape(9, 96, 128)


def block(ref, offset):
    start = offset // 9 * 16
    return ref[:, offset % 9, start : start + 64, :].reshape(512, 128)


def convolve(ref, weight):
    total = None
    for offset in range(27):
        part = dot(block(ref, offset), weight[offset])
        total = part if total is None else total + part
    return total


def convolve_back(ref, weight):
    total = None
    for offset in range(27):
        part = lax.dot_general(
            block(ref, 26 - offset), weight[offset], (((1,), (1,)), ((), ())), preferred_element_type=F32
        )
        total = part if total is None else total + part
    return total


def around(ids, own, before, after, other, turn):
    return (
        own.at[turn],
        other.at[1 - ids[2], (turn - ids[3] * (1 - ids[2])) & 3],
        before.at[(turn - ids[3]) & 3],
        other.at[ids[2], (turn + ids[4] * ids[2]) & 3],
        after.at[(turn + ids[4]) & 3],
    )


def gather_first(
    ids, mine, before, after, other, pick, pick_back, local, spread, lanes, sources, q_in, q_back, own, matched
):
    @pl.loop(0, 4)
    def _(turn):
        at = (ids[1] + turn) & 3
        views = around(ids, mine, before, after, other, turn)
        compact = None
        for device, view in enumerate(views):
            part = view[192:224, :] * sources[device : device + 1, :]
            compact = part if compact is None else compact + part
        matched[at] = compact
        own[at] = views[0][64:192, :]
        found = dot(compact, lanes[...]).astype(BF)
        rows = [views[0][0:64, :], views[0][224:288, :]]
        rows += [view[device % 2 * 224 : device % 2 * 224 + 64, :] for device, view in enumerate(views[1:])]
        fill(q_in, at * 2, found[:, :768], jnp.concatenate(rows, 0), pick[...], local[...], spread[...])
        rows = jnp.concatenate([view[64:192, :] for view in views], 0)
        fill(q_back, at * 2, found[:, 768:], rows, pick_back[...], local[...], spread[...])


def apply_first(q_in, q_back, weights, out):
    forward = convolve(q_in, weights.at[0])
    backward = convolve_back(q_back, weights.at[1])
    for at in range(4):
        out[at, 0:128, :] = forward[at * 128 : (at + 1) * 128]
        out[at, 128:256, :] = backward[at * 128 : (at + 1) * 128]


def weight_blocks(ref, gradient, keep, send, scratch, core):
    @pl.loop(0, 3)
    def _(move):
        start = pl.multiple_of(move * 16, 16)
        for rest in range(9):
            columns = ref[:, rest, pl.ds(start, 64), :].reshape(512, 128)
            scratch[rest % 2] = lax.dot_general(
                columns, gradient, (((0,), (0,)), ((), ())), preferred_element_type=F32
            )
            for z in range(8):
                keep[z, move * 9 + rest] = scratch[rest % 2, pl.ds(z * 16 + core * 8, 8), :]
                send[z, move * 9 + rest] = scratch[rest % 2, pl.ds(z * 16 + 8 - core * 8, 8), :]


def weigh_first(ids, mine, q_in, keep, send, own, scratch):
    for turn in range(4):
        own[(ids[0] + turn) & 3] = mine[turn, 128:256, :]
    weight_blocks(q_in, own[...].reshape(512, 128), keep, send, scratch, ids[2])


def apply_second(
    ids, mine, before, after, other, matched, own, weights, pick, pick_back, local, spread, lanes, sources,
    reduced, keep, send, q_hidden, q_back, scratch,
):
    @pl.loop(0, 4)
    def _(turn):
        at = (ids[0] + turn) & 3
        views = around(ids, mine, before, after, other, turn)
        found = dot(matched[at], lanes[...]).astype(BF)
        rows = [views[0][0:128, :]]
        rows += [view[device % 2 * 64 : device % 2 * 64 + 64, :] for device, view in enumerate(views[1:])]
        fill(q_hidden, at * 2, found[:, :768], jnp.concatenate(rows, 0), pick[...], local[...], spread[...])
        rows = jnp.concatenate([view[128:256, :] for view in views], 0)
        fill(q_back, at * 2, found[:, 768:], rows, pick_back[...], local[...], spread[...])

    forward = convolve(q_hidden, weights.at[1])
    backward = convolve_back(q_back, weights.at[0])
    for at in range(4):
        turn = (at - ids[1]) & 3
        reduced[turn, 0:128, :] = forward[at * 128 : (at + 1) * 128]
        reduced[turn, 128:256, :] = backward[at * 128 : (at + 1) * 128]
    weight_blocks(q_hidden, own[...].reshape(512, 128), keep, send, scratch, ids[2])


def call(kernel, outs, scratch, *args):
    smem = pl.BlockSpec(memory_space=pltpu.SMEM)
    vmem = pl.BlockSpec(memory_space=pltpu.VMEM)
    return pl.pallas_call(
        kernel,
        out_shape=outs,
        in_specs=[smem if value.dtype == jnp.int32 else vmem for value in args],
        out_specs=[vmem] * len(outs),
        scratch_shapes=scratch,
        compiler_params=pltpu.CompilerParams(vmem_limit_bytes=52 * 2**20),
    )(*args)


def spread_out(mine):
    before = lax.ppermute(mine, "z", [(i, (i + 1) % 8) for i in range(8)])
    after = lax.ppermute(mine, "z", [(i, (i - 1) % 8) for i in range(8)])
    cross = jnp.where(lax.axis_index("core") == 1, before, after)
    other = lax.ppermute(jnp.stack([mine, cross]), "core", [(0, 1), (1, 0)])
    return before, after, other


def on_device(features, mask, rulebook, weight_first, weight_second, cotangent):
    shape = jax.ShapeDtypeStruct
    x = lax.axis_index("x")
    core = lax.axis_index("core")
    here = lax.axis_index(SPACE)
    chan = lax.axis_index("chan")
    z = lax.axis_index("z")
    ids = jnp.stack([x, chan, core, (z == 0).astype(jnp.int32), (z == 7).astype(jnp.int32)]).astype(jnp.int32)
    swap = [(a * 4 + b, b * 4 + a) for a in range(4) for b in range(4)]

    shards = jnp.stack([weight_first, lax.ppermute(weight_second, ("x", "chan"), swap)])
    blocks = jnp.transpose(lax.all_gather(shards, ("z", "core"), axis=1, tiled=True), (0, 2, 1, 3))

    active = mask.astype(F32)[:, None]
    masked = (features.astype(F32) * active).astype(BF)
    grad_second = (cotangent.astype(F32) * active).astype(BF)

    padded = jnp.pad(rulebook.T, ((0, 5), (0, 0)), constant_values=-1)
    lane = np.arange(128)
    back_lane = np.where((lane >= 12) & (lane < 32), lane - 12, 0)
    read_by = np.where(lane < 12, lane // 6, back_lane % 2)
    reading = jnp.where(jnp.asarray(read_by == 0)[None], padded[:, 0:1], padded[:, 1:2])
    sources = np.array([0, 1, -2, -3, 2, 5])

    relative = jnp.where(reading >= 0, reading - here * 2, -(2**20))

    def lane_match(offsets, valid):
        target = np.where(valid, offsets, 2**20).astype(np.int32)
        return (relative == jnp.asarray(target)[None]).astype(BF)

    def back_match(position):
        valid = (lane >= 12) & (lane < 32) & (back_lane // 2 % 5 == position)
        step = 0 if position == 0 else STEPS[position - 1]
        return lane_match(2 * step + back_lane // 10, valid)

    compact = lane_match(sources[lane % 6], lane < 12)
    for position in range(5):
        compact = compact + back_match(position)
    packed = jnp.concatenate([masked[:64], grad_second, compact, masked[64:]], 0)
    turned = jnp.stack(
        [
            lax.ppermute(packed, ("x", "chan"), [(a * 4 + b, b * 4 + (a - r) % 4) for a in range(4) for b in range(4)])
            for r in range(4)
        ]
    )
    consts = tables()
    columns = shape((8, 9, 96, 128), BF)
    q_in, q_back, own, matched = call(
        gather_first,
        [columns, columns, shape((4, 128, 128), BF), shape((4, 32, 128), BF)],
        [],
        ids,
        turned,
        *spread_out(turned),
        *consts,
    )
    (partial,) = call(apply_first, [shape((4, 256, 128), F32)], [], q_in, q_back, blocks)
    summed = jnp.sum(lax.all_to_all(partial, "x", 0, 0, tiled=True), axis=0)
    first_act = active * summed[0:128]
    hidden_grad = summed[128:256]
    sigmoid_first = jax.nn.sigmoid(first_act)
    hidden = (first_act * sigmoid_first).astype(BF)
    grad_first = (
        active * hidden_grad * sigmoid_first * (1.0 + first_act * (1.0 - sigmoid_first))
    ).astype(BF)

    packed = jnp.concatenate([hidden, grad_first], 0)
    along = jnp.stack(
        [packed] + [lax.ppermute(packed, "x", [(a, (a - r) % 4) for a in range(4)]) for r in range(1, 4)]
    )
    pieces = shape((8, 27, 8, 128), F32)
    pair = pltpu.VMEM((2, 128, 128), F32)
    keep1, send1 = call(weigh_first, [pieces, pieces], [pltpu.VMEM((4, 128, 128), BF), pair], ids, along, q_in)
    reduced, keep2, send2 = call(
        apply_second,
        [shape((4, 256, 128), F32), pieces, pieces],
        [pltpu.VMEM((8, 9, 96, 128), BF), pltpu.VMEM((8, 9, 96, 128), BF), pair],
        ids,
        along,
        *spread_out(along),
        matched,
        own,
        blocks,
        *consts,
    )
    total = None
    for r in range(4):
        part = lax.ppermute(
            reduced[r], ("x", "chan"), [(a * 4 + b, (b + r) % 4 * 4 + a) for a in range(4) for b in range(4)]
        )
        total = part if total is None else total + part
    output = (active * total[0:128]).astype(BF)
    features_grad = (active * total[128:256]).astype(BF)

    def settle(keep, send):
        mine = keep + lax.ppermute(send, "core", [(0, 1), (1, 0)])
        moved = lax.all_to_all(mine.astype(BF).reshape(8, 27 * 8, 128), "z", 0, 0, tiled=True)
        return jnp.sum(moved.astype(F32), axis=0).reshape(27, 8, 128)

    second_sum = lax.ppermute(settle(keep2, send2), ("x", "chan"), swap)
    first_sum = settle(keep1, send1)
    return (
        output,
        features_grad,
        jnp.transpose(first_sum, (1, 0, 2)),
        jnp.transpose(second_sum, (1, 0, 2)),
    )


def solution(mesh):
    split = Mesh(mesh.devices.reshape(4, 8, 2, 4), ("x", "z", "core", "chan"))
    placed = (
        P(SPACE, "chan"),
        P(SPACE),
        P(SPACE, None),
        P(SPACE, None, "chan"),
        P(SPACE, None, "chan"),
        P(SPACE, "chan"),
    )
    return jax.shard_map(
        on_device,
        mesh=split,
        in_specs=placed,
        out_specs=(
            P(SPACE, "chan"),
            P(SPACE, "chan"),
            P(SPACE, None, "chan"),
            P(SPACE, None, "chan"),
        ),
        check_vma=False,
    )
```

time: 880 us -> 185 us (0.21)
  matrix products: 175 us -> 0 us
  waiting for transfers between devices: 242 us -> 67.5 us
  local copies, waits for them, and re-layouts: 147 us -> 3.2 us
  loops' own time: 111 us -> 0 us
  other arithmetic: 106 us -> 7.56 us
  Pallas kernels: 0 us -> 31.3 us
  blocking collectives: 23.9 us -> 12 us
    dot_general x162 -> x0, matrix products: 175 us -> none  [the longest x54 53.9 us: advance(): lax.dot_general(picked, gradient, (((0,), (0,)), ((), ())), preferred_ele...]
    all_gather x2 -> x1, waiting for transfers between devices: 133 us -> 0.01 us  [on_device(): lax.all_gather(shards, ('z', 'core'), axis=1, tiled=True)]
    another operation x6 -> x0, loops' own time: 111 us -> none  [the longest x2 106 us: weight_term(): stacked = lax.map(advance, jnp.arange(27, dtype=jnp.int32))]
    reduce_scatter x4 -> x0, waiting for transfers between devices: 99.4 us -> none  [the longest x1 99.3 us: on_device(): lax.psum_scatter(weight_term(ext_hidden, grad_second), 'space', scatter_d...]
    scatter-add x62 -> x0, other arithmetic: 96.9 us -> none  [the longest x27 45.9 us: backward_step(): return running.at[lookup[offset]].add(contrib)]
    gather x109 -> x0, local copies, waits for them, and re-layouts: 94.9 us -> none  [the longest x54 45.8 us: advance(): picked = jnp.take(extended, lookup[offset], axis=0)]
    ppermute x16 -> x21, waiting for transfers between devices: 8.91 us -> 52 us  [the longest x2 11.8 us: spread_out(): after = lax.ppermute(mine, 'z', [(i, (i - 1) % 8) for i in range(8)])]
    dynamic_slice x54 -> x0, local copies, waits for them, and re-layouts: 31.4 us -> none  [weight_term(): stacked = lax.map(advance, jnp.arange(27, dtype=jnp.int32))]
  transfers between devices with their start and end apart: 22 -> 24, of which waited for: 7 -> 17; matrix products, arithmetic and copies ran while one was open for 30% -> 4% of each run, Pallas kernels for 0% -> 7%
where the time goes in v1:
time: 185 us; the launch traced here: 184 us
  waiting for transfers between devices  67.5 us (36%)
  starting transfers between devices  48.3 us (26%)
  Pallas kernels  31.3 us (17%)
  between operations  14.3 us (8%)
  blocking collectives  12 us (6%)
  other arithmetic  7.56 us (4%)
  local copies, waits for them, and re-layouts  3.2 us (2%)
    pallas_call x4, Pallas kernels, call(): pl.pallas_call(kernel, out_shape=outs, in_specs=[smem if value.dtype == j...  31.3 us
    all_to_all x2, waiting for transfers between devices, settle(): lax.all_to_all(mine.astype(BF).reshape(8, 27 * 8, 128), 'z', 0, 0, tiled=...  15.5 us
    all_to_all x1, blocking collectives, on_device(): summed = jnp.sum(lax.all_to_all(partial, 'x', 0, 0, tiled=True), axis=0)  12 us
    ppermute x2, waiting for transfers between devices, spread_out(): after = lax.ppermute(mine, 'z', [(i, (i - 1) % 8) for i in range(8)])  11.8 us
    ppermute x4, starting transfers between devices, on_device(): lax.ppermute(reduced[r], ('x', 'chan'), [(a * 4 + b, (b + r) % 4 * 4 + a)...  9.27 us
    ppermute x4, starting transfers between devices, on_device(): lax.ppermute(packed, ('x', 'chan'), [(a * 4 + b, b * 4 + (a - r) % 4) for...  8.97 us
    ppermute x4, waiting for transfers between devices, on_device(): lax.ppermute(reduced[r], ('x', 'chan'), [(a * 4 + b, (b + r) % 4 * 4 + a)...  8.62 us
    ppermute x4, waiting for transfers between devices, on_device(): lax.ppermute(packed, ('x', 'chan'), [(a * 4 + b, b * 4 + (a - r) % 4) for...  7.87 us
  transfers between devices with their start and end apart: 24, of which 17 were waited for; matrix products, arithmetic and copies ran while one was open for 4% of the time, Pallas kernels for 7%

profile of v1, /device:TPU:6, one launch (start us, length us, event | category | flops | bytes accessed | tf_op | source)
XLA Modules:
  0.0 184.2 jit_solution(6660077758014290558)
XLA Ops:
  7.2 0.0 all-gather.2.cloned.1.call-start
  7.2 4.8 %collective-permute-start.7 = (bf16[8,27,128]{2,0,1:T(8,128)(2,1)}, bf16[8,27,128]{2,0,1:T(8,128)(2,1)S(1)}, u32[]{:S(2)}, u32[]{:S(2)}) collective-permute-start(bf16[8,27,128]{2,0,1:T(8,128)(2,1)} %param.23), channel_id=1, source_target_pairs={{0,0},{1,64},{2,128},{3,192},{64,1},{65,65},{66,129},{67,193},{128... | collective-permute-start | bytes 165896 | tf_op jit(solution)/shard_map/ppermute | solution.py:210
  12.1 5.3 %collective-permute-done.7 = bf16[8,27,128]{2,0,1:T(8,128)(2,1)S(1)} collective-permute-done((bf16[8,27,128]{2,0,1:T(8,128)(2,1)}, bf16[8,27,128]{2,0,1:T(8,128)(2,1)S(1)}, u32[]{:S(2)}, u32[]{:S(2)}) %collective-permute-start.7) | collective-permute-done | bytes 55328 | tf_op jit(solution)/shard_map/ppermute | solution.py:210
  17.4 1.5 pad_maximum_fusion.4
  18.9 0.0 all-gather.2.cloned.1.call-update
  18.9 0.7 convert_element_type.59
  19.6 0.8 fusion.25
  20.4 0.8 fusion.20
  21.2 0.9 multiply_convert_fusion.1
  22.1 0.1 collective-permute-start.3
  22.2 0.1 collective-permute-start.2
  22.3 4.4 %collective-permute-start.1 = (bf16[288,128]{1,0:T(8,128)(2,1)S(1)}, bf16[288,128]{1,0:T(8,128)(2,1)S(1)}, u32[]{:S(2)}, u32[]{:S(2)}) collective-permute-start(bf16[288,128]{1,0:T(8,128)(2,1)S(1)} %pad_maximum_fusion.5), channel_id=1, source_target_pairs={{0,3},{1,67},{2,131},{3,195},{64,0},{65,64},{66,128},{67,192},{128... | collective-permute-start | bytes 221192 | tf_op jit(solution)/shard_map/ppermute | solution.py:241
  26.7 4.4 %collective-permute-start = (bf16[288,128]{1,0:T(8,128)(2,1)S(1)}, bf16[288,128]{1,0:T(8,128)(2,1)S(1)}, u32[]{:S(2)}, u32[]{:S(2)}) collective-permute-start(bf16[288,128]{1,0:T(8,128)(2,1)S(1)} %pad_maximum_fusion.5), channel_id=1, source_target_pairs={{0,0},{1,64},{2,128},{3,192},{64,1},{65,65},{66,129},{67,193},{128... | collective-permute-start | bytes 221192 | tf_op jit(solution)/shard_map/ppermute | solution.py:241
  31.1 1.7 collective-permute-done.1
  32.8 6.2 %collective-permute-done = bf16[288,128]{1,0:T(8,128)(2,1)S(1)} collective-permute-done((bf16[288,128]{1,0:T(8,128)(2,1)S(1)}, bf16[288,128]{1,0:T(8,128)(2,1)S(1)}, u32[]{:S(2)}, u32[]{:S(2)}) %collective-permute-start) | collective-permute-done | bytes 73760 | tf_op jit(solution)/shard_map/ppermute | solution.py:241
  39.0 0.1 fusion.29
  39.0 5.9 %collective-permute-start.5 = (bf16[4,288,128]{2,1,0:T(8,128)(2,1)S(1)}, bf16[4,288,128]{2,1,0:T(8,128)(2,1)S(1)}, u32[]{:S(2)}, u32[]{:S(2)}) collective-permute-start(bf16[4,288,128]{2,1,0:T(8,128)(2,1)S(1)} %get-tuple-element.27.mine), channel_id=1, source_target_pairs={{0,56},{8,0},{16,8},{24,16},{32,24},{40,32},{48,40},{56,48},{1,57}... | collective-permute-start | bytes 884744 | tf_op jit(solution)/shard_map/ppermute | solution.py:194
  45.0 7.5 %collective-permute-done.5.after = bf16[4,288,128]{2,1,0:T(8,128)(2,1)S(1)} collective-permute-done((bf16[4,288,128]{2,1,0:T(8,128)(2,1)S(1)}, bf16[4,288,128]{2,1,0:T(8,128)(2,1)S(1)}, u32[]{:S(2)}, u32[]{:S(2)}) %collective-permute-start.5) | collective-permute-done | bytes 294944 | tf_op jit(solution)/shard_map/ppermute | solution.py:194
  52.4 4.6 %collective-permute-done.4.before = bf16[4,288,128]{2,1,0:T(8,128)(2,1)S(1)} collective-permute-done((bf16[4,288,128]{2,1,0:T(8,128)(2,1)S(1)}, bf16[4,288,128]{2,1,0:T(8,128)(2,1)S(1)}, u32[]{:S(2)}, u32[]{:S(2)}) %collective-permute-start.4) | collective-permute-done | bytes 294944 | tf_op jit(solution)/shard_map/ppermute | solution.py:193
  57.1 0.1 pad_maximum_fusion
  57.2 0.1 collective-permute-start.6
  57.3 0.1 stack.88.ids
  57.4 1.9 %collective-permute-done.6.other = bf16[2,4,288,128]{3,2,1,0:T(8,128)(2,1)S(1)} collective-permute-done((bf16[2,4,288,128]{3,2,1,0:T(8,128)(2,1)S(1)}, bf16[2,4,288,128]{3,2,1,0:T(8,128)(2,1)S(1)}, u32[]{:S(2)}, u32[]{:S(2)}) %collective-permute-start.6) | collective-permute-done | bytes 589856 | tf_op jit(solution)/shard_map/ppermute | solution.py:196
  59.3 0.8 copy-done.6
  60.1 9.3 %shard_map.210 = (bf16[8,9,96,128]{3,2,1,0:T(8,128)(2,1)}, bf16[8,9,96,128]{3,2,1,0:T(8,128)(2,1)}, bf16[4,128,128]{2,1,0:T(8,128)(2,1)S(1)}, bf16[4,32,128]{2,1,0:T(8,128)(2,1)S(1)}) custom-call(s32[5]{0:T(128)S(1)} %stack.88.ids, bf16[4,288,128]{2,1,0:T(8,128)(2,1)S(1)} %get-tuple-element.27.mine, bf16[4,288,128]{2,1,0:T(8,128)(2,1)S(1)} %collective-permute-done.4.before, ...), custom_call_target="tpu_custom_call" | custom-call | tf_op jit(solution)/shard_map/pallas_call | solution.py:182
  69.4 4.5 %shard_map.211 = f32[4,256,128]{2,1,0:T(8,128)S(1)} custom-call(bf16[8,9,96,128]{3,2,1,0:T(8,128)(2,1)} %get-tuple-element.13.q_in, bf16[8,9,96,128]{3,2,1,0:T(8,128)(2,1)} %get-tuple-element.14.q_back, bf16[2,27,128,128]{3,2,1,0:T(8,128)(2,1)} %bitcast.47), custom_call_target="tpu_custom_call" | custom-call | tf_op jit(solution)/shard_map/pallas_call | solution.py:182
  73.9 12.0 %all_to_all.15 = f32[4,256,128]{2,1,0:T(8,128)S(1)} all-to-all(f32[4,256,128]{2,1,0:T(8,128)S(1)} %shard_map.211), channel_id=1, replica_groups=mesh['x'=4,'z'=8,'core'=2,'chan'=4] {'x'}, dimensions={0} | all-to-all | bytes 1048576 | tf_op jit(solution)/shard_map/all_to_all | solution.py:257
  86.0 0.1 multiply_convert_fusion
  86.1 2.2 %collective-permute-start.9 = (bf16[256,128]{1,0:T(8,128)(2,1)S(1)}, bf16[256,128]{1,0:T(8,128)(2,1)S(1)}, u32[]{:S(2)}, u32[]{:S(2)}) collective-permute-start(bf16[256,128]{1,0:T(8,128)(2,1)S(1)} %get-tuple-element.35), channel_id=1, source_target_pairs={{0,128},{64,192},{128,0},{192,64},{1,129},{65,193},{129,1},{193,65... | collective-permute-start | bytes 196616 | tf_op jit(solution)/shard_map/ppermute | solution.py:268
  88.3 0.9 collective-permute-start.8
  89.1 2.4 %collective-permute-start.10 = (bf16[256,128]{1,0:T(8,128)(2,1)S(1)}, bf16[256,128]{1,0:T(8,128)(2,1)S(1)}, u32[]{:S(2)}, u32[]{:S(2)}) collective-permute-start(bf16[256,128]{1,0:T(8,128)(2,1)S(1)} %get-tuple-element.35), channel_id=1, source_target_pairs={{0,64},{64,128},{128,192},{192,0},{1,65},{65,129},{129,193},{193,1... | collective-permute-start | bytes 196616 | tf_op jit(solution)/shard_map/ppermute | solution.py:268
  91.5 0.5 collective-permute-done.9
  92.0 1.8 collective-permute-done.8
  93.8 0.2 collective-permute-start.12
  94.0 1.9 %collective-permute-start.11 = (bf16[4,256,128]{2,1,0:T(8,128)(2,1)S(1)}, bf16[4,256,128]{2,1,0:T(8,128)(2,1)S(1)}, u32[]{:S(2)}, u32[]{:S(2)}) collective-permute-start(bf16[4,256,128]{2,1,0:T(8,128)(2,1)S(1)} %get-tuple-element.29.mine), channel_id=1, source_target_pairs={{0,8},{8,16},{16,24},{24,32},{32,40},{40,48},{48,56},{56,0},{1,9},... | collective-permute-start | bytes 786440 | tf_op jit(solution)/shard_map/ppermute | solution.py:193
  95.9 4.3 %collective-permute-done.12.after = bf16[4,256,128]{2,1,0:T(8,128)(2,1)S(1)} collective-permute-done((bf16[4,256,128]{2,1,0:T(8,128)(2,1)S(1)}, bf16[4,256,128]{2,1,0:T(8,128)(2,1)S(1)}, u32[]{:S(2)}, u32[]{:S(2)}) %collective-permute-start.12) | collective-permute-done | bytes 262176 | tf_op jit(solution)/shard_map/ppermute | solution.py:194
  100.3 1.3 collective-permute-done.11.before
  101.6 0.1 pad_maximum_fusion.1
  101.7 0.3 collective-permute-start.13
  101.9 1.9 %collective-permute-done.13.other = bf16[2,4,256,128]{3,2,1,0:T(8,128)(2,1)S(1)} collective-permute-done((bf16[2,4,256,128]{3,2,1,0:T(8,128)(2,1)S(1)}, bf16[2,4,256,128]{3,2,1,0:T(8,128)(2,1)S(1)}, u32[]{:S(2)}, u32[]{:S(2)}) %collective-permute-start.13) | collective-permute-done | bytes 524320 | tf_op jit(solution)/shard_map/ppermute | solution.py:196
  103.8 0.8 copy-done.8
  104.6 13.4 %shard_map.212 = (f32[4,256,128]{2,1,0:T(8,128)}, f32[8,27,8,128]{3,2,1,0:T(8,128)}, f32[8,27,8,128]{3,2,1,0:T(8,128)}) custom-call(s32[5]{0:T(128)S(1)} %stack.88.ids, bf16[4,256,128]{2,1,0:T(8,128)(2,1)S(1)} %get-tuple-element.29.mine, bf16[4,256,128]{2,1,0:T(8,128)(2,1)S(1)} %collective-permute-done.11.before, ...), custom_call_target="tpu_custom_call" | custom-call | tf_op jit(solution)/shard_map/pallas_call | solution.py:182
  118.0 0.1 collective-permute-start.19
  118.2 4.1 %shard_map.213 = (f32[8,27,8,128]{3,2,1,0:T(8,128)S(1)}, f32[8,27,8,128]{3,2,1,0:T(8,128)}) custom-call(s32[5]{0:T(128)S(1)} %stack.88.ids, bf16[4,256,128]{2,1,0:T(8,128)(2,1)S(1)} %get-tuple-element.29.mine, bf16[8,9,96,128]{3,2,1,0:T(8,128)(2,1)} %get-tuple-element.13.q_in), custom_call_target="tpu_custom_call" | custom-call | tf_op jit(solution)/shard_map/pallas_call | solution.py:182
  122.3 0.3 collective-permute-start.18
  122.6 0.9 fusion.1
  123.5 3.5 %all-to-all-start.2 = ((bf16[8,216,128]{2,1,0:T(8,128)(2,1)}), bf16[8,216,128]{2,1,0:T(8,128)(2,1)S(1)}, u32[]{:S(2)}, u32[]{:S(2)}) async-start(bf16[8,216,128]{2,1,0:T(8,128)(2,1)} %fusion.1), calls=%async_computation.2 | async-start | bytes 884736 | tf_op jit(solution)/shard_map/all_to_all | solution.py:296
  127.0 0.9 fusion
  127.8 15.5 %all-to-all-done.2 = bf16[8,216,128]{2,1,0:T(8,128)(2,1)S(1)} async-done(((bf16[8,216,128]{2,1,0:T(8,128)(2,1)}), bf16[8,216,128]{2,1,0:T(8,128)(2,1)S(1)}, u32[]{:S(2)}, u32[]{:S(2)}) %all-to-all-start.2) | async-done | bytes 442400 | tf_op jit(solution)/shard_map/all_to_all | solution.py:296
  143.3 3.5 %all-to-all-start.1 = ((bf16[8,216,128]{2,1,0:T(8,128)(2,1)}), bf16[8,216,128]{2,1,0:T(8,128)(2,1)S(1)}, u32[]{:S(2)}, u32[]{:S(2)}) async-start(bf16[8,216,128]{2,1,0:T(8,128)(2,1)} %fusion), calls=%async_computation.1 | async-start | bytes 884736 | tf_op jit(solution)/shard_map/all_to_all | solution.py:296
  146.9 2.0 %collective-permute-start.15 = (f32[256,128]{1,0:T(8,128)S(1)}, f32[256,128]{1,0:T(8,128)S(1)}, u32[]{:S(2)}, u32[]{:S(2)}) collective-permute-start(f32[256,128]{1,0:T(8,128)S(1)} %get-tuple-element.22), channel_id=1, source_target_pairs={{0,64},{1,128},{2,192},{3,0},{64,65},{65,129},{66,193},{67,1},{128... | collective-permute-start | bytes 393224 | tf_op jit(solution)/shard_map/ppermute | solution.py:287
  148.9 2.3 %collective-permute-start.17 = (f32[256,128]{1,0:T(8,128)S(1)}, f32[256,128]{1,0:T(8,128)S(1)}, u32[]{:S(2)}, u32[]{:S(2)}) collective-permute-start(f32[256,128]{1,0:T(8,128)S(1)} %get-tuple-element.23), channel_id=1, source_target_pairs={{0,192},{1,0},{2,64},{3,128},{64,193},{65,1},{66,65},{67,129},{128... | collective-permute-start | bytes 393224 | tf_op jit(solution)/shard_map/ppermute | solution.py:287
  151.2 0.6 collective-permute-start.16
  151.8 4.3 %collective-permute-start.14 = (f32[256,128]{1,0:T(8,128)S(1)}, f32[256,128]{1,0:T(8,128)S(1)}, u32[]{:S(2)}, u32[]{:S(2)}) collective-permute-start(f32[256,128]{1,0:T(8,128)S(1)} %get-tuple-element.25), channel_id=1, source_target_pairs={{0,0},{1,64},{2,128},{3,192},{64,1},{65,65},{66,129},{67,193},{128... | collective-permute-start | bytes 393224 | tf_op jit(solution)/shard_map/ppermute | solution.py:287
  156.1 0.6 collective-permute-done.15
  156.8 0.8 collective-permute-done.17
  157.5 3.5 %collective-permute-done.16 = f32[256,128]{1,0:T(8,128)S(1)} collective-permute-done((f32[256,128]{1,0:T(8,128)S(1)}, f32[256,128]{1,0:T(8,128)S(1)}, u32[]{:S(2)}, u32[]{:S(2)}) %collective-permute-start.16) | collective-permute-done | bytes 131104 | tf_op jit(solution)/shard_map/ppermute | solution.py:287
  161.0 3.8 %collective-permute-done.14 = f32[256,128]{1,0:T(8,128)S(1)} collective-permute-done((f32[256,128]{1,0:T(8,128)S(1)}, f32[256,128]{1,0:T(8,128)S(1)}, u32[]{:S(2)}, u32[]{:S(2)}) %collective-permute-start.14) | collective-permute-done | bytes 131104 | tf_op jit(solution)/shard_map/ppermute | solution.py:287
  164.8 0.7 fusion.2
  165.5 0.1 convert_reduce_fusion
  165.6 4.0 %collective-permute-start.20 = (f32[27,8,128]{2,1,0:T(8,128)S(1)}, f32[27,8,128]{2,1,0:T(8,128)S(1)}, u32[]{:S(2)}, u32[]{:S(2)}) collective-permute-start(f32[27,8,128]{2,1,0:T(8,128)S(1)} %bitcast.51), channel_id=1, source_target_pairs={{0,0},{1,64},{2,128},{3,192},{64,1},{65,65},{66,129},{67,193},{128... | collective-permute-start | bytes 331784 | tf_op jit(solution)/shard_map/ppermute | solution.py:299
  169.6 0.7 convert_reduce_fusion.1
  170.3 6.4 %collective-permute-done.20 = f32[27,8,128]{2,1,0:T(8,128)S(1)} collective-permute-done((f32[27,8,128]{2,1,0:T(8,128)S(1)}, f32[27,8,128]{2,1,0:T(8,128)S(1)}, u32[]{:S(2)}, u32[]{:S(2)}) %collective-permute-start.20) | collective-permute-done | bytes 110624 | tf_op jit(solution)/shard_map/ppermute | solution.py:299
  176.7 0.6 copy.24
  (33 shorter events, 0.3 us)
Async XLA Ops:
  7.2 62.3 %all-gather.2.cloned.1.call-start = ((), (), s32[]{:S(2)}) async-start(), calls=%async_computation.3 | async-start | bytes 1880064 | tf_op jit(solution)/shard_map/all_gather | solution.py:211
  7.2 10.2 %collective-permute-start.7 = (bf16[8,27,128]{2,0,1:T(8,128)(2,1)}, bf16[8,27,128]{2,0,1:T(8,128)(2,1)S(1)}, u32[]{:S(2)}, u32[]{:S(2)}) collective-permute-start(bf16[8,27,128]{2,0,1:T(8,128)(2,1)} %param.23), channel_id=1, source_target_pairs={{0,0},{1,64},{2,128},{3,192},{64,1},{65,65},{66,129},{67,193},{128... | collective-permute-start | bytes 165896 | tf_op jit(solution)/shard_map/ppermute | solution.py:210
  18.9 41.2 %copy-start = (bf16[864,224]{1,0:T(8,128)(2,1)S(1)}, bf16[864,224]{1,0:T(8,128)(2,1)}, u32[]{:S(2)}) copy-start(bf16[864,224]{1,0:T(8,128)(2,1)} %constant.72.clone.spread) | copy-start | bytes 1161220
  18.9 41.2 %copy-start.1 = (f32[224,128]{1,0:T(8,128)S(1)}, f32[224,128]{1,0:T(8,128)}, u32[]{:S(2)}) copy-start(f32[224,128]{1,0:T(8,128)} %constant.71.clone.local) | copy-start | bytes 344068
  18.9 41.2 %copy-start.2 = (bf16[224,32]{1,0:T(8,128)(2,1)S(1)}, bf16[224,32]{1,0:T(8,128)(2,1)}, u32[]{:S(2)}) copy-start(bf16[224,32]{1,0:T(8,128)(2,1)} %constant.70.clone.pick_back) | copy-start | bytes 43012
  18.9 41.2 %copy-start.3 = (bf16[224,32]{1,0:T(8,128)(2,1)S(1)}, bf16[224,32]{1,0:T(8,128)(2,1)}, u32[]{:S(2)}) copy-start(bf16[224,32]{1,0:T(8,128)(2,1)} %constant.69.clone.pick) | copy-start | bytes 43012
  18.9 41.2 %copy-start.4 = (bf16[16,128]{1,0:T(8,128)(2,1)S(1)}, bf16[16,128]{1,0:T(8,128)(2,1)}, u32[]{:S(2)}) copy-start(bf16[16,128]{1,0:T(8,128)(2,1)} %constant.74.clone.sources) | copy-start | bytes 12292
  22.1 9.0 %collective-permute-start.3 = (bf16[288,128]{1,0:T(8,128)(2,1)S(1)}, bf16[288,128]{1,0:T(8,128)(2,1)S(1)}, u32[]{:S(2)}, u32[]{:S(2)}) collective-permute-start(bf16[288,128]{1,0:T(8,128)(2,1)S(1)} %pad_maximum_fusion.5), channel_id=1, source_target_pairs={{0,1},{1,65},{2,129},{3,193},{64,2},{65,66},{66,130},{67,194},{128... | collective-permute-start | bytes 221192 | tf_op jit(solution)/shard_map/ppermute | solution.py:241
  22.2 8.9 %collective-permute-start.2 = (bf16[288,128]{1,0:T(8,128)(2,1)S(1)}, bf16[288,128]{1,0:T(8,128)(2,1)S(1)}, u32[]{:S(2)}, u32[]{:S(2)}) collective-permute-start(bf16[288,128]{1,0:T(8,128)(2,1)S(1)} %pad_maximum_fusion.5), channel_id=1, source_target_pairs={{0,2},{1,66},{2,130},{3,194},{64,3},{65,67},{66,131},{67,195},{128... | collective-permute-start | bytes 221192 | tf_op jit(solution)/shard_map/ppermute | solution.py:241
  22.3 10.5 %collective-permute-start.1 = (bf16[288,128]{1,0:T(8,128)(2,1)S(1)}, bf16[288,128]{1,0:T(8,128)(2,1)S(1)}, u32[]{:S(2)}, u32[]{:S(2)}) collective-permute-start(bf16[288,128]{1,0:T(8,128)(2,1)S(1)} %pad_maximum_fusion.5), channel_id=1, source_target_pairs={{0,3},{1,67},{2,131},{3,195},{64,0},{65,64},{66,128},{67,192},{128... | collective-permute-start | bytes 221192 | tf_op jit(solution)/shard_map/ppermute | solution.py:241
  26.7 12.2 %collective-permute-start = (bf16[288,128]{1,0:T(8,128)(2,1)S(1)}, bf16[288,128]{1,0:T(8,128)(2,1)S(1)}, u32[]{:S(2)}, u32[]{:S(2)}) collective-permute-start(bf16[288,128]{1,0:T(8,128)(2,1)S(1)} %pad_maximum_fusion.5), channel_id=1, source_target_pairs={{0,0},{1,64},{2,128},{3,192},{64,1},{65,65},{66,129},{67,193},{128... | collective-permute-start | bytes 221192 | tf_op jit(solution)/shard_map/ppermute | solution.py:241
  39.0 13.4 %collective-permute-start.5 = (bf16[4,288,128]{2,1,0:T(8,128)(2,1)S(1)}, bf16[4,288,128]{2,1,0:T(8,128)(2,1)S(1)}, u32[]{:S(2)}, u32[]{:S(2)}) collective-permute-start(bf16[4,288,128]{2,1,0:T(8,128)(2,1)S(1)} %get-tuple-element.27.mine), channel_id=1, source_target_pairs={{0,56},{8,0},{16,8},{24,16},{32,24},{40,32},{48,40},{56,48},{1,57}... | collective-permute-start | bytes 884744 | tf_op jit(solution)/shard_map/ppermute | solution.py:194
  45.0 12.1 %collective-permute-start.4 = (bf16[4,288,128]{2,1,0:T(8,128)(2,1)S(1)}, bf16[4,288,128]{2,1,0:T(8,128)(2,1)S(1)}, u32[]{:S(2)}, u32[]{:S(2)}) collective-permute-start(bf16[4,288,128]{2,1,0:T(8,128)(2,1)S(1)} %get-tuple-element.27.mine), channel_id=1, source_target_pairs={{0,8},{8,16},{16,24},{24,32},{32,40},{40,48},{48,56},{56,0},{1,9},... | collective-permute-start | bytes 884744 | tf_op jit(solution)/shard_map/ppermute | solution.py:193
  57.2 2.1 %collective-permute-start.6 = (bf16[2,4,288,128]{3,2,1,0:T(8,128)(2,1)S(1)}, bf16[2,4,288,128]{3,2,1,0:T(8,128)(2,1)S(1)}, u32[]{:S(2)}, u32[]{:S(2)}) collective-permute-start(bf16[2,4,288,128]{3,2,1,0:T(8,128)(2,1)S(1)} %pad_maximum_fusion), channel_id=1, source_target_pairs={{0,4},{4,0},{1,5},{5,1},{2,6},{6,2},{3,7},{7,3},{8,12},{12,8},{9,1... | collective-permute-start | bytes 1769480 | tf_op jit(solution)/shard_map/ppermute | solution.py:196
  59.3 0.8 copy-start.6
  86.1 5.9 %collective-permute-start.9 = (bf16[256,128]{1,0:T(8,128)(2,1)S(1)}, bf16[256,128]{1,0:T(8,128)(2,1)S(1)}, u32[]{:S(2)}, u32[]{:S(2)}) collective-permute-start(bf16[256,128]{1,0:T(8,128)(2,1)S(1)} %get-tuple-element.35), channel_id=1, source_target_pairs={{0,128},{64,192},{128,0},{192,64},{1,129},{65,193},{129,1},{193,65... | collective-permute-start | bytes 196616 | tf_op jit(solution)/shard_map/ppermute | solution.py:268
  88.3 5.5 %collective-permute-start.8 = (bf16[256,128]{1,0:T(8,128)(2,1)S(1)}, bf16[256,128]{1,0:T(8,128)(2,1)S(1)}, u32[]{:S(2)}, u32[]{:S(2)}) collective-permute-start(bf16[256,128]{1,0:T(8,128)(2,1)S(1)} %get-tuple-element.35), channel_id=1, source_target_pairs={{0,192},{64,0},{128,64},{192,128},{1,193},{65,1},{129,65},{193,129... | collective-permute-start | bytes 196616 | tf_op jit(solution)/shard_map/ppermute | solution.py:268
  89.1 4.6 %collective-permute-start.10 = (bf16[256,128]{1,0:T(8,128)(2,1)S(1)}, bf16[256,128]{1,0:T(8,128)(2,1)S(1)}, u32[]{:S(2)}, u32[]{:S(2)}) collective-permute-start(bf16[256,128]{1,0:T(8,128)(2,1)S(1)} %get-tuple-element.35), channel_id=1, source_target_pairs={{0,64},{64,128},{128,192},{192,0},{1,65},{65,129},{129,193},{193,1... | collective-permute-start | bytes 196616 | tf_op jit(solution)/shard_map/ppermute | solution.py:268
  93.8 6.5 %collective-permute-start.12 = (bf16[4,256,128]{2,1,0:T(8,128)(2,1)S(1)}, bf16[4,256,128]{2,1,0:T(8,128)(2,1)S(1)}, u32[]{:S(2)}, u32[]{:S(2)}) collective-permute-start(bf16[4,256,128]{2,1,0:T(8,128)(2,1)S(1)} %get-tuple-element.29.mine), channel_id=1, source_target_pairs={{0,56},{8,0},{16,8},{24,16},{32,24},{40,32},{48,40},{56,48},{1,57}... | collective-permute-start | bytes 786440 | tf_op jit(solution)/shard_map/ppermute | solution.py:194
  94.0 7.6 %collective-permute-start.11 = (bf16[4,256,128]{2,1,0:T(8,128)(2,1)S(1)}, bf16[4,256,128]{2,1,0:T(8,128)(2,1)S(1)}, u32[]{:S(2)}, u32[]{:S(2)}) collective-permute-start(bf16[4,256,128]{2,1,0:T(8,128)(2,1)S(1)} %get-tuple-element.29.mine), channel_id=1, source_target_pairs={{0,8},{8,16},{16,24},{24,32},{32,40},{40,48},{48,56},{56,0},{1,9},... | collective-permute-start | bytes 786440 | tf_op jit(solution)/shard_map/ppermute | solution.py:193
  101.7 2.2 %collective-permute-start.13 = (bf16[2,4,256,128]{3,2,1,0:T(8,128)(2,1)S(1)}, bf16[2,4,256,128]{3,2,1,0:T(8,128)(2,1)S(1)}, u32[]{:S(2)}, u32[]{:S(2)}) collective-permute-start(bf16[2,4,256,128]{3,2,1,0:T(8,128)(2,1)S(1)} %pad_maximum_fusion.1), channel_id=1, source_target_pairs={{0,4},{4,0},{1,5},{5,1},{2,6},{6,2},{3,7},{7,3},{8,12},{12,8},{9,1... | collective-permute-start | bytes 1572872 | tf_op jit(solution)/shard_map/ppermute | solution.py:196
  103.8 0.8 copy-start.8
  118.0 4.6 %copy-start.5 = (f32[8,27,8,128]{3,2,1,0:T(8,128)S(1)}, f32[8,27,8,128]{3,2,1,0:T(8,128)}, u32[]{:S(2)}) copy-start(f32[8,27,8,128]{3,2,1,0:T(8,128)} %get-tuple-element.20) | copy-start | bytes 2654212
  118.0 4.6 %collective-permute-start.19 = (f32[8,27,8,128]{3,2,1,0:T(8,128)}, f32[8,27,8,128]{3,2,1,0:T(8,128)S(1)}, u32[]{:S(2)}, u32[]{:S(2)}) collective-permute-start(f32[8,27,8,128]{3,2,1,0:T(8,128)} %get-tuple-element.21), channel_id=1, source_target_pairs={{0,4},{4,0},{1,5},{5,1},{2,6},{6,2},{3,7},{7,3},{8,12},{12,8},{9,1... | collective-permute-start | bytes 2654216 | tf_op jit(solution)/shard_map/ppermute | solution.py:295
  122.3 4.7 %collective-permute-start.18 = (f32[8,27,8,128]{3,2,1,0:T(8,128)}, f32[8,27,8,128]{3,2,1,0:T(8,128)S(1)}, u32[]{:S(2)}, u32[]{:S(2)}) collective-permute-start(f32[8,27,8,128]{3,2,1,0:T(8,128)} %get-tuple-element.19), channel_id=1, source_target_pairs={{0,4},{4,0},{1,5},{5,1},{2,6},{6,2},{3,7},{7,3},{8,12},{12,8},{9,1... | collective-permute-start | bytes 2654216 | tf_op jit(solution)/shard_map/ppermute | solution.py:295
  123.5 19.8 %all-to-all-start.2 = ((bf16[8,216,128]{2,1,0:T(8,128)(2,1)}), bf16[8,216,128]{2,1,0:T(8,128)(2,1)S(1)}, u32[]{:S(2)}, u32[]{:S(2)}) async-start(bf16[8,216,128]{2,1,0:T(8,128)(2,1)} %fusion.1), calls=%async_computation.2 | async-start | bytes 884736 | tf_op jit(solution)/shard_map/all_to_all | solution.py:296
  127.0 19.8 %copy-start.7 = (f32[4,256,128]{2,1,0:T(8,128)S(1)}, f32[4,256,128]{2,1,0:T(8,128)}, u32[]{:S(2)}) copy-start(f32[4,256,128]{2,1,0:T(8,128)} %get-tuple-element.17) | copy-start | bytes 1572868
  143.3 26.2 %all-to-all-start.1 = ((bf16[8,216,128]{2,1,0:T(8,128)(2,1)}), bf16[8,216,128]{2,1,0:T(8,128)(2,1)S(1)}, u32[]{:S(2)}, u32[]{:S(2)}) async-start(bf16[8,216,128]{2,1,0:T(8,128)(2,1)} %fusion), calls=%async_computation.1 | async-start | bytes 884736 | tf_op jit(solution)/shard_map/all_to_all | solution.py:296
  146.9 9.9 %collective-permute-start.15 = (f32[256,128]{1,0:T(8,128)S(1)}, f32[256,128]{1,0:T(8,128)S(1)}, u32[]{:S(2)}, u32[]{:S(2)}) collective-permute-start(f32[256,128]{1,0:T(8,128)S(1)} %get-tuple-element.22), channel_id=1, source_target_pairs={{0,64},{1,128},{2,192},{3,0},{64,65},{65,129},{66,193},{67,1},{128... | collective-permute-start | bytes 393224 | tf_op jit(solution)/shard_map/ppermute | solution.py:287
  148.9 8.6 %collective-permute-start.17 = (f32[256,128]{1,0:T(8,128)S(1)}, f32[256,128]{1,0:T(8,128)S(1)}, u32[]{:S(2)}, u32[]{:S(2)}) collective-permute-start(f32[256,128]{1,0:T(8,128)S(1)} %get-tuple-element.23), channel_id=1, source_target_pairs={{0,192},{1,0},{2,64},{3,128},{64,193},{65,1},{66,65},{67,129},{128... | collective-permute-start | bytes 393224 | tf_op jit(solution)/shard_map/ppermute | solution.py:287
  151.2 9.8 %collective-permute-start.16 = (f32[256,128]{1,0:T(8,128)S(1)}, f32[256,128]{1,0:T(8,128)S(1)}, u32[]{:S(2)}, u32[]{:S(2)}) collective-permute-start(f32[256,128]{1,0:T(8,128)S(1)} %get-tuple-element.24), channel_id=1, source_target_pairs={{0,128},{1,192},{2,0},{3,64},{64,129},{65,193},{66,1},{67,65},{128... | collective-permute-start | bytes 393224 | tf_op jit(solution)/shard_map/ppermute | solution.py:287
  151.8 13.0 %collective-permute-start.14 = (f32[256,128]{1,0:T(8,128)S(1)}, f32[256,128]{1,0:T(8,128)S(1)}, u32[]{:S(2)}, u32[]{:S(2)}) collective-permute-start(f32[256,128]{1,0:T(8,128)S(1)} %get-tuple-element.25), channel_id=1, source_target_pairs={{0,0},{1,64},{2,128},{3,192},{64,1},{65,65},{66,129},{67,193},{128... | collective-permute-start | bytes 393224 | tf_op jit(solution)/shard_map/ppermute | solution.py:287
  165.6 11.1 %collective-permute-start.20 = (f32[27,8,128]{2,1,0:T(8,128)S(1)}, f32[27,8,128]{2,1,0:T(8,128)S(1)}, u32[]{:S(2)}, u32[]{:S(2)}) collective-permute-start(f32[27,8,128]{2,1,0:T(8,128)S(1)} %bitcast.51), channel_id=1, source_target_pairs={{0,0},{1,64},{2,128},{3,192},{64,1},{65,65},{66,129},{67,193},{128... | collective-permute-start | bytes 331784 | tf_op jit(solution)/shard_map/ppermute | solution.py:299
Sparse Core Ops, SparseCore 0:
  19.0 42.6 all-gather.1

commit v2 on v1

--- a/solution.py
+++ b/solution.py
@@ -60,12 +60,10 @@
 
 def fill(out, base, matches, rows, pick, local, spread):
     count = rows.shape[0]
-    padded = []
-    for brick in range(2):
-        chosen = dot(pick, matches[:, brick * count : (brick + 1) * count])
-        select = (chosen * jnp.concatenate([local] * (count // 128), axis=1)).astype(BF)
-        padded.append(dot(select, rows).astype(BF))
-    wide = dot(spread, jnp.concatenate(padded, axis=1)).astype(BF)
+    chosen = dot(pick, matches)
+    select = (chosen * jnp.concatenate([local] * (count // 64), axis=1)).astype(BF)
+    found = dot(jnp.concatenate([select[:, :count], select[:, count:]], axis=0), rows).astype(BF)
+    wide = dot(spread, jnp.concatenate([found[:CELLS], found[CELLS:]], axis=1)).astype(BF)
     for brick in range(2):
         out[base + brick] = wide[:, brick * 128 : (brick + 1) * 128].reshape(9, 96, 128)
 
@@ -152,20 +150,33 @@
     weight_blocks(q_in, own[...].reshape(512, 128), keep, send, scratch, ids[2])
 
 
-def apply_second(
-    ids, mine, before, after, other, matched, own, weights, pick, pick_back, local, spread, lanes, sources,
-    reduced, keep, send, q_hidden, q_back, scratch,
+def weigh_second(
+    ids, mine, before, after, other, matched, own, pick, pick_back, local, spread, lanes, sources,
+    keep, send, q_hidden, scratch,
 ):
     @pl.loop(0, 4)
     def _(turn):
         at = (ids[0] + turn) & 3
         views = around(ids, mine, before, after, other, turn)
-        found = dot(matched[at], lanes[...]).astype(BF)
+        found = dot(matched[at], lanes[:, :768]).astype(BF)
         rows = [views[0][0:128, :]]
         rows += [view[device % 2 * 64 : device % 2 * 64 + 64, :] for device, view in enumerate(views[1:])]
-        fill(q_hidden, at * 2, found[:, :768], jnp.concatenate(rows, 0), pick[...], local[...], spread[...])
+        fill(q_hidden, at * 2, found, jnp.concatenate(rows, 0), pick[...], local[...], spread[...])
+
+    weight_blocks(q_hidden, own[...].reshape(512, 128), keep, send, scratch, ids[2])
+
+
+def apply_second(
+    ids, mine, before, after, other, matched, q_hidden, weights, pick, pick_back, local, spread, lanes, sources,
+    reduced, q_back,
+):
+    @pl.loop(0, 4)
+    def _(turn):
+        at = (ids[0] + turn) & 3
+        views = around(ids, mine, before, after, other, turn)
+        found = dot(matched[at], lanes[:, 768:]).astype(BF)
         rows = jnp.concatenate([view[128:256, :] for view in views], 0)
-        fill(q_back, at * 2, found[:, 768:], rows, pick_back[...], local[...], spread[...])
+        fill(q_back, at * 2, found, rows, pick_back[...], local[...], spread[...])
 
     forward = convolve(q_hidden, weights.at[1])
     backward = convolve_back(q_back, weights.at[0])
@@ -173,7 +184,6 @@
         turn = (at - ids[1]) & 3
         reduced[turn, 0:128, :] = forward[at * 128 : (at + 1) * 128]
         reduced[turn, 128:256, :] = backward[at * 128 : (at + 1) * 128]
-    weight_blocks(q_hidden, own[...].reshape(512, 128), keep, send, scratch, ids[2])
 
 
 def call(kernel, outs, scratch, *args):
@@ -189,6 +199,18 @@
     )(*args)
 
 
+def turn_over(value, target):
+    places = [(a, b) for a in range(4) for b in range(4)]
+    moved = {place: tuple(v % 4 for v in target(*place)) for place in places}
+    still = [place for place in places if moved[place] == place]
+    for at, place in enumerate(still):
+        moved[place] = still[(at + 1) % len(still)]
+    came = lax.ppermute(value, ("x", "chan"), [(p[0] * 4 + p[1], q[0] * 4 + q[1]) for p, q in moved.items()])
+    if not still:
+        return came
+    return jnp.where(lax.axis_index("x") == lax.axis_index("chan"), value, came)
+
+
 def spread_out(mine):
     before = lax.ppermute(mine, "z", [(i, (i + 1) % 8) for i in range(8)])
     after = lax.ppermute(mine, "z", [(i, (i - 1) % 8) for i in range(8)])
@@ -205,9 +227,8 @@
     chan = lax.axis_index("chan")
     z = lax.axis_index("z")
     ids = jnp.stack([x, chan, core, (z == 0).astype(jnp.int32), (z == 7).astype(jnp.int32)]).astype(jnp.int32)
-    swap = [(a * 4 + b, b * 4 + a) for a in range(4) for b in range(4)]
-
-    shards = jnp.stack([weight_first, lax.ppermute(weight_second, ("x", "chan"), swap)])
+
+    shards = jnp.stack([weight_first, turn_over(weight_second, lambda a, b: (b, a))])
     blocks = jnp.transpose(lax.all_gather(shards, ("z", "core"), axis=1, tiled=True), (0, 2, 1, 3))
 
     active = mask.astype(F32)[:, None]
@@ -238,7 +259,7 @@
     packed = jnp.concatenate([masked[:64], grad_second, compact, masked[64:]], 0)
     turned = jnp.stack(
         [
-            lax.ppermute(packed, ("x", "chan"), [(a * 4 + b, b * 4 + (a - r) % 4) for a in range(4) for b in range(4)])
+            turn_over(packed, lambda a, b: (b, a - r))
             for r in range(4)
         ]
     )
@@ -270,34 +291,51 @@
     pieces = shape((8, 27, 8, 128), F32)
     pair = pltpu.VMEM((2, 128, 128), F32)
     keep1, send1 = call(weigh_first, [pieces, pieces], [pltpu.VMEM((4, 128, 128), BF), pair], ids, along, q_in)
-    reduced, keep2, send2 = call(
-        apply_second,
-        [shape((4, 256, 128), F32), pieces, pieces],
-        [pltpu.VMEM((8, 9, 96, 128), BF), pltpu.VMEM((8, 9, 96, 128), BF), pair],
+
+    def both_cores(keep, send):
+        return keep + lax.ppermute(send, "core", [(0, 1), (1, 0)])
+
+    first_mine = both_cores(keep1, send1)
+    first_sum = lax.psum_scatter(first_mine, "z", scatter_dimension=0, tiled=True).reshape(27, 8, 128)
+    before, after, other, _ = lax.optimization_barrier((*spread_out(along), first_mine))
+    keep2, send2, q_hidden = call(
+        weigh_second,
+        [pieces, pieces, columns],
+        [pair],
         ids,
         along,
-        *spread_out(along),
+        before,
+        after,
+        other,
         matched,
         own,
+        *consts,
+    )
+    second_mine = both_cores(keep2, send2).astype(BF).reshape(8, 216, 128)
+    q_hidden, second_mine = lax.optimization_barrier((q_hidden, second_mine))
+    moved = lax.all_to_all(second_mine, "z", 0, 0, tiled=True)
+    (reduced,) = call(
+        apply_second,
+        [shape((4, 256, 128), F32)],
+        [pltpu.VMEM((8, 9, 96, 128), BF)],
+        ids,
+        along,
+        before,
+        after,
+        other,
+        matched,
+        q_hidden,
         blocks,
         *consts,
     )
     total = None
     for r in range(4):
-        part = lax.ppermute(
-            reduced[r], ("x", "chan"), [(a * 4 + b, (b + r) % 4 * 4 + a) for a in range(4) for b in range(4)]
-        )
+        part = turn_over(reduced[r], lambda a, b: (b + r, a))
         total = part if total is None else total + part
     output = (active * total[0:128]).astype(BF)
     features_grad = (active * total[128:256]).astype(BF)
 
-    def settle(keep, send):
-        mine = keep + lax.ppermute(send, "core", [(0, 1), (1, 0)])
-        moved = lax.all_to_all(mine.astype(BF).reshape(8, 27 * 8, 128), "z", 0, 0, tiled=True)
-        return jnp.sum(moved.astype(F32), axis=0).reshape(27, 8, 128)
-
-    second_sum = lax.ppermute(settle(keep2, send2), ("x", "chan"), swap)
-    first_sum = settle(keep1, send1)
+    second_sum = turn_over(jnp.sum(moved.astype(F32), axis=0).reshape(27, 8, 128), lambda a, b: (b, a))
     return (
         output,
         features_grad,

time: 185 us -> 159 us (0.86)
  waiting for transfers between devices: 67.5 us -> 49.2 us
  starting transfers between devices: 48.3 us -> 36.6 us
  blocking collectives: 12 us -> 14 us
    all_to_all x2 -> x1, waiting for transfers between devices: 15.5 us -> 0.01 us  [on_device(): moved = lax.all_to_all(second_mine, 'z', 0, 0, tiled=True)]
    ppermute x12, starting transfers between devices: 27.5 us -> 19.4 us  [the longest x10 19.3 us: turn_over(): lax.ppermute(value, ('x', 'chan'), [(p[0] * 4 + p[1], q[0] * 4 + q[1]) fo...]
    ppermute x2, waiting for transfers between devices: 11.8 us -> 8.24 us  [spread_out(): after = lax.ppermute(mine, 'z', [(i, (i - 1) % 8) for i in range(8)])]
    all_to_all x2 -> x1, starting transfers between devices: 6.93 us -> 3.47 us  [on_device(): moved = lax.all_to_all(second_mine, 'z', 0, 0, tiled=True)]
    ppermute x12, waiting for transfers between devices: 28.2 us -> 30.6 us  [the longest x10 27.9 us: turn_over(): lax.ppermute(value, ('x', 'chan'), [(p[0] * 4 + p[1], q[0] * 4 + q[1]) fo...]
    all_to_all x1, blocking collectives: 12 us -> 14 us  [on_device(): summed = jnp.sum(lax.all_to_all(partial, 'x', 0, 0, tiled=True), axis=0)]
    pallas_call x4 -> x5, Pallas kernels: 31.3 us -> 32.9 us  [call(): pl.pallas_call(kernel, out_shape=outs, in_specs=[smem if value.dtype == j...]
  transfers between devices with their start and end apart: 24 -> 24, of which waited for: 17 -> 18; matrix products, arithmetic and copies ran while one was open for 4% -> 5% of each run, Pallas kernels for 7% -> 13%
where the time goes in v2:
time: 159 us; the launch traced here: 158 us
  waiting for transfers between devices  49.2 us (31%)
  starting transfers between devices  36.6 us (23%)
  Pallas kernels  32.9 us (21%)
  between operations  14.3 us (9%)
  blocking collectives  14 us (9%)
  other arithmetic  8.89 us (6%)
  local copies, waits for them, and re-layouts  2.56 us (2%)
    pallas_call x5, Pallas kernels, call(): pl.pallas_call(kernel, out_shape=outs, in_specs=[smem if value.dtype == j...  32.9 us
    ppermute x10, waiting for transfers between devices, turn_over(): lax.ppermute(value, ('x', 'chan'), [(p[0] * 4 + p[1], q[0] * 4 + q[1]) fo...  27.9 us
    ppermute x10, starting transfers between devices, turn_over(): lax.ppermute(value, ('x', 'chan'), [(p[0] * 4 + p[1], q[0] * 4 + q[1]) fo...  19.3 us
    all_to_all x1, blocking collectives, on_device(): summed = jnp.sum(lax.all_to_all(partial, 'x', 0, 0, tiled=True), axis=0)  14 us
    ppermute x2, waiting for transfers between devices, spread_out(): after = lax.ppermute(mine, 'z', [(i, (i - 1) % 8) for i in range(8)])  8.24 us
    ppermute x2, starting transfers between devices, spread_out(): after = lax.ppermute(mine, 'z', [(i, (i - 1) % 8) for i in range(8)])  6.28 us
    ppermute x2, waiting for transfers between devices, spread_out(): before = lax.ppermute(mine, 'z', [(i, (i + 1) % 8) for i in range(8)])  5.55 us
    ppermute x3, starting transfers between devices, on_device(): lax.ppermute(packed, 'x', [(a, (a - r) % 4) for a in range(4)])  5.4 us
  transfers between devices with their start and end apart: 24, of which 18 were waited for; matrix products, arithmetic and copies ran while one was open for 5% of the time, Pallas kernels for 13%

profile of v2, /device:TPU:6, one launch (start us, length us, event | category | flops | bytes accessed | tf_op | source)
XLA Modules:
  0.0 158.4 jit_solution(17732305226267186190)
XLA Ops:
  7.2 0.0 all-gather.2.cloned.1.call-start
  7.2 3.0 %collective-permute-start.7 = (bf16[8,27,128]{2,0,1:T(8,128)(2,1)}, bf16[8,27,128]{2,0,1:T(8,128)(2,1)S(1)}, u32[]{:S(2)}, u32[]{:S(2)}) collective-permute-start(bf16[8,27,128]{2,0,1:T(8,128)(2,1)} %param.23), channel_id=1, source_target_pairs={{0,65},{1,64},{2,128},{3,192},{64,1},{65,130},{66,129},{67,193},{1... | collective-permute-start | bytes 165896 | tf_op jit(solution)/shard_map/ppermute | solution.py:208
  10.2 5.4 %collective-permute-done.7 = bf16[8,27,128]{2,0,1:T(8,128)(2,1)S(1)} collective-permute-done((bf16[8,27,128]{2,0,1:T(8,128)(2,1)}, bf16[8,27,128]{2,0,1:T(8,128)(2,1)S(1)}, u32[]{:S(2)}, u32[]{:S(2)}) %collective-permute-start.7) | collective-permute-done | bytes 55328 | tf_op jit(solution)/shard_map/ppermute | solution.py:208
  15.6 1.5 pad_maximum_fusion.4
  17.1 0.0 all-gather.2.cloned.1.call-update
  17.1 0.0 reduce-scatter.4.cloned.1.call-start
  17.1 0.7 convert_element_type.53
  17.8 0.8 fusion.24
  18.6 0.8 fusion.19
  19.4 0.0 copy-start
  19.5 0.9 multiply_convert_fusion.1
  20.4 3.0 %collective-permute-start = (bf16[288,128]{1,0:T(8,128)(2,1)S(1)}, bf16[288,128]{1,0:T(8,128)(2,1)S(1)}, u32[]{:S(2)}, u32[]{:S(2)}) collective-permute-start(bf16[288,128]{1,0:T(8,128)(2,1)S(1)} %pad_maximum_fusion.5), channel_id=1, source_target_pairs={{0,65},{1,64},{2,128},{3,192},{64,1},{65,130},{66,129},{67,193},{1... | collective-permute-start | bytes 221192 | tf_op jit(solution)/shard_map/ppermute | solution.py:208
  23.5 3.1 %collective-permute-start.1 = (bf16[288,128]{1,0:T(8,128)(2,1)S(1)}, bf16[288,128]{1,0:T(8,128)(2,1)S(1)}, u32[]{:S(2)}, u32[]{:S(2)}) collective-permute-start(bf16[288,128]{1,0:T(8,128)(2,1)S(1)} %pad_maximum_fusion.5), channel_id=1, source_target_pairs={{0,3},{1,67},{2,131},{3,195},{64,0},{65,64},{66,128},{67,192},{128... | collective-permute-start | bytes 221192 | tf_op jit(solution)/shard_map/ppermute | solution.py:208
  26.5 0.6 collective-permute-start.3
  27.1 7.2 %collective-permute-done = bf16[288,128]{1,0:T(8,128)(2,1)S(1)} collective-permute-done((bf16[288,128]{1,0:T(8,128)(2,1)S(1)}, bf16[288,128]{1,0:T(8,128)(2,1)S(1)}, u32[]{:S(2)}, u32[]{:S(2)}) %collective-permute-start) | collective-permute-done | bytes 73760 | tf_op jit(solution)/shard_map/ppermute | solution.py:208
  34.3 0.5 collective-permute-done.3
  34.9 0.1 fusion.28
  34.9 5.9 %collective-permute-start.5 = (bf16[4,288,128]{2,1,0:T(8,128)(2,1)S(1)}, bf16[4,288,128]{2,1,0:T(8,128)(2,1)S(1)}, u32[]{:S(2)}, u32[]{:S(2)}) collective-permute-start(bf16[4,288,128]{2,1,0:T(8,128)(2,1)S(1)} %get-tuple-element.37.mine), channel_id=1, source_target_pairs={{0,56},{8,0},{16,8},{24,16},{32,24},{40,32},{48,40},{56,48},{1,57}... | collective-permute-start | bytes 884744 | tf_op jit(solution)/shard_map/ppermute | solution.py:216
  40.8 7.6 %collective-permute-done.5.after = bf16[4,288,128]{2,1,0:T(8,128)(2,1)S(1)} collective-permute-done((bf16[4,288,128]{2,1,0:T(8,128)(2,1)S(1)}, bf16[4,288,128]{2,1,0:T(8,128)(2,1)S(1)}, u32[]{:S(2)}, u32[]{:S(2)}) %collective-permute-start.5) | collective-permute-done | bytes 294944 | tf_op jit(solution)/shard_map/ppermute | solution.py:216
  48.4 4.1 %collective-permute-done.4.before = bf16[4,288,128]{2,1,0:T(8,128)(2,1)S(1)} collective-permute-done((bf16[4,288,128]{2,1,0:T(8,128)(2,1)S(1)}, bf16[4,288,128]{2,1,0:T(8,128)(2,1)S(1)}, u32[]{:S(2)}, u32[]{:S(2)}) %collective-permute-start.4) | collective-permute-done | bytes 294944 | tf_op jit(solution)/shard_map/ppermute | solution.py:215
  52.5 0.1 pad_maximum_fusion
  52.6 0.1 collective-permute-start.6
  52.7 0.1 stack.88.ids
  52.8 1.9 %collective-permute-done.6.other = bf16[2,4,288,128]{3,2,1,0:T(8,128)(2,1)S(1)} collective-permute-done((bf16[2,4,288,128]{3,2,1,0:T(8,128)(2,1)S(1)}, bf16[2,4,288,128]{3,2,1,0:T(8,128)(2,1)S(1)}, u32[]{:S(2)}, u32[]{:S(2)}) %collective-permute-start.6) | collective-permute-done | bytes 589856 | tf_op jit(solution)/shard_map/ppermute | solution.py:218
  54.7 0.8 copy-done.6
  55.5 8.3 %shard_map.210 = (bf16[8,9,96,128]{3,2,1,0:T(8,128)(2,1)}, bf16[8,9,96,128]{3,2,1,0:T(8,128)(2,1)}, bf16[4,128,128]{2,1,0:T(8,128)(2,1)S(1)}, bf16[4,32,128]{2,1,0:T(8,128)(2,1)S(1)}) custom-call(s32[5]{0:T(128)S(1)} %stack.88.ids, bf16[4,288,128]{2,1,0:T(8,128)(2,1)S(1)} %get-tuple-element.37.mine, bf16[4,288,128]{2,1,0:T(8,128)(2,1)S(1)} %collective-permute-done.4.before, ...), custom_call_target="tpu_custom_call" | custom-call | tf_op jit(solution)/shard_map/pallas_call | solution.py:192
  63.8 4.5 %shard_map.211 = f32[4,256,128]{2,1,0:T(8,128)S(1)} custom-call(bf16[8,9,96,128]{3,2,1,0:T(8,128)(2,1)} %get-tuple-element.18.q_in, bf16[8,9,96,128]{3,2,1,0:T(8,128)(2,1)} %get-tuple-element.19.q_back, bf16[2,27,128,128]{3,2,1,0:T(8,128)(2,1)} %bitcast.52), custom_call_target="tpu_custom_call" | custom-call | tf_op jit(solution)/shard_map/pallas_call | solution.py:192
  68.3 14.0 %all_to_all.10 = f32[4,256,128]{2,1,0:T(8,128)S(1)} all-to-all(f32[4,256,128]{2,1,0:T(8,128)S(1)} %shard_map.211), channel_id=1, replica_groups=mesh['x'=4,'z'=8,'core'=2,'chan'=4] {'x'}, dimensions={0} | all-to-all | bytes 1048576 | tf_op jit(solution)/shard_map/all_to_all | solution.py:278
  82.4 0.1 multiply_convert_fusion
  82.5 2.2 %collective-permute-start.9 = (bf16[256,128]{1,0:T(8,128)(2,1)S(1)}, bf16[256,128]{1,0:T(8,128)(2,1)S(1)}, u32[]{:S(2)}, u32[]{:S(2)}) collective-permute-start(bf16[256,128]{1,0:T(8,128)(2,1)S(1)} %get-tuple-element.45), channel_id=1, source_target_pairs={{0,128},{64,192},{128,0},{192,64},{1,129},{65,193},{129,1},{193,65... | collective-permute-start | bytes 196616 | tf_op jit(solution)/shard_map/ppermute | solution.py:289
  84.7 0.9 collective-permute-start.8
  85.5 2.4 %collective-permute-start.10 = (bf16[256,128]{1,0:T(8,128)(2,1)S(1)}, bf16[256,128]{1,0:T(8,128)(2,1)S(1)}, u32[]{:S(2)}, u32[]{:S(2)}) collective-permute-start(bf16[256,128]{1,0:T(8,128)(2,1)S(1)} %get-tuple-element.45), channel_id=1, source_target_pairs={{0,64},{64,128},{128,192},{192,0},{1,65},{65,129},{129,193},{193,1... | collective-permute-start | bytes 196616 | tf_op jit(solution)/shard_map/ppermute | solution.py:289
  87.9 0.6 collective-permute-done.9
  88.5 1.7 %collective-permute-done.8 = bf16[256,128]{1,0:T(8,128)(2,1)S(1)} collective-permute-done((bf16[256,128]{1,0:T(8,128)(2,1)S(1)}, bf16[256,128]{1,0:T(8,128)(2,1)S(1)}, u32[]{:S(2)}, u32[]{:S(2)}) %collective-permute-start.8) | collective-permute-done | bytes 65568 | tf_op jit(solution)/shard_map/ppermute | solution.py:289
  90.2 0.4 collective-permute-start.12
  90.5 1.8 %collective-permute-start.11 = (bf16[4,256,128]{2,1,0:T(8,128)(2,1)S(1)}, bf16[4,256,128]{2,1,0:T(8,128)(2,1)S(1)}, u32[]{:S(2)}, u32[]{:S(2)}) collective-permute-start(bf16[4,256,128]{2,1,0:T(8,128)(2,1)S(1)} %get-tuple-element.39.mine), channel_id=1, source_target_pairs={{0,8},{8,16},{16,24},{24,32},{32,40},{40,48},{48,56},{56,0},{1,9},... | collective-permute-start | bytes 786440 | tf_op jit(solution)/shard_map/ppermute | solution.py:215
  92.3 4.1 %shard_map.212 = (f32[8,27,8,128]{3,2,1,0:T(8,128)S(1)}, f32[8,27,8,128]{3,2,1,0:T(8,128)}) custom-call(s32[5]{0:T(128)S(1)} %stack.88.ids, bf16[4,256,128]{2,1,0:T(8,128)(2,1)S(1)} %get-tuple-element.39.mine, bf16[8,9,96,128]{3,2,1,0:T(8,128)(2,1)} %get-tuple-element.18.q_in), custom_call_target="tpu_custom_call" | custom-call | tf_op jit(solution)/shard_map/pallas_call | solution.py:192
  96.3 0.7 collective-permute-done.12.after
  97.0 1.5 collective-permute-done.11.before
  98.5 0.1 pad_maximum_fusion.1
  98.6 0.1 collective-permute-start.13
  98.7 0.3 collective-permute-done.14
  99.0 1.0 add.55
  100.0 0.6 collective-permute-done.13.other
  100.6 0.8 copy-done.5
  101.4 7.7 %shard_map.213 = (f32[8,27,8,128]{3,2,1,0:T(8,128)}, f32[8,27,8,128]{3,2,1,0:T(8,128)}, bf16[8,9,96,128]{3,2,1,0:T(8,128)(2,1)}) custom-call(s32[5]{0:T(128)S(1)} %stack.88.ids, bf16[4,256,128]{2,1,0:T(8,128)(2,1)S(1)} %get-tuple-element.39.mine, bf16[4,256,128]{2,1,0:T(8,128)(2,1)S(1)} %collective-permute-done.11.before, ...), custom_call_target="tpu_custom_call" | custom-call | tf_op jit(solution)/shard_map/pallas_call | solution.py:192
  109.1 0.1 collective-permute-start.15
  109.2 0.0 reduce-scatter.4.cloned.1.call-update
  109.3 2.5 %collective-permute-done.15 = f32[8,27,8,128]{3,2,1,0:T(8,128)S(1)} collective-permute-done((f32[8,27,8,128]{3,2,1,0:T(8,128)}, f32[8,27,8,128]{3,2,1,0:T(8,128)S(1)}, u32[]{:S(2)}, u32[]{:S(2)}) %collective-permute-start.15) | collective-permute-done | bytes 884768 | tf_op jit(solution)/shard_map/ppermute | solution.py:296
  111.7 2.1 %fusion = bf16[8,216,128]{2,1,0:T(8,128)(2,1)} fusion(f32[8,27,8,128]{3,2,1,0:T(8,128)} %get-tuple-element.28, f32[8,27,8,128]{3,2,1,0:T(8,128)S(1)} %collective-permute-done.15), kind=kLoop, calls=%fused_computation.4 | loop fusion | flops 442368 | bytes 2211840 | tf_op jit(solution)/shard_map/reshape | solution.py:314
  113.8 3.5 %all-to-all-start.1 = ((bf16[8,216,128]{2,1,0:T(8,128)(2,1)}), bf16[8,216,128]{2,1,0:T(8,128)(2,1)S(1)}, u32[]{:S(2)}, u32[]{:S(2)}) async-start(bf16[8,216,128]{2,1,0:T(8,128)(2,1)} %fusion), calls=%async_computation.1 | async-start | bytes 884736 | tf_op jit(solution)/shard_map/all_to_all | solution.py:316
  117.3 8.3 %shard_map.214 = f32[4,256,128]{2,1,0:T(8,128)S(1)} custom-call(s32[5]{0:T(128)S(1)} %stack.88.ids, bf16[4,256,128]{2,1,0:T(8,128)(2,1)S(1)} %get-tuple-element.39.mine, bf16[4,256,128]{2,1,0:T(8,128)(2,1)S(1)} %collective-permute-done.11.before, bf16[4,256,128]{2,1,0:T(8,128)(2,1)S(1)} %collective-permute-done.12.after, bf16[2,4,256,128]{3,2,1,0:T(8,128)(2,1)} %copy-done.5, ...), custom_call_target="tpu_custom_call" | custom-call | tf_op jit(solution)/shard_map/pallas_call | solution.py:192
  125.7 3.3 %collective-permute-start.16 = (f32[256,128]{1,0:T(8,128)S(1)}, f32[256,128]{1,0:T(8,128)S(1)}, u32[]{:S(2)}, u32[]{:S(2)}) collective-permute-start(f32[256,128]{1,0:T(8,128)S(1)} %get-tuple-element.32), channel_id=1, source_target_pairs={{0,65},{1,64},{2,128},{3,192},{64,1},{65,130},{66,129},{67,193},{1... | collective-permute-start | bytes 393224 | tf_op jit(solution)/shard_map/ppermute | solution.py:208
  129.0 2.2 %collective-permute-start.19 = (f32[256,128]{1,0:T(8,128)S(1)}, f32[256,128]{1,0:T(8,128)S(1)}, u32[]{:S(2)}, u32[]{:S(2)}) collective-permute-start(f32[256,128]{1,0:T(8,128)S(1)} %get-tuple-element.33), channel_id=1, source_target_pairs={{0,192},{1,0},{2,64},{3,128},{64,193},{65,1},{66,65},{67,129},{128... | collective-permute-start | bytes 393224 | tf_op jit(solution)/shard_map/ppermute | solution.py:208
  131.3 2.2 %collective-permute-start.17 = (f32[256,128]{1,0:T(8,128)S(1)}, f32[256,128]{1,0:T(8,128)S(1)}, u32[]{:S(2)}, u32[]{:S(2)}) collective-permute-start(f32[256,128]{1,0:T(8,128)S(1)} %get-tuple-element.35), channel_id=1, source_target_pairs={{0,64},{1,128},{2,192},{3,0},{64,65},{65,129},{66,193},{67,1},{128... | collective-permute-start | bytes 393224 | tf_op jit(solution)/shard_map/ppermute | solution.py:208
  133.5 4.0 %collective-permute-done.16 = f32[256,128]{1,0:T(8,128)S(1)} collective-permute-done((f32[256,128]{1,0:T(8,128)S(1)}, f32[256,128]{1,0:T(8,128)S(1)}, u32[]{:S(2)}, u32[]{:S(2)}) %collective-permute-start.16) | collective-permute-done | bytes 131104 | tf_op jit(solution)/shard_map/ppermute | solution.py:208
  137.5 0.8 collective-permute-done.19
  138.3 2.4 %collective-permute-done.18 = f32[256,128]{1,0:T(8,128)S(1)} collective-permute-done((f32[256,128]{1,0:T(8,128)S(1)}, f32[256,128]{1,0:T(8,128)S(1)}, u32[]{:S(2)}, u32[]{:S(2)}) %collective-permute-start.18) | collective-permute-done | bytes 131104 | tf_op jit(solution)/shard_map/ppermute | solution.py:208
  140.7 1.8 %collective-permute-done.17 = f32[256,128]{1,0:T(8,128)S(1)} collective-permute-done((f32[256,128]{1,0:T(8,128)S(1)}, f32[256,128]{1,0:T(8,128)S(1)}, u32[]{:S(2)}, u32[]{:S(2)}) %collective-permute-start.17) | collective-permute-done | bytes 131104 | tf_op jit(solution)/shard_map/ppermute | solution.py:208
  142.6 0.1 convert_reduce_fusion
  142.6 1.8 %collective-permute-start.20 = (f32[27,8,128]{2,1,0:T(8,128)S(1)}, f32[27,8,128]{2,1,0:T(8,128)S(1)}, u32[]{:S(2)}, u32[]{:S(2)}) collective-permute-start(f32[27,8,128]{2,1,0:T(8,128)S(1)} %bitcast.54), channel_id=1, source_target_pairs={{0,65},{1,64},{2,128},{3,192},{64,1},{65,130},{66,129},{67,193},{1... | collective-permute-start | bytes 331784 | tf_op jit(solution)/shard_map/ppermute | solution.py:208
  144.4 0.7 fusion.1
  145.2 5.8 %collective-permute-done.20 = f32[27,8,128]{2,1,0:T(8,128)S(1)} collective-permute-done((f32[27,8,128]{2,1,0:T(8,128)S(1)}, f32[27,8,128]{2,1,0:T(8,128)S(1)}, u32[]{:S(2)}, u32[]{:S(2)}) %collective-permute-start.20) | collective-permute-done | bytes 110624 | tf_op jit(solution)/shard_map/ppermute | solution.py:208
  150.9 0.7 select_bitcast_fusion.2
  (32 shorter events, 0.3 us)
Async XLA Ops:
  7.2 56.6 %all-gather.2.cloned.1.call-start = ((), (), s32[]{:S(2)}) async-start(), calls=%async_computation.3 | async-start | bytes 1880064 | tf_op jit(solution)/shard_map/all_gather | solution.py:232
  7.2 8.4 %collective-permute-start.7 = (bf16[8,27,128]{2,0,1:T(8,128)(2,1)}, bf16[8,27,128]{2,0,1:T(8,128)(2,1)S(1)}, u32[]{:S(2)}, u32[]{:S(2)}) collective-permute-start(bf16[8,27,128]{2,0,1:T(8,128)(2,1)} %param.23), channel_id=1, source_target_pairs={{0,65},{1,64},{2,128},{3,192},{64,1},{65,130},{66,129},{67,193},{1... | collective-permute-start | bytes 165896 | tf_op jit(solution)/shard_map/ppermute | solution.py:208
  17.1 134.5 %reduce-scatter.4.cloned.1.call-start = ((), (), s32[]{:S(2)}) async-start(), calls=%async_computation.4 | async-start | bytes 995328
  19.4 36.1 %copy-start = (bf16[864,224]{1,0:T(8,128)(2,1)S(1)}, bf16[864,224]{1,0:T(8,128)(2,1)}, u32[]{:S(2)}) copy-start(bf16[864,224]{1,0:T(8,128)(2,1)} %constant.72.clone.spread) | copy-start | bytes 1161220
  19.4 36.1 %copy-start.1 = (f32[224,128]{1,0:T(8,128)S(1)}, f32[224,128]{1,0:T(8,128)}, u32[]{:S(2)}) copy-start(f32[224,128]{1,0:T(8,128)} %constant.71.clone.local) | copy-start | bytes 344068
  19.4 36.1 %copy-start.2 = (bf16[224,32]{1,0:T(8,128)(2,1)S(1)}, bf16[224,32]{1,0:T(8,128)(2,1)}, u32[]{:S(2)}) copy-start(bf16[224,32]{1,0:T(8,128)(2,1)} %constant.70.clone.pick_back) | copy-start | bytes 43012
  19.4 36.0 %copy-start.3 = (bf16[224,32]{1,0:T(8,128)(2,1)S(1)}, bf16[224,32]{1,0:T(8,128)(2,1)}, u32[]{:S(2)}) copy-start(bf16[224,32]{1,0:T(8,128)(2,1)} %constant.69.clone.pick) | copy-start | bytes 43012
  19.5 36.0 %copy-start.4 = (bf16[16,128]{1,0:T(8,128)(2,1)S(1)}, bf16[16,128]{1,0:T(8,128)(2,1)}, u32[]{:S(2)}) copy-start(bf16[16,128]{1,0:T(8,128)(2,1)} %constant.74.clone.sources) | copy-start | bytes 12292
  20.4 13.9 %collective-permute-start = (bf16[288,128]{1,0:T(8,128)(2,1)S(1)}, bf16[288,128]{1,0:T(8,128)(2,1)S(1)}, u32[]{:S(2)}, u32[]{:S(2)}) collective-permute-start(bf16[288,128]{1,0:T(8,128)(2,1)S(1)} %pad_maximum_fusion.5), channel_id=1, source_target_pairs={{0,65},{1,64},{2,128},{3,192},{64,1},{65,130},{66,129},{67,193},{1... | collective-permute-start | bytes 221192 | tf_op jit(solution)/shard_map/ppermute | solution.py:208
  23.5 10.9 %collective-permute-start.2 = (bf16[288,128]{1,0:T(8,128)(2,1)S(1)}, bf16[288,128]{1,0:T(8,128)(2,1)S(1)}, u32[]{:S(2)}, u32[]{:S(2)}) collective-permute-start(bf16[288,128]{1,0:T(8,128)(2,1)S(1)} %pad_maximum_fusion.5), channel_id=1, source_target_pairs={{0,2},{1,66},{2,130},{3,194},{64,3},{65,67},{66,131},{67,195},{128... | collective-permute-start | bytes 221192 | tf_op jit(solution)/shard_map/ppermute | solution.py:208
  23.5 10.9 %collective-permute-start.1 = (bf16[288,128]{1,0:T(8,128)(2,1)S(1)}, bf16[288,128]{1,0:T(8,128)(2,1)S(1)}, u32[]{:S(2)}, u32[]{:S(2)}) collective-permute-start(bf16[288,128]{1,0:T(8,128)(2,1)S(1)} %pad_maximum_fusion.5), channel_id=1, source_target_pairs={{0,3},{1,67},{2,131},{3,195},{64,0},{65,64},{66,128},{67,192},{128... | collective-permute-start | bytes 221192 | tf_op jit(solution)/shard_map/ppermute | solution.py:208
  26.5 8.3 %collective-permute-start.3 = (bf16[288,128]{1,0:T(8,128)(2,1)S(1)}, bf16[288,128]{1,0:T(8,128)(2,1)S(1)}, u32[]{:S(2)}, u32[]{:S(2)}) collective-permute-start(bf16[288,128]{1,0:T(8,128)(2,1)S(1)} %pad_maximum_fusion.5), channel_id=1, source_target_pairs={{0,1},{1,65},{2,129},{3,193},{64,2},{65,66},{66,130},{67,194},{128... | collective-permute-start | bytes 221192 | tf_op jit(solution)/shard_map/ppermute | solution.py:208
  34.9 13.5 %collective-permute-start.5 = (bf16[4,288,128]{2,1,0:T(8,128)(2,1)S(1)}, bf16[4,288,128]{2,1,0:T(8,128)(2,1)S(1)}, u32[]{:S(2)}, u32[]{:S(2)}) collective-permute-start(bf16[4,288,128]{2,1,0:T(8,128)(2,1)S(1)} %get-tuple-element.37.mine), channel_id=1, source_target_pairs={{0,56},{8,0},{16,8},{24,16},{32,24},{40,32},{48,40},{56,48},{1,57}... | collective-permute-start | bytes 884744 | tf_op jit(solution)/shard_map/ppermute | solution.py:216
  40.8 11.6 %collective-permute-start.4 = (bf16[4,288,128]{2,1,0:T(8,128)(2,1)S(1)}, bf16[4,288,128]{2,1,0:T(8,128)(2,1)S(1)}, u32[]{:S(2)}, u32[]{:S(2)}) collective-permute-start(bf16[4,288,128]{2,1,0:T(8,128)(2,1)S(1)} %get-tuple-element.37.mine), channel_id=1, source_target_pairs={{0,8},{8,16},{16,24},{24,32},{32,40},{40,48},{48,56},{56,0},{1,9},... | collective-permute-start | bytes 884744 | tf_op jit(solution)/shard_map/ppermute | solution.py:215
  52.6 2.1 %collective-permute-start.6 = (bf16[2,4,288,128]{3,2,1,0:T(8,128)(2,1)S(1)}, bf16[2,4,288,128]{3,2,1,0:T(8,128)(2,1)S(1)}, u32[]{:S(2)}, u32[]{:S(2)}) collective-permute-start(bf16[2,4,288,128]{3,2,1,0:T(8,128)(2,1)S(1)} %pad_maximum_fusion), channel_id=1, source_target_pairs={{0,4},{4,0},{1,5},{5,1},{2,6},{6,2},{3,7},{7,3},{8,12},{12,8},{9,1... | collective-permute-start | bytes 1769480 | tf_op jit(solution)/shard_map/ppermute | solution.py:218
  54.7 0.8 copy-start.6
  82.5 6.0 %collective-permute-start.9 = (bf16[256,128]{1,0:T(8,128)(2,1)S(1)}, bf16[256,128]{1,0:T(8,128)(2,1)S(1)}, u32[]{:S(2)}, u32[]{:S(2)}) collective-permute-start(bf16[256,128]{1,0:T(8,128)(2,1)S(1)} %get-tuple-element.45), channel_id=1, source_target_pairs={{0,128},{64,192},{128,0},{192,64},{1,129},{65,193},{129,1},{193,65... | collective-permute-start | bytes 196616 | tf_op jit(solution)/shard_map/ppermute | solution.py:289
  84.7 5.5 %collective-permute-start.8 = (bf16[256,128]{1,0:T(8,128)(2,1)S(1)}, bf16[256,128]{1,0:T(8,128)(2,1)S(1)}, u32[]{:S(2)}, u32[]{:S(2)}) collective-permute-start(bf16[256,128]{1,0:T(8,128)(2,1)S(1)} %get-tuple-element.45), channel_id=1, source_target_pairs={{0,192},{64,0},{128,64},{192,128},{1,193},{65,1},{129,65},{193,129... | collective-permute-start | bytes 196616 | tf_op jit(solution)/shard_map/ppermute | solution.py:289
  85.5 4.6 %collective-permute-start.10 = (bf16[256,128]{1,0:T(8,128)(2,1)S(1)}, bf16[256,128]{1,0:T(8,128)(2,1)S(1)}, u32[]{:S(2)}, u32[]{:S(2)}) collective-permute-start(bf16[256,128]{1,0:T(8,128)(2,1)S(1)} %get-tuple-element.45), channel_id=1, source_target_pairs={{0,64},{64,128},{128,192},{192,0},{1,65},{65,129},{129,193},{193,1... | collective-permute-start | bytes 196616 | tf_op jit(solution)/shard_map/ppermute | solution.py:289
  90.2 6.8 %collective-permute-start.12 = (bf16[4,256,128]{2,1,0:T(8,128)(2,1)S(1)}, bf16[4,256,128]{2,1,0:T(8,128)(2,1)S(1)}, u32[]{:S(2)}, u32[]{:S(2)}) collective-permute-start(bf16[4,256,128]{2,1,0:T(8,128)(2,1)S(1)} %get-tuple-element.39.mine), channel_id=1, source_target_pairs={{0,56},{8,0},{16,8},{24,16},{32,24},{40,32},{48,40},{56,48},{1,57}... | collective-permute-start | bytes 786440 | tf_op jit(solution)/shard_map/ppermute | solution.py:216
  90.5 8.0 %collective-permute-start.11 = (bf16[4,256,128]{2,1,0:T(8,128)(2,1)S(1)}, bf16[4,256,128]{2,1,0:T(8,128)(2,1)S(1)}, u32[]{:S(2)}, u32[]{:S(2)}) collective-permute-start(bf16[4,256,128]{2,1,0:T(8,128)(2,1)S(1)} %get-tuple-element.39.mine), channel_id=1, source_target_pairs={{0,8},{8,16},{16,24},{24,32},{32,40},{40,48},{48,56},{56,0},{1,9},... | collective-permute-start | bytes 786440 | tf_op jit(solution)/shard_map/ppermute | solution.py:215
  96.3 2.6 %collective-permute-start.14 = (f32[8,27,8,128]{3,2,1,0:T(8,128)}, f32[8,27,8,128]{3,2,1,0:T(8,128)S(1)}, u32[]{:S(2)}, u32[]{:S(2)}) collective-permute-start(f32[8,27,8,128]{3,2,1,0:T(8,128)} %get-tuple-element.21), channel_id=1, source_target_pairs={{0,4},{4,0},{1,5},{5,1},{2,6},{6,2},{3,7},{7,3},{8,12},{12,8},{9,1... | collective-permute-start | bytes 2654216 | tf_op jit(solution)/shard_map/ppermute | solution.py:296
  98.6 2.0 %collective-permute-start.13 = (bf16[2,4,256,128]{3,2,1,0:T(8,128)(2,1)S(1)}, bf16[2,4,256,128]{3,2,1,0:T(8,128)(2,1)S(1)}, u32[]{:S(2)}, u32[]{:S(2)}) collective-permute-start(bf16[2,4,256,128]{3,2,1,0:T(8,128)(2,1)S(1)} %pad_maximum_fusion.1), channel_id=1, source_target_pairs={{0,4},{4,0},{1,5},{5,1},{2,6},{6,2},{3,7},{7,3},{8,12},{12,8},{9,1... | collective-permute-start | bytes 1572872 | tf_op jit(solution)/shard_map/ppermute | solution.py:218
  100.6 0.8 copy-start.5
  109.1 2.6 %collective-permute-start.15 = (f32[8,27,8,128]{3,2,1,0:T(8,128)}, f32[8,27,8,128]{3,2,1,0:T(8,128)S(1)}, u32[]{:S(2)}, u32[]{:S(2)}) collective-permute-start(f32[8,27,8,128]{3,2,1,0:T(8,128)} %get-tuple-element.29), channel_id=1, source_target_pairs={{0,4},{4,0},{1,5},{5,1},{2,6},{6,2},{3,7},{7,3},{8,12},{12,8},{9,1... | collective-permute-start | bytes 2654216 | tf_op jit(solution)/shard_map/ppermute | solution.py:296
  113.8 28.8 %all-to-all-start.1 = ((bf16[8,216,128]{2,1,0:T(8,128)(2,1)}), bf16[8,216,128]{2,1,0:T(8,128)(2,1)S(1)}, u32[]{:S(2)}, u32[]{:S(2)}) async-start(bf16[8,216,128]{2,1,0:T(8,128)(2,1)} %fusion), calls=%async_computation.1 | async-start | bytes 884736 | tf_op jit(solution)/shard_map/all_to_all | solution.py:316
  125.7 11.8 %collective-permute-start.16 = (f32[256,128]{1,0:T(8,128)S(1)}, f32[256,128]{1,0:T(8,128)S(1)}, u32[]{:S(2)}, u32[]{:S(2)}) collective-permute-start(f32[256,128]{1,0:T(8,128)S(1)} %get-tuple-element.32), channel_id=1, source_target_pairs={{0,65},{1,64},{2,128},{3,192},{64,1},{65,130},{66,129},{67,193},{1... | collective-permute-start | bytes 393224 | tf_op jit(solution)/shard_map/ppermute | solution.py:208
  129.0 9.3 %collective-permute-start.19 = (f32[256,128]{1,0:T(8,128)S(1)}, f32[256,128]{1,0:T(8,128)S(1)}, u32[]{:S(2)}, u32[]{:S(2)}) collective-permute-start(f32[256,128]{1,0:T(8,128)S(1)} %get-tuple-element.33), channel_id=1, source_target_pairs={{0,192},{1,0},{2,64},{3,128},{64,193},{65,1},{66,65},{67,129},{128... | collective-permute-start | bytes 393224 | tf_op jit(solution)/shard_map/ppermute | solution.py:208
  131.3 9.4 %collective-permute-start.18 = (f32[256,128]{1,0:T(8,128)S(1)}, f32[256,128]{1,0:T(8,128)S(1)}, u32[]{:S(2)}, u32[]{:S(2)}) collective-permute-start(f32[256,128]{1,0:T(8,128)S(1)} %get-tuple-element.34), channel_id=1, source_target_pairs={{0,128},{1,192},{2,0},{3,64},{64,129},{65,193},{66,1},{67,65},{128... | collective-permute-start | bytes 393224 | tf_op jit(solution)/shard_map/ppermute | solution.py:208
  131.3 11.2 %collective-permute-start.17 = (f32[256,128]{1,0:T(8,128)S(1)}, f32[256,128]{1,0:T(8,128)S(1)}, u32[]{:S(2)}, u32[]{:S(2)}) collective-permute-start(f32[256,128]{1,0:T(8,128)S(1)} %get-tuple-element.35), channel_id=1, source_target_pairs={{0,64},{1,128},{2,192},{3,0},{64,65},{65,129},{66,193},{67,1},{128... | collective-permute-start | bytes 393224 | tf_op jit(solution)/shard_map/ppermute | solution.py:208
  142.6 8.3 %collective-permute-start.20 = (f32[27,8,128]{2,1,0:T(8,128)S(1)}, f32[27,8,128]{2,1,0:T(8,128)S(1)}, u32[]{:S(2)}, u32[]{:S(2)}) collective-permute-start(f32[27,8,128]{2,1,0:T(8,128)S(1)} %bitcast.54), channel_id=1, source_target_pairs={{0,65},{1,64},{2,128},{3,192},{64,1},{65,130},{66,129},{67,193},{1... | collective-permute-start | bytes 331784 | tf_op jit(solution)/shard_map/ppermute | solution.py:208
Sparse Core Ops, SparseCore 0:
  17.2 43.0 all-gather.1
  109.4 36.4 reduce-scatter.3

commit v3 on v2

--- a/solution.py
+++ b/solution.py
@@ -104,7 +104,7 @@
 def gather_first(
     ids, mine, before, after, other, pick, pick_back, local, spread, lanes, sources, q_in, q_back, own, matched
 ):
-    @pl.loop(0, 4)
+    @pl.loop(0, 4, unroll=2)
     def _(turn):
         at = (ids[1] + turn) & 3
         views = around(ids, mine, before, after, other, turn)
@@ -122,26 +122,30 @@
         fill(q_back, at * 2, found[:, 768:], rows, pick_back[...], local[...], spread[...])
 
 
-def apply_first(q_in, q_back, weights, out):
+def apply_first(ids, q_in, q_back, weights, out):
     forward = convolve(q_in, weights.at[0])
     backward = convolve_back(q_back, weights.at[1])
     for at in range(4):
-        out[at, 0:128, :] = forward[at * 128 : (at + 1) * 128]
-        out[at, 128:256, :] = backward[at * 128 : (at + 1) * 128]
+        turn = (at - ids[0]) & 3
+        out[turn, 0:128, :] = forward[at * 128 : (at + 1) * 128]
+        out[turn, 128:256, :] = backward[at * 128 : (at + 1) * 128]
 
 
 def weight_blocks(ref, gradient, keep, send, scratch, core):
+    turned = gradient.T
+
     @pl.loop(0, 3)
-    def _(move):
-        start = pl.multiple_of(move * 16, 16)
-        for rest in range(9):
-            columns = ref[:, rest, pl.ds(start, 64), :].reshape(512, 128)
-            scratch[rest % 2] = lax.dot_general(
-                columns, gradient, (((0,), (0,)), ((), ())), preferred_element_type=F32
-            )
-            for z in range(8):
-                keep[z, move * 9 + rest] = scratch[rest % 2, pl.ds(z * 16 + core * 8, 8), :]
-                send[z, move * 9 + rest] = scratch[rest % 2, pl.ds(z * 16 + 8 - core * 8, 8), :]
+    def _(side):
+        for step in range(3):
+            rest = side * 3 + step
+            columns = [ref[:, rest, move * 16 : move * 16 + 64, :].reshape(512, 128) for move in range(3)]
+            found = dot(turned, jnp.concatenate(columns, 1))
+            for move in range(3):
+                scratch[step % 2, move * 128 : (move + 1) * 128] = found[:, move * 128 : (move + 1) * 128].T
+                for z in range(8):
+                    start = move * 128 + z * 16
+                    keep[z, move * 9 + rest] = scratch[step % 2, pl.ds(start + core * 8, 8), :]
+                    send[z, move * 9 + rest] = scratch[step % 2, pl.ds(start + 8 - core * 8, 8), :]
 
 
 def weigh_first(ids, mine, q_in, keep, send, own, scratch):
@@ -154,7 +158,7 @@
     ids, mine, before, after, other, matched, own, pick, pick_back, local, spread, lanes, sources,
     keep, send, q_hidden, scratch,
 ):
-    @pl.loop(0, 4)
+    @pl.loop(0, 4, unroll=2)
     def _(turn):
         at = (ids[0] + turn) & 3
         views = around(ids, mine, before, after, other, turn)
@@ -170,7 +174,7 @@
     ids, mine, before, after, other, matched, q_hidden, weights, pick, pick_back, local, spread, lanes, sources,
     reduced, q_back,
 ):
-    @pl.loop(0, 4)
+    @pl.loop(0, 4, unroll=2)
     def _(turn):
         at = (ids[0] + turn) & 3
         views = around(ids, mine, before, after, other, turn)
@@ -274,8 +278,10 @@
         *spread_out(turned),
         *consts,
     )
-    (partial,) = call(apply_first, [shape((4, 256, 128), F32)], [], q_in, q_back, blocks)
-    summed = jnp.sum(lax.all_to_all(partial, "x", 0, 0, tiled=True), axis=0)
+    (partial,) = call(apply_first, [shape((4, 256, 128), F32)], [], ids, q_in, q_back, blocks)
+    summed = partial[0]
+    for r in range(1, 4):
+        summed = summed + lax.ppermute(partial[r], "x", [(a, (a + r) % 4) for a in range(4)])
     first_act = active * summed[0:128]
     hidden_grad = summed[128:256]
     sigmoid_first = jax.nn.sigmoid(first_act)
@@ -289,7 +295,7 @@
         [packed] + [lax.ppermute(packed, "x", [(a, (a - r) % 4) for a in range(4)]) for r in range(1, 4)]
     )
     pieces = shape((8, 27, 8, 128), F32)
-    pair = pltpu.VMEM((2, 128, 128), F32)
+    pair = pltpu.VMEM((2, 384, 128), F32)
     keep1, send1 = call(weigh_first, [pieces, pieces], [pltpu.VMEM((4, 128, 128), BF), pair], ids, along, q_in)
 
     def both_cores(keep, send):
@@ -328,14 +334,14 @@
         blocks,
         *consts,
     )
-    total = None
-    for r in range(4):
-        part = turn_over(reduced[r], lambda a, b: (b + r, a))
-        total = part if total is None else total + part
+    parts = [turn_over(reduced[r], lambda a, b: (b + r, a)) for r in range(4)]
+    second_sum = jnp.sum(moved.astype(F32), axis=0).reshape(27, 8, 128)
+    *parts, _ = lax.optimization_barrier((*parts, second_sum))
+    second_sum = turn_over(second_sum, lambda a, b: (b, a))
+    total = parts[0] + parts[1] + parts[2] + parts[3]
     output = (active * total[0:128]).astype(BF)
     features_grad = (active * total[128:256]).astype(BF)
 
-    second_sum = turn_over(jnp.sum(moved.astype(F32), axis=0).reshape(27, 8, 128), lambda a, b: (b, a))
     return (
         output,
         features_grad,

time: 159 us -> 153 us (0.962)
  blocking collectives: 14 us -> 0 us
  starting transfers between devices: 36.6 us -> 42.1 us
  waiting for transfers between devices: 49.2 us -> 52.1 us
  Pallas kernels: 32.9 us -> 31.1 us
    all_to_all x1 -> x0, blocking collectives: 14 us -> none  [on_device(): summed = jnp.sum(lax.all_to_all(partial, 'x', 0, 0, tiled=True), axis=0)]
    ppermute x0 -> x3, waiting for transfers between devices: none -> 7.71 us  [on_device(): lax.ppermute(partial[r], 'x', [(a, (a + r) % 4) for a in range(4)])]
    ppermute x0 -> x3, starting transfers between devices: none -> 5.27 us  [on_device(): lax.ppermute(partial[r], 'x', [(a, (a + r) % 4) for a in range(4)])]
    ppermute x10, waiting for transfers between devices: 27.9 us -> 22.9 us  [turn_over(): lax.ppermute(value, ('x', 'chan'), [(p[0] * 4 + p[1], q[0] * 4 + q[1]) fo...]
    pallas_call x5, Pallas kernels: 32.9 us -> 31.1 us  [call(): pl.pallas_call(kernel, out_shape=outs, in_specs=[smem if value.dtype == j...]
  transfers between devices with their start and end apart: 24 -> 27, of which waited for: 18 -> 18; matrix products, arithmetic and copies ran while one was open for 5% -> 5% of each run, Pallas kernels for 13% -> 13%
where the time goes in v3:
time: 153 us; the launch traced here: 151 us
  waiting for transfers between devices  52.1 us (34%)
  starting transfers between devices  42.1 us (28%)
  Pallas kernels  31.1 us (20%)
  between operations  14.3 us (9%)
  other arithmetic  8.9 us (6%)
  local copies, waits for them, and re-layouts  2.58 us (2%)
    pallas_call x5, Pallas kernels, call(): pl.pallas_call(kernel, out_shape=outs, in_specs=[smem if value.dtype == j...  31.1 us
    ppermute x10, waiting for transfers between devices, turn_over(): lax.ppermute(value, ('x', 'chan'), [(p[0] * 4 + p[1], q[0] * 4 + q[1]) fo...  22.9 us
    ppermute x10, starting transfers between devices, turn_over(): lax.ppermute(value, ('x', 'chan'), [(p[0] * 4 + p[1], q[0] * 4 + q[1]) fo...  20.8 us
    ppermute x2, waiting for transfers between devices, spread_out(): after = lax.ppermute(mine, 'z', [(i, (i - 1) % 8) for i in range(8)])  7.94 us
    ppermute x3, waiting for transfers between devices, on_device(): lax.ppermute(partial[r], 'x', [(a, (a + r) % 4) for a in range(4)])  7.71 us
    ppermute x2, starting transfers between devices, spread_out(): after = lax.ppermute(mine, 'z', [(i, (i - 1) % 8) for i in range(8)])  6.29 us
    ppermute x2, waiting for transfers between devices, spread_out(): before = lax.ppermute(mine, 'z', [(i, (i + 1) % 8) for i in range(8)])  5.57 us
    ppermute x3, starting transfers between devices, on_device(): lax.ppermute(partial[r], 'x', [(a, (a + r) % 4) for a in range(4)])  5.27 us
  transfers between devices with their start and end apart: 27, of which 18 were waited for; matrix products, arithmetic and copies ran while one was open for 5% of the time, Pallas kernels for 13%

profile of v3, /device:TPU:6, one launch (start us, length us, event | category | flops | bytes accessed | tf_op | source)
XLA Modules:
  0.0 151.0 jit_solution(17681513648011022659)
XLA Ops:
  7.2 0.0 all-gather.2.cloned.1.call-start
  7.2 3.0 %collective-permute-start.7 = (bf16[8,27,128]{2,0,1:T(8,128)(2,1)}, bf16[8,27,128]{2,0,1:T(8,128)(2,1)S(1)}, u32[]{:S(2)}, u32[]{:S(2)}) collective-permute-start(bf16[8,27,128]{2,0,1:T(8,128)(2,1)} %param.23), channel_id=1, source_target_pairs={{0,65},{1,64},{2,128},{3,192},{64,1},{65,130},{66,129},{67,193},{1... | collective-permute-start | bytes 165896 | tf_op jit(solution)/shard_map/ppermute | solution.py:212
  10.2 5.4 %collective-permute-done.7 = bf16[8,27,128]{2,0,1:T(8,128)(2,1)S(1)} collective-permute-done((bf16[8,27,128]{2,0,1:T(8,128)(2,1)}, bf16[8,27,128]{2,0,1:T(8,128)(2,1)S(1)}, u32[]{:S(2)}, u32[]{:S(2)}) %collective-permute-start.7) | collective-permute-done | bytes 55328 | tf_op jit(solution)/shard_map/ppermute | solution.py:212
  15.6 1.5 pad_maximum_fusion.4
  17.1 0.0 all-gather.2.cloned.1.call-update
  17.1 0.0 reduce-scatter.4.cloned.1.call-start
  17.1 0.7 convert_element_type.53
  17.8 0.8 fusion.27
  18.6 0.8 fusion.22
  19.5 0.9 multiply_convert_fusion.1
  20.4 3.0 %collective-permute-start = (bf16[288,128]{1,0:T(8,128)(2,1)S(1)}, bf16[288,128]{1,0:T(8,128)(2,1)S(1)}, u32[]{:S(2)}, u32[]{:S(2)}) collective-permute-start(bf16[288,128]{1,0:T(8,128)(2,1)S(1)} %pad_maximum_fusion.5), channel_id=1, source_target_pairs={{0,65},{1,64},{2,128},{3,192},{64,1},{65,130},{66,129},{67,193},{1... | collective-permute-start | bytes 221192 | tf_op jit(solution)/shard_map/ppermute | solution.py:212
  23.5 3.1 %collective-permute-start.1 = (bf16[288,128]{1,0:T(8,128)(2,1)S(1)}, bf16[288,128]{1,0:T(8,128)(2,1)S(1)}, u32[]{:S(2)}, u32[]{:S(2)}) collective-permute-start(bf16[288,128]{1,0:T(8,128)(2,1)S(1)} %pad_maximum_fusion.5), channel_id=1, source_target_pairs={{0,3},{1,67},{2,131},{3,195},{64,0},{65,64},{66,128},{67,192},{128... | collective-permute-start | bytes 221192 | tf_op jit(solution)/shard_map/ppermute | solution.py:212
  26.5 0.6 collective-permute-start.3
  27.1 7.2 %collective-permute-done = bf16[288,128]{1,0:T(8,128)(2,1)S(1)} collective-permute-done((bf16[288,128]{1,0:T(8,128)(2,1)S(1)}, bf16[288,128]{1,0:T(8,128)(2,1)S(1)}, u32[]{:S(2)}, u32[]{:S(2)}) %collective-permute-start) | collective-permute-done | bytes 73760 | tf_op jit(solution)/shard_map/ppermute | solution.py:212
  34.3 0.5 collective-permute-done.3
  34.9 0.1 fusion.31
  34.9 5.9 %collective-permute-start.5 = (bf16[4,288,128]{2,1,0:T(8,128)(2,1)S(1)}, bf16[4,288,128]{2,1,0:T(8,128)(2,1)S(1)}, u32[]{:S(2)}, u32[]{:S(2)}) collective-permute-start(bf16[4,288,128]{2,1,0:T(8,128)(2,1)S(1)} %get-tuple-element.48.mine), channel_id=1, source_target_pairs={{0,56},{8,0},{16,8},{24,16},{32,24},{40,32},{48,40},{56,48},{1,57}... | collective-permute-start | bytes 884744 | tf_op jit(solution)/shard_map/ppermute | solution.py:220
  40.8 7.6 %collective-permute-done.5.after = bf16[4,288,128]{2,1,0:T(8,128)(2,1)S(1)} collective-permute-done((bf16[4,288,128]{2,1,0:T(8,128)(2,1)S(1)}, bf16[4,288,128]{2,1,0:T(8,128)(2,1)S(1)}, u32[]{:S(2)}, u32[]{:S(2)}) %collective-permute-start.5) | collective-permute-done | bytes 294944 | tf_op jit(solution)/shard_map/ppermute | solution.py:220
  48.4 4.1 %collective-permute-done.4.before = bf16[4,288,128]{2,1,0:T(8,128)(2,1)S(1)} collective-permute-done((bf16[4,288,128]{2,1,0:T(8,128)(2,1)S(1)}, bf16[4,288,128]{2,1,0:T(8,128)(2,1)S(1)}, u32[]{:S(2)}, u32[]{:S(2)}) %collective-permute-start.4) | collective-permute-done | bytes 294944 | tf_op jit(solution)/shard_map/ppermute | solution.py:219
  52.5 0.1 pad_maximum_fusion
  52.6 0.1 collective-permute-start.6
  52.7 0.1 stack.88.ids
  52.8 1.9 %collective-permute-done.6.other = bf16[2,4,288,128]{3,2,1,0:T(8,128)(2,1)S(1)} collective-permute-done((bf16[2,4,288,128]{3,2,1,0:T(8,128)(2,1)S(1)}, bf16[2,4,288,128]{3,2,1,0:T(8,128)(2,1)S(1)}, u32[]{:S(2)}, u32[]{:S(2)}) %collective-permute-start.6) | collective-permute-done | bytes 589856 | tf_op jit(solution)/shard_map/ppermute | solution.py:222
  54.7 0.8 copy-done.6
  55.5 7.7 %shard_map.210 = (bf16[8,9,96,128]{3,2,1,0:T(8,128)(2,1)}, bf16[8,9,96,128]{3,2,1,0:T(8,128)(2,1)}, bf16[4,128,128]{2,1,0:T(8,128)(2,1)S(1)}, bf16[4,32,128]{2,1,0:T(8,128)(2,1)S(1)}) custom-call(s32[5]{0:T(128)S(1)} %stack.88.ids, bf16[4,288,128]{2,1,0:T(8,128)(2,1)S(1)} %get-tuple-element.48.mine, bf16[4,288,128]{2,1,0:T(8,128)(2,1)S(1)} %collective-permute-done.4.before, ...), custom_call_target="tpu_custom_call" | custom-call | tf_op jit(solution)/shard_map/pallas_call | solution.py:196
  63.2 4.5 %shard_map.211 = f32[4,256,128]{2,1,0:T(8,128)S(1)} custom-call(s32[5]{0:T(128)S(1)} %stack.88.ids, bf16[8,9,96,128]{3,2,1,0:T(8,128)(2,1)} %get-tuple-element.22.q_in, bf16[8,9,96,128]{3,2,1,0:T(8,128)(2,1)} %get-tuple-element.23.q_back, bf16[2,27,128,128]{3,2,1,0:T(8,128)(2,1)} %bitcast.66), custom_call_target="tpu_custom_call" | custom-call | tf_op jit(solution)/shard_map/pallas_call | solution.py:196
  67.8 3.7 %collective-permute-start.8 = (f32[256,128]{1,0:T(8,128)S(1)}, f32[256,128]{1,0:T(8,128)S(1)}, u32[]{:S(2)}, u32[]{:S(2)}) collective-permute-start(f32[256,128]{1,0:T(8,128)S(1)} %get-tuple-element.44), channel_id=1, source_target_pairs={{0,64},{64,128},{128,192},{192,0},{1,65},{65,129},{129,193},{193,1... | collective-permute-start | bytes 393224 | tf_op jit(solution)/shard_map/ppermute | solution.py:284
  71.5 1.6 %collective-permute-start.9 = (f32[256,128]{1,0:T(8,128)S(1)}, f32[256,128]{1,0:T(8,128)S(1)}, u32[]{:S(2)}, u32[]{:S(2)}) collective-permute-start(f32[256,128]{1,0:T(8,128)S(1)} %get-tuple-element.46), channel_id=1, source_target_pairs={{0,128},{64,192},{128,0},{192,64},{1,129},{65,193},{129,1},{193,65... | collective-permute-start | bytes 393224 | tf_op jit(solution)/shard_map/ppermute | solution.py:284
  73.1 1.5 collective-permute-done.8
  74.5 6.2 %collective-permute-done.10 = f32[256,128]{1,0:T(8,128)S(1)} collective-permute-done((f32[256,128]{1,0:T(8,128)S(1)}, f32[256,128]{1,0:T(8,128)S(1)}, u32[]{:S(2)}, u32[]{:S(2)}) %collective-permute-start.10) | collective-permute-done | bytes 131104 | tf_op jit(solution)/shard_map/ppermute | solution.py:284
  80.8 0.1 multiply_convert_fusion
  80.9 0.8 collective-permute-start.12
  81.8 0.7 collective-permute-start.11
  82.5 2.5 %collective-permute-start.13 = (bf16[256,128]{1,0:T(8,128)(2,1)S(1)}, bf16[256,128]{1,0:T(8,128)(2,1)S(1)}, u32[]{:S(2)}, u32[]{:S(2)}) collective-permute-start(bf16[256,128]{1,0:T(8,128)(2,1)S(1)} %get-tuple-element.56), channel_id=1, source_target_pairs={{0,64},{64,128},{128,192},{192,0},{1,65},{65,129},{129,193},{193,1... | collective-permute-start | bytes 196616 | tf_op jit(solution)/shard_map/ppermute | solution.py:295
  85.0 2.0 %collective-permute-done.12 = bf16[256,128]{1,0:T(8,128)(2,1)S(1)} collective-permute-done((bf16[256,128]{1,0:T(8,128)(2,1)S(1)}, bf16[256,128]{1,0:T(8,128)(2,1)S(1)}, u32[]{:S(2)}, u32[]{:S(2)}) %collective-permute-start.12) | collective-permute-done | bytes 65568 | tf_op jit(solution)/shard_map/ppermute | solution.py:295
  87.0 0.7 collective-permute-done.11
  87.7 0.4 collective-permute-start.15
  88.1 1.7 %collective-permute-start.14 = (bf16[4,256,128]{2,1,0:T(8,128)(2,1)S(1)}, bf16[4,256,128]{2,1,0:T(8,128)(2,1)S(1)}, u32[]{:S(2)}, u32[]{:S(2)}) collective-permute-start(bf16[4,256,128]{2,1,0:T(8,128)(2,1)S(1)} %get-tuple-element.50.mine), channel_id=1, source_target_pairs={{0,8},{8,16},{16,24},{24,32},{32,40},{40,48},{48,56},{56,0},{1,9},... | collective-permute-start | bytes 786440 | tf_op jit(solution)/shard_map/ppermute | solution.py:219
  89.8 4.0 %shard_map.212 = (f32[8,27,8,128]{3,2,1,0:T(8,128)S(1)}, f32[8,27,8,128]{3,2,1,0:T(8,128)}) custom-call(s32[5]{0:T(128)S(1)} %stack.88.ids, bf16[4,256,128]{2,1,0:T(8,128)(2,1)S(1)} %get-tuple-element.50.mine, bf16[8,9,96,128]{3,2,1,0:T(8,128)(2,1)} %get-tuple-element.22.q_in), custom_call_target="tpu_custom_call" | custom-call | tf_op jit(solution)/shard_map/pallas_call | solution.py:196
  93.8 0.4 collective-permute-done.15.after
  94.2 1.5 collective-permute-done.14.before
  95.7 0.1 pad_maximum_fusion.1
  95.8 0.1 collective-permute-start.16
  95.9 0.6 collective-permute-done.17
  96.4 1.0 add.67
  97.4 0.3 collective-permute-done.16.other
  97.8 0.8 copy-done.5
  98.6 7.3 %shard_map.213 = (f32[8,27,8,128]{3,2,1,0:T(8,128)}, f32[8,27,8,128]{3,2,1,0:T(8,128)}, bf16[8,9,96,128]{3,2,1,0:T(8,128)(2,1)}) custom-call(s32[5]{0:T(128)S(1)} %stack.88.ids, bf16[4,256,128]{2,1,0:T(8,128)(2,1)S(1)} %get-tuple-element.50.mine, bf16[4,256,128]{2,1,0:T(8,128)(2,1)S(1)} %collective-permute-done.14.before, ...), custom_call_target="tpu_custom_call" | custom-call | tf_op jit(solution)/shard_map/pallas_call | solution.py:196
  105.8 0.1 collective-permute-start.18
  106.0 0.0 reduce-scatter.4.cloned.1.call-update
  106.0 2.5 %collective-permute-done.18 = f32[8,27,8,128]{3,2,1,0:T(8,128)S(1)} collective-permute-done((f32[8,27,8,128]{3,2,1,0:T(8,128)}, f32[8,27,8,128]{3,2,1,0:T(8,128)S(1)}, u32[]{:S(2)}, u32[]{:S(2)}) %collective-permute-start.18) | collective-permute-done | bytes 884768 | tf_op jit(solution)/shard_map/ppermute | solution.py:302
  108.5 2.1 %fusion = bf16[8,216,128]{2,1,0:T(8,128)(2,1)} fusion(f32[8,27,8,128]{3,2,1,0:T(8,128)} %get-tuple-element.32, f32[8,27,8,128]{3,2,1,0:T(8,128)S(1)} %collective-permute-done.18), kind=kLoop, calls=%fused_computation.4 | loop fusion | flops 442368 | bytes 2211840 | tf_op jit(solution)/shard_map/reshape | solution.py:320
  110.5 3.5 %all-to-all-start = ((bf16[8,216,128]{2,1,0:T(8,128)(2,1)}), bf16[8,216,128]{2,1,0:T(8,128)(2,1)S(1)}, u32[]{:S(2)}, u32[]{:S(2)}) async-start(bf16[8,216,128]{2,1,0:T(8,128)(2,1)} %fusion), calls=%async_computation | async-start | bytes 884736 | tf_op jit(solution)/shard_map/all_to_all | solution.py:322
  114.0 7.7 %shard_map.214 = f32[4,256,128]{2,1,0:T(8,128)S(1)} custom-call(s32[5]{0:T(128)S(1)} %stack.88.ids, bf16[4,256,128]{2,1,0:T(8,128)(2,1)S(1)} %get-tuple-element.50.mine, bf16[4,256,128]{2,1,0:T(8,128)(2,1)S(1)} %collective-permute-done.14.before, bf16[4,256,128]{2,1,0:T(8,128)(2,1)S(1)} %collective-permute-done.15.after, bf16[2,4,256,128]{3,2,1,0:T(8,128)(2,1)} %copy-done.5, ...), custom_call_target="tpu_custom_call" | custom-call | tf_op jit(solution)/shard_map/pallas_call | solution.py:196
  121.8 3.0 %collective-permute-start.19 = (f32[256,128]{1,0:T(8,128)S(1)}, f32[256,128]{1,0:T(8,128)S(1)}, u32[]{:S(2)}, u32[]{:S(2)}) collective-permute-start(f32[256,128]{1,0:T(8,128)S(1)} %get-tuple-element.43), channel_id=1, source_target_pairs={{0,65},{1,64},{2,128},{3,192},{64,1},{65,130},{66,129},{67,193},{1... | collective-permute-start | bytes 393224 | tf_op jit(solution)/shard_map/ppermute | solution.py:212
  124.8 2.5 %collective-permute-start.22 = (f32[256,128]{1,0:T(8,128)S(1)}, f32[256,128]{1,0:T(8,128)S(1)}, u32[]{:S(2)}, u32[]{:S(2)}) collective-permute-start(f32[256,128]{1,0:T(8,128)S(1)} %get-tuple-element.40), channel_id=1, source_target_pairs={{0,192},{1,0},{2,64},{3,128},{64,193},{65,1},{66,65},{67,129},{128... | collective-permute-start | bytes 393224 | tf_op jit(solution)/shard_map/ppermute | solution.py:212
  127.3 2.2 %collective-permute-start.20 = (f32[256,128]{1,0:T(8,128)S(1)}, f32[256,128]{1,0:T(8,128)S(1)}, u32[]{:S(2)}, u32[]{:S(2)}) collective-permute-start(f32[256,128]{1,0:T(8,128)S(1)} %get-tuple-element.42), channel_id=1, source_target_pairs={{0,64},{1,128},{2,192},{3,0},{64,65},{65,129},{66,193},{67,1},{128... | collective-permute-start | bytes 393224 | tf_op jit(solution)/shard_map/ppermute | solution.py:212
  129.6 4.0 %collective-permute-done.19 = f32[256,128]{1,0:T(8,128)S(1)} collective-permute-done((f32[256,128]{1,0:T(8,128)S(1)}, f32[256,128]{1,0:T(8,128)S(1)}, u32[]{:S(2)}, u32[]{:S(2)}) %collective-permute-start.19) | collective-permute-done | bytes 131104 | tf_op jit(solution)/shard_map/ppermute | solution.py:212
  133.6 0.1 convert_reduce_fusion
  133.6 3.3 %collective-permute-start.23 = (f32[27,8,128]{2,1,0:T(8,128)S(1)}, f32[27,8,128]{2,1,0:T(8,128)S(1)}, u32[]{:S(2)}, u32[]{:S(2)}) collective-permute-start(f32[27,8,128]{2,1,0:T(8,128)S(1)} %bitcast.68), channel_id=1, source_target_pairs={{0,65},{1,64},{2,128},{3,192},{64,1},{65,130},{66,129},{67,193},{1... | collective-permute-start | bytes 331784 | tf_op jit(solution)/shard_map/ppermute | solution.py:212
  137.0 2.8 %collective-permute-done.20 = f32[256,128]{1,0:T(8,128)S(1)} collective-permute-done((f32[256,128]{1,0:T(8,128)S(1)}, f32[256,128]{1,0:T(8,128)S(1)}, u32[]{:S(2)}, u32[]{:S(2)}) %collective-permute-start.20) | collective-permute-done | bytes 131104 | tf_op jit(solution)/shard_map/ppermute | solution.py:212
  139.8 0.7 fusion.4
  140.5 3.1 %collective-permute-done.23 = f32[27,8,128]{2,1,0:T(8,128)S(1)} collective-permute-done((f32[27,8,128]{2,1,0:T(8,128)S(1)}, f32[27,8,128]{2,1,0:T(8,128)S(1)}, u32[]{:S(2)}, u32[]{:S(2)}) %collective-permute-start.23) | collective-permute-done | bytes 110624 | tf_op jit(solution)/shard_map/ppermute | solution.py:212
  143.5 0.7 select_bitcast_fusion.2
  (39 shorter events, 0.4 us)
Async XLA Ops:
  7.2 56.0 %all-gather.2.cloned.1.call-start = ((), (), s32[]{:S(2)}) async-start(), calls=%async_computation.2 | async-start | bytes 1880064 | tf_op jit(solution)/shard_map/all_gather | solution.py:236
  7.2 8.4 %collective-permute-start.7 = (bf16[8,27,128]{2,0,1:T(8,128)(2,1)}, bf16[8,27,128]{2,0,1:T(8,128)(2,1)S(1)}, u32[]{:S(2)}, u32[]{:S(2)}) collective-permute-start(bf16[8,27,128]{2,0,1:T(8,128)(2,1)} %param.23), channel_id=1, source_target_pairs={{0,65},{1,64},{2,128},{3,192},{64,1},{65,130},{66,129},{67,193},{1... | collective-permute-start | bytes 165896 | tf_op jit(solution)/shard_map/ppermute | solution.py:212
  17.1 127.1 %reduce-scatter.4.cloned.1.call-start = ((), (), s32[]{:S(2)}) async-start(), calls=%async_computation.3 | async-start | bytes 995328
  19.4 36.1 %copy-start = (bf16[864,224]{1,0:T(8,128)(2,1)S(1)}, bf16[864,224]{1,0:T(8,128)(2,1)}, u32[]{:S(2)}) copy-start(bf16[864,224]{1,0:T(8,128)(2,1)} %constant.72.clone.spread) | copy-start | bytes 1161220
  19.4 36.1 %copy-start.1 = (f32[224,128]{1,0:T(8,128)S(1)}, f32[224,128]{1,0:T(8,128)}, u32[]{:S(2)}) copy-start(f32[224,128]{1,0:T(8,128)} %constant.71.clone.local) | copy-start | bytes 344068
  19.4 36.1 %copy-start.2 = (bf16[224,32]{1,0:T(8,128)(2,1)S(1)}, bf16[224,32]{1,0:T(8,128)(2,1)}, u32[]{:S(2)}) copy-start(bf16[224,32]{1,0:T(8,128)(2,1)} %constant.70.clone.pick_back) | copy-start | bytes 43012
  19.4 36.0 %copy-start.3 = (bf16[224,32]{1,0:T(8,128)(2,1)S(1)}, bf16[224,32]{1,0:T(8,128)(2,1)}, u32[]{:S(2)}) copy-start(bf16[224,32]{1,0:T(8,128)(2,1)} %constant.69.clone.pick) | copy-start | bytes 43012
  19.5 36.0 %copy-start.4 = (bf16[16,128]{1,0:T(8,128)(2,1)S(1)}, bf16[16,128]{1,0:T(8,128)(2,1)}, u32[]{:S(2)}) copy-start(bf16[16,128]{1,0:T(8,128)(2,1)} %constant.74.clone.sources) | copy-start | bytes 12292
  20.4 13.9 %collective-permute-start = (bf16[288,128]{1,0:T(8,128)(2,1)S(1)}, bf16[288,128]{1,0:T(8,128)(2,1)S(1)}, u32[]{:S(2)}, u32[]{:S(2)}) collective-permute-start(bf16[288,128]{1,0:T(8,128)(2,1)S(1)} %pad_maximum_fusion.5), channel_id=1, source_target_pairs={{0,65},{1,64},{2,128},{3,192},{64,1},{65,130},{66,129},{67,193},{1... | collective-permute-start | bytes 221192 | tf_op jit(solution)/shard_map/ppermute | solution.py:212
  23.5 10.9 %collective-permute-start.2 = (bf16[288,128]{1,0:T(8,128)(2,1)S(1)}, bf16[288,128]{1,0:T(8,128)(2,1)S(1)}, u32[]{:S(2)}, u32[]{:S(2)}) collective-permute-start(bf16[288,128]{1,0:T(8,128)(2,1)S(1)} %pad_maximum_fusion.5), channel_id=1, source_target_pairs={{0,2},{1,66},{2,130},{3,194},{64,3},{65,67},{66,131},{67,195},{128... | collective-permute-start | bytes 221192 | tf_op jit(solution)/shard_map/ppermute | solution.py:212
  23.5 10.9 %collective-permute-start.1 = (bf16[288,128]{1,0:T(8,128)(2,1)S(1)}, bf16[288,128]{1,0:T(8,128)(2,1)S(1)}, u32[]{:S(2)}, u32[]{:S(2)}) collective-permute-start(bf16[288,128]{1,0:T(8,128)(2,1)S(1)} %pad_maximum_fusion.5), channel_id=1, source_target_pairs={{0,3},{1,67},{2,131},{3,195},{64,0},{65,64},{66,128},{67,192},{128... | collective-permute-start | bytes 221192 | tf_op jit(solution)/shard_map/ppermute | solution.py:212
  26.5 8.3 %collective-permute-start.3 = (bf16[288,128]{1,0:T(8,128)(2,1)S(1)}, bf16[288,128]{1,0:T(8,128)(2,1)S(1)}, u32[]{:S(2)}, u32[]{:S(2)}) collective-permute-start(bf16[288,128]{1,0:T(8,128)(2,1)S(1)} %pad_maximum_fusion.5), channel_id=1, source_target_pairs={{0,1},{1,65},{2,129},{3,193},{64,2},{65,66},{66,130},{67,194},{128... | collective-permute-start | bytes 221192 | tf_op jit(solution)/shard_map/ppermute | solution.py:212
  34.9 13.5 %collective-permute-start.5 = (bf16[4,288,128]{2,1,0:T(8,128)(2,1)S(1)}, bf16[4,288,128]{2,1,0:T(8,128)(2,1)S(1)}, u32[]{:S(2)}, u32[]{:S(2)}) collective-permute-start(bf16[4,288,128]{2,1,0:T(8,128)(2,1)S(1)} %get-tuple-element.48.mine), channel_id=1, source_target_pairs={{0,56},{8,0},{16,8},{24,16},{32,24},{40,32},{48,40},{56,48},{1,57}... | collective-permute-start | bytes 884744 | tf_op jit(solution)/shard_map/ppermute | solution.py:220
  40.8 11.6 %collective-permute-start.4 = (bf16[4,288,128]{2,1,0:T(8,128)(2,1)S(1)}, bf16[4,288,128]{2,1,0:T(8,128)(2,1)S(1)}, u32[]{:S(2)}, u32[]{:S(2)}) collective-permute-start(bf16[4,288,128]{2,1,0:T(8,128)(2,1)S(1)} %get-tuple-element.48.mine), channel_id=1, source_target_pairs={{0,8},{8,16},{16,24},{24,32},{32,40},{40,48},{48,56},{56,0},{1,9},... | collective-permute-start | bytes 884744 | tf_op jit(solution)/shard_map/ppermute | solution.py:219
  52.6 2.1 %collective-permute-start.6 = (bf16[2,4,288,128]{3,2,1,0:T(8,128)(2,1)S(1)}, bf16[2,4,288,128]{3,2,1,0:T(8,128)(2,1)S(1)}, u32[]{:S(2)}, u32[]{:S(2)}) collective-permute-start(bf16[2,4,288,128]{3,2,1,0:T(8,128)(2,1)S(1)} %pad_maximum_fusion), channel_id=1, source_target_pairs={{0,4},{4,0},{1,5},{5,1},{2,6},{6,2},{3,7},{7,3},{8,12},{12,8},{9,1... | collective-permute-start | bytes 1769480 | tf_op jit(solution)/shard_map/ppermute | solution.py:222
  54.7 0.8 copy-start.6
  67.8 6.8 %collective-permute-start.8 = (f32[256,128]{1,0:T(8,128)S(1)}, f32[256,128]{1,0:T(8,128)S(1)}, u32[]{:S(2)}, u32[]{:S(2)}) collective-permute-start(f32[256,128]{1,0:T(8,128)S(1)} %get-tuple-element.44), channel_id=1, source_target_pairs={{0,64},{64,128},{128,192},{192,0},{1,65},{65,129},{129,193},{193,1... | collective-permute-start | bytes 393224 | tf_op jit(solution)/shard_map/ppermute | solution.py:284
  71.5 9.3 %collective-permute-start.10 = (f32[256,128]{1,0:T(8,128)S(1)}, f32[256,128]{1,0:T(8,128)S(1)}, u32[]{:S(2)}, u32[]{:S(2)}) collective-permute-start(f32[256,128]{1,0:T(8,128)S(1)} %get-tuple-element.45), channel_id=1, source_target_pairs={{0,192},{64,0},{128,64},{192,128},{1,193},{65,1},{129,65},{193,129... | collective-permute-start | bytes 393224 | tf_op jit(solution)/shard_map/ppermute | solution.py:284
  71.5 9.3 %collective-permute-start.9 = (f32[256,128]{1,0:T(8,128)S(1)}, f32[256,128]{1,0:T(8,128)S(1)}, u32[]{:S(2)}, u32[]{:S(2)}) collective-permute-start(f32[256,128]{1,0:T(8,128)S(1)} %get-tuple-element.46), channel_id=1, source_target_pairs={{0,128},{64,192},{128,0},{192,64},{1,129},{65,193},{129,1},{193,65... | collective-permute-start | bytes 393224 | tf_op jit(solution)/shard_map/ppermute | solution.py:284
  80.9 6.1 %collective-permute-start.12 = (bf16[256,128]{1,0:T(8,128)(2,1)S(1)}, bf16[256,128]{1,0:T(8,128)(2,1)S(1)}, u32[]{:S(2)}, u32[]{:S(2)}) collective-permute-start(bf16[256,128]{1,0:T(8,128)(2,1)S(1)} %get-tuple-element.56), channel_id=1, source_target_pairs={{0,128},{64,192},{128,0},{192,64},{1,129},{65,193},{129,1},{193,65... | collective-permute-start | bytes 196616 | tf_op jit(solution)/shard_map/ppermute | solution.py:295
  81.8 5.9 %collective-permute-start.11 = (bf16[256,128]{1,0:T(8,128)(2,1)S(1)}, bf16[256,128]{1,0:T(8,128)(2,1)S(1)}, u32[]{:S(2)}, u32[]{:S(2)}) collective-permute-start(bf16[256,128]{1,0:T(8,128)(2,1)S(1)} %get-tuple-element.56), channel_id=1, source_target_pairs={{0,192},{64,0},{128,64},{192,128},{1,193},{65,1},{129,65},{193,129... | collective-permute-start | bytes 196616 | tf_op jit(solution)/shard_map/ppermute | solution.py:295
  82.5 5.2 %collective-permute-start.13 = (bf16[256,128]{1,0:T(8,128)(2,1)S(1)}, bf16[256,128]{1,0:T(8,128)(2,1)S(1)}, u32[]{:S(2)}, u32[]{:S(2)}) collective-permute-start(bf16[256,128]{1,0:T(8,128)(2,1)S(1)} %get-tuple-element.56), channel_id=1, source_target_pairs={{0,64},{64,128},{128,192},{192,0},{1,65},{65,129},{129,193},{193,1... | collective-permute-start | bytes 196616 | tf_op jit(solution)/shard_map/ppermute | solution.py:295
  87.7 6.5 %collective-permute-start.15 = (bf16[4,256,128]{2,1,0:T(8,128)(2,1)S(1)}, bf16[4,256,128]{2,1,0:T(8,128)(2,1)S(1)}, u32[]{:S(2)}, u32[]{:S(2)}) collective-permute-start(bf16[4,256,128]{2,1,0:T(8,128)(2,1)S(1)} %get-tuple-element.50.mine), channel_id=1, source_target_pairs={{0,56},{8,0},{16,8},{24,16},{32,24},{40,32},{48,40},{56,48},{1,57}... | collective-permute-start | bytes 786440 | tf_op jit(solution)/shard_map/ppermute | solution.py:220
  88.1 7.6 %collective-permute-start.14 = (bf16[4,256,128]{2,1,0:T(8,128)(2,1)S(1)}, bf16[4,256,128]{2,1,0:T(8,128)(2,1)S(1)}, u32[]{:S(2)}, u32[]{:S(2)}) collective-permute-start(bf16[4,256,128]{2,1,0:T(8,128)(2,1)S(1)} %get-tuple-element.50.mine), channel_id=1, source_target_pairs={{0,8},{8,16},{16,24},{24,32},{32,40},{40,48},{48,56},{56,0},{1,9},... | collective-permute-start | bytes 786440 | tf_op jit(solution)/shard_map/ppermute | solution.py:219
  93.8 2.6 %collective-permute-start.17 = (f32[8,27,8,128]{3,2,1,0:T(8,128)}, f32[8,27,8,128]{3,2,1,0:T(8,128)S(1)}, u32[]{:S(2)}, u32[]{:S(2)}) collective-permute-start(f32[8,27,8,128]{3,2,1,0:T(8,128)} %get-tuple-element.25), channel_id=1, source_target_pairs={{0,4},{4,0},{1,5},{5,1},{2,6},{6,2},{3,7},{7,3},{8,12},{12,8},{9,1... | collective-permute-start | bytes 2654216 | tf_op jit(solution)/shard_map/ppermute | solution.py:302
  95.8 2.0 %collective-permute-start.16 = (bf16[2,4,256,128]{3,2,1,0:T(8,128)(2,1)S(1)}, bf16[2,4,256,128]{3,2,1,0:T(8,128)(2,1)S(1)}, u32[]{:S(2)}, u32[]{:S(2)}) collective-permute-start(bf16[2,4,256,128]{3,2,1,0:T(8,128)(2,1)S(1)} %pad_maximum_fusion.1), channel_id=1, source_target_pairs={{0,4},{4,0},{1,5},{5,1},{2,6},{6,2},{3,7},{7,3},{8,12},{12,8},{9,1... | collective-permute-start | bytes 1572872 | tf_op jit(solution)/shard_map/ppermute | solution.py:222
  97.8 0.8 copy-start.5
  105.8 2.6 %collective-permute-start.18 = (f32[8,27,8,128]{3,2,1,0:T(8,128)}, f32[8,27,8,128]{3,2,1,0:T(8,128)S(1)}, u32[]{:S(2)}, u32[]{:S(2)}) collective-permute-start(f32[8,27,8,128]{3,2,1,0:T(8,128)} %get-tuple-element.33), channel_id=1, source_target_pairs={{0,4},{4,0},{1,5},{5,1},{2,6},{6,2},{3,7},{7,3},{8,12},{12,8},{9,1... | collective-permute-start | bytes 2654216 | tf_op jit(solution)/shard_map/ppermute | solution.py:302
  110.5 23.0 %all-to-all-start = ((bf16[8,216,128]{2,1,0:T(8,128)(2,1)}), bf16[8,216,128]{2,1,0:T(8,128)(2,1)S(1)}, u32[]{:S(2)}, u32[]{:S(2)}) async-start(bf16[8,216,128]{2,1,0:T(8,128)(2,1)} %fusion), calls=%async_computation | async-start | bytes 884736 | tf_op jit(solution)/shard_map/all_to_all | solution.py:322
  121.8 11.8 %collective-permute-start.19 = (f32[256,128]{1,0:T(8,128)S(1)}, f32[256,128]{1,0:T(8,128)S(1)}, u32[]{:S(2)}, u32[]{:S(2)}) collective-permute-start(f32[256,128]{1,0:T(8,128)S(1)} %get-tuple-element.43), channel_id=1, source_target_pairs={{0,65},{1,64},{2,128},{3,192},{64,1},{65,130},{66,129},{67,193},{1... | collective-permute-start | bytes 393224 | tf_op jit(solution)/shard_map/ppermute | solution.py:212
  124.8 12.2 %collective-permute-start.22 = (f32[256,128]{1,0:T(8,128)S(1)}, f32[256,128]{1,0:T(8,128)S(1)}, u32[]{:S(2)}, u32[]{:S(2)}) collective-permute-start(f32[256,128]{1,0:T(8,128)S(1)} %get-tuple-element.40), channel_id=1, source_target_pairs={{0,192},{1,0},{2,64},{3,128},{64,193},{65,1},{66,65},{67,129},{128... | collective-permute-start | bytes 393224 | tf_op jit(solution)/shard_map/ppermute | solution.py:212
  127.3 9.6 %collective-permute-start.21 = (f32[256,128]{1,0:T(8,128)S(1)}, f32[256,128]{1,0:T(8,128)S(1)}, u32[]{:S(2)}, u32[]{:S(2)}) collective-permute-start(f32[256,128]{1,0:T(8,128)S(1)} %get-tuple-element.41), channel_id=1, source_target_pairs={{0,128},{1,192},{2,0},{3,64},{64,129},{65,193},{66,1},{67,65},{128... | collective-permute-start | bytes 393224 | tf_op jit(solution)/shard_map/ppermute | solution.py:212
  127.3 12.4 %collective-permute-start.20 = (f32[256,128]{1,0:T(8,128)S(1)}, f32[256,128]{1,0:T(8,128)S(1)}, u32[]{:S(2)}, u32[]{:S(2)}) collective-permute-start(f32[256,128]{1,0:T(8,128)S(1)} %get-tuple-element.42), channel_id=1, source_target_pairs={{0,64},{1,128},{2,192},{3,0},{64,65},{65,129},{66,193},{67,1},{128... | collective-permute-start | bytes 393224 | tf_op jit(solution)/shard_map/ppermute | solution.py:212
  133.6 9.9 %collective-permute-start.23 = (f32[27,8,128]{2,1,0:T(8,128)S(1)}, f32[27,8,128]{2,1,0:T(8,128)S(1)}, u32[]{:S(2)}, u32[]{:S(2)}) collective-permute-start(f32[27,8,128]{2,1,0:T(8,128)S(1)} %bitcast.68), channel_id=1, source_target_pairs={{0,65},{1,64},{2,128},{3,192},{64,1},{65,130},{66,129},{67,193},{1... | collective-permute-start | bytes 331784 | tf_op jit(solution)/shard_map/ppermute | solution.py:212
Sparse Core Ops, SparseCore 0:
  17.2 43.0 all-gather.1
  106.1 36.8 reduce-scatter.3

commit v4 on v3

--- a/solution.py
+++ b/solution.py
@@ -10,6 +10,7 @@
 STEPS = (1, 2, -1, -2)
 SPACE = ("x", "z", "core")
 CELLS = 224
+EARLY = 24
 BF = jnp.bfloat16
 F32 = jnp.float32
 
@@ -33,7 +34,7 @@
             for j in range(4):
                 for k in range(4):
                     spread[move, i, j, k, i * 36 + (j + move // 3) * 6 + k + move % 3] = 1
-    lanes = np.zeros((128, 2048), np.float32)
+    lanes = np.zeros((32, 2048), np.float32)
     for brick in range(2):
         for column in range(384):
             lanes[brick * 6 + column // 64, brick * 384 + column] = 1
@@ -114,7 +115,7 @@
             compact = part if compact is None else compact + part
         matched[at] = compact
         own[at] = views[0][64:192, :]
-        found = dot(compact, lanes[...]).astype(BF)
+        found = dot(compact[:, :32], lanes[...]).astype(BF)
         rows = [views[0][0:64, :], views[0][224:288, :]]
         rows += [view[device % 2 * 224 : device % 2 * 224 + 64, :] for device, view in enumerate(views[1:])]
         fill(q_in, at * 2, found[:, :768], jnp.concatenate(rows, 0), pick[...], local[...], spread[...])
@@ -162,7 +163,7 @@
     def _(turn):
         at = (ids[0] + turn) & 3
         views = around(ids, mine, before, after, other, turn)
-        found = dot(matched[at], lanes[:, :768]).astype(BF)
+        found = dot(matched[at, :, :32], lanes[:, :768]).astype(BF)
         rows = [views[0][0:128, :]]
         rows += [view[device % 2 * 64 : device % 2 * 64 + 64, :] for device, view in enumerate(views[1:])]
         fill(q_hidden, at * 2, found, jnp.concatenate(rows, 0), pick[...], local[...], spread[...])
@@ -178,7 +179,7 @@
     def _(turn):
         at = (ids[0] + turn) & 3
         views = around(ids, mine, before, after, other, turn)
-        found = dot(matched[at], lanes[:, 768:]).astype(BF)
+        found = dot(matched[at, :, :32], lanes[:, 768:]).astype(BF)
         rows = jnp.concatenate([view[128:256, :] for view in views], 0)
         fill(q_back, at * 2, found, rows, pick_back[...], local[...], spread[...])
 
@@ -210,9 +211,11 @@
     for at, place in enumerate(still):
         moved[place] = still[(at + 1) % len(still)]
     came = lax.ppermute(value, ("x", "chan"), [(p[0] * 4 + p[1], q[0] * 4 + q[1]) for p, q in moved.items()])
-    if not still:
-        return came
-    return jnp.where(lax.axis_index("x") == lax.axis_index("chan"), value, came)
+    return (value, came) if still else (came, came)
+
+
+def settled(value, came):
+    return came if value is came else jnp.where(lax.axis_index("x") == lax.axis_index("chan"), value, came)
 
 
 def spread_out(mine):
@@ -232,7 +235,7 @@
     z = lax.axis_index("z")
     ids = jnp.stack([x, chan, core, (z == 0).astype(jnp.int32), (z == 7).astype(jnp.int32)]).astype(jnp.int32)
 
-    shards = jnp.stack([weight_first, turn_over(weight_second, lambda a, b: (b, a))])
+    shards = jnp.stack([weight_first, settled(*turn_over(weight_second, lambda a, b: (b, a)))])
     blocks = jnp.transpose(lax.all_gather(shards, ("z", "core"), axis=1, tiled=True), (0, 2, 1, 3))
 
     active = mask.astype(F32)[:, None]
@@ -263,7 +266,7 @@
     packed = jnp.concatenate([masked[:64], grad_second, compact, masked[64:]], 0)
     turned = jnp.stack(
         [
-            turn_over(packed, lambda a, b: (b, a - r))
+            settled(*turn_over(packed, lambda a, b: (b, a - r)))
             for r in range(4)
         ]
     )
@@ -302,8 +305,9 @@
         return keep + lax.ppermute(send, "core", [(0, 1), (1, 0)])
 
     first_mine = both_cores(keep1, send1)
-    first_sum = lax.psum_scatter(first_mine, "z", scatter_dimension=0, tiled=True).reshape(27, 8, 128)
-    before, after, other, _ = lax.optimization_barrier((*spread_out(along), first_mine))
+    first_early = first_mine[:, :EARLY]
+    first_sum = lax.psum_scatter(first_early, "z", scatter_dimension=0, tiled=True).reshape(EARLY, 8, 128)
+    before, after, other, _ = lax.optimization_barrier((*spread_out(along), first_early))
     keep2, send2, q_hidden = call(
         weigh_second,
         [pieces, pieces, columns],
@@ -317,7 +321,8 @@
         own,
         *consts,
     )
-    second_mine = both_cores(keep2, send2).astype(BF).reshape(8, 216, 128)
+    second_mine = jnp.concatenate([both_cores(keep2, send2).astype(BF), first_mine[:, EARLY:].astype(BF)], 1)
+    second_mine = second_mine.reshape(8, -1, 128)
     q_hidden, second_mine = lax.optimization_barrier((q_hidden, second_mine))
     moved = lax.all_to_all(second_mine, "z", 0, 0, tiled=True)
     (reduced,) = call(
@@ -335,10 +340,11 @@
         *consts,
     )
     parts = [turn_over(reduced[r], lambda a, b: (b + r, a)) for r in range(4)]
-    second_sum = jnp.sum(moved.astype(F32), axis=0).reshape(27, 8, 128)
-    *parts, _ = lax.optimization_barrier((*parts, second_sum))
-    second_sum = turn_over(second_sum, lambda a, b: (b, a))
-    total = parts[0] + parts[1] + parts[2] + parts[3]
+    sums = jnp.sum(moved.astype(F32), axis=0).reshape(-1, 8, 128)
+    second_sum = settled(*turn_over(sums[:27], lambda a, b: (b, a)))
+    first_sum = jnp.concatenate([first_sum, sums[27:]], 0)
+    *came, _ = lax.optimization_barrier((*(part[1] for part in parts), second_sum))
+    total = settled(parts[0][0], came[0]) + came[1] + came[2] + came[3]
     output = (active * total[0:128]).astype(BF)
     features_grad = (active * total[128:256]).astype(BF)
 

time: 153 us -> 158 us (1.033)
  other arithmetic: 8.9 us -> 11.3 us
  local copies, waits for them, and re-layouts: 2.58 us -> 4.67 us
    ppermute x10, waiting for transfers between devices: 22.9 us -> 13.9 us  [turn_over(): lax.ppermute(value, ('x', 'chan'), [(p[0] * 4 + p[1], q[0] * 4 + q[1]) fo...]
    reduce_scatter x0 -> x1, waiting for transfers between devices: none -> 6.4 us  [on_device(): lax.psum_scatter(first_early, 'z', scatter_dimension=0, tiled=True)]
    all_to_all x1, waiting for transfers between devices: 0.01 us -> 2.09 us  [on_device(): moved = lax.all_to_all(second_mine, 'z', 0, 0, tiled=True)]
  transfers between devices with their start and end apart: 27 -> 27, of which waited for: 18 -> 17; matrix products, arithmetic and copies ran while one was open for 5% -> 7% of each run, Pallas kernels for 13% -> 13%
where the time goes in v4:
time: 158 us; the launch traced here: 155 us
  waiting for transfers between devices  51.8 us (33%)
  starting transfers between devices  41.9 us (27%)
  Pallas kernels  31.4 us (20%)
  between operations  14.3 us (9%)
  other arithmetic  11.3 us (7%)
  local copies, waits for them, and re-layouts  4.67 us (3%)
    pallas_call x5, Pallas kernels, call(): pl.pallas_call(kernel, out_shape=outs, in_specs=[smem if value.dtype == j...  31.4 us
    ppermute x10, starting transfers between devices, turn_over(): lax.ppermute(value, ('x', 'chan'), [(p[0] * 4 + p[1], q[0] * 4 + q[1]) fo...  20.7 us
    ppermute x10, waiting for transfers between devices, turn_over(): lax.ppermute(value, ('x', 'chan'), [(p[0] * 4 + p[1], q[0] * 4 + q[1]) fo...  13.9 us
    ppermute x2, waiting for transfers between devices, spread_out(): after = lax.ppermute(mine, 'z', [(i, (i - 1) % 8) for i in range(8)])  7.93 us
    ppermute x3, waiting for transfers between devices, on_device(): lax.ppermute(partial[r], 'x', [(a, (a + r) % 4) for a in range(4)])  7.73 us
    reduce_scatter x1, waiting for transfers between devices, on_device(): lax.psum_scatter(first_early, 'z', scatter_dimension=0, tiled=True)  6.4 us
    ppermute x2, starting transfers between devices, spread_out(): after = lax.ppermute(mine, 'z', [(i, (i - 1) % 8) for i in range(8)])  6.28 us
    ppermute x2, waiting for transfers between devices, spread_out(): before = lax.ppermute(mine, 'z', [(i, (i + 1) % 8) for i in range(8)])  5.56 us
  transfers between devices with their start and end apart: 27, of which 17 were waited for; matrix products, arithmetic and copies ran while one was open for 7% of the time, Pallas kernels for 13%

profile of v4, /device:TPU:6, one launch (start us, length us, event | category | flops | bytes accessed | tf_op | source)
XLA Modules:
  0.0 155.4 jit_solution(17970840831188252397)
XLA Ops:
  7.2 3.0 %collective-permute-start.7 = (bf16[8,27,128]{2,0,1:T(8,128)(2,1)}, bf16[8,27,128]{2,0,1:T(8,128)(2,1)S(1)}, u32[]{:S(2)}, u32[]{:S(2)}) collective-permute-start(bf16[8,27,128]{2,0,1:T(8,128)(2,1)} %param.23), channel_id=1, source_target_pairs={{0,65},{1,64},{2,128},{3,192},{64,1},{65,130},{66,129},{67,193},{1... | collective-permute-start | bytes 165896 | tf_op jit(solution)/shard_map/ppermute | solution.py:213
  10.2 5.4 %collective-permute-done.7 = bf16[8,27,128]{2,0,1:T(8,128)(2,1)S(1)} collective-permute-done((bf16[8,27,128]{2,0,1:T(8,128)(2,1)}, bf16[8,27,128]{2,0,1:T(8,128)(2,1)S(1)}, u32[]{:S(2)}, u32[]{:S(2)}) %collective-permute-start.7) | collective-permute-done | bytes 55328 | tf_op jit(solution)/shard_map/ppermute | solution.py:213
  15.6 1.5 pad_maximum_fusion.4
  17.1 0.7 convert_element_type.54
  17.8 0.8 fusion.26
  18.6 0.8 fusion.21
  19.5 0.9 multiply_convert_fusion.1
  20.4 3.0 %collective-permute-start = (bf16[288,128]{1,0:T(8,128)(2,1)S(1)}, bf16[288,128]{1,0:T(8,128)(2,1)S(1)}, u32[]{:S(2)}, u32[]{:S(2)}) collective-permute-start(bf16[288,128]{1,0:T(8,128)(2,1)S(1)} %pad_maximum_fusion.5), channel_id=1, source_target_pairs={{0,65},{1,64},{2,128},{3,192},{64,1},{65,130},{66,129},{67,193},{1... | collective-permute-start | bytes 221192 | tf_op jit(solution)/shard_map/ppermute | solution.py:213
  23.5 3.1 %collective-permute-start.1 = (bf16[288,128]{1,0:T(8,128)(2,1)S(1)}, bf16[288,128]{1,0:T(8,128)(2,1)S(1)}, u32[]{:S(2)}, u32[]{:S(2)}) collective-permute-start(bf16[288,128]{1,0:T(8,128)(2,1)S(1)} %pad_maximum_fusion.5), channel_id=1, source_target_pairs={{0,3},{1,67},{2,131},{3,195},{64,0},{65,64},{66,128},{67,192},{128... | collective-permute-start | bytes 221192 | tf_op jit(solution)/shard_map/ppermute | solution.py:213
  26.6 0.6 collective-permute-start.3
  27.1 7.2 %collective-permute-done = bf16[288,128]{1,0:T(8,128)(2,1)S(1)} collective-permute-done((bf16[288,128]{1,0:T(8,128)(2,1)S(1)}, bf16[288,128]{1,0:T(8,128)(2,1)S(1)}, u32[]{:S(2)}, u32[]{:S(2)}) %collective-permute-start) | collective-permute-done | bytes 73760 | tf_op jit(solution)/shard_map/ppermute | solution.py:213
  34.4 0.5 collective-permute-done.3
  34.9 0.1 fusion.30
  34.9 5.9 %collective-permute-start.5 = (bf16[4,288,128]{2,1,0:T(8,128)(2,1)S(1)}, bf16[4,288,128]{2,1,0:T(8,128)(2,1)S(1)}, u32[]{:S(2)}, u32[]{:S(2)}) collective-permute-start(bf16[4,288,128]{2,1,0:T(8,128)(2,1)S(1)} %get-tuple-element.48.mine), channel_id=1, source_target_pairs={{0,56},{8,0},{16,8},{24,16},{32,24},{40,32},{48,40},{56,48},{1,57}... | collective-permute-start | bytes 884744 | tf_op jit(solution)/shard_map/ppermute | solution.py:223
  40.9 7.5 %collective-permute-done.5.after = bf16[4,288,128]{2,1,0:T(8,128)(2,1)S(1)} collective-permute-done((bf16[4,288,128]{2,1,0:T(8,128)(2,1)S(1)}, bf16[4,288,128]{2,1,0:T(8,128)(2,1)S(1)}, u32[]{:S(2)}, u32[]{:S(2)}) %collective-permute-start.5) | collective-permute-done | bytes 294944 | tf_op jit(solution)/shard_map/ppermute | solution.py:223
  48.4 4.1 %collective-permute-done.4.before = bf16[4,288,128]{2,1,0:T(8,128)(2,1)S(1)} collective-permute-done((bf16[4,288,128]{2,1,0:T(8,128)(2,1)S(1)}, bf16[4,288,128]{2,1,0:T(8,128)(2,1)S(1)}, u32[]{:S(2)}, u32[]{:S(2)}) %collective-permute-start.4) | collective-permute-done | bytes 294944 | tf_op jit(solution)/shard_map/ppermute | solution.py:222
  52.5 0.1 pad_maximum_fusion
  52.6 0.1 collective-permute-start.6
  52.7 0.1 stack.88.ids
  52.8 1.9 %collective-permute-done.6.other = bf16[2,4,288,128]{3,2,1,0:T(8,128)(2,1)S(1)} collective-permute-done((bf16[2,4,288,128]{3,2,1,0:T(8,128)(2,1)S(1)}, bf16[2,4,288,128]{3,2,1,0:T(8,128)(2,1)S(1)}, u32[]{:S(2)}, u32[]{:S(2)}) %collective-permute-start.6) | collective-permute-done | bytes 589856 | tf_op jit(solution)/shard_map/ppermute | solution.py:225
  54.7 0.8 copy-done.7
  55.5 7.4 %shard_map.210 = (bf16[8,9,96,128]{3,2,1,0:T(8,128)(2,1)}, bf16[8,9,96,128]{3,2,1,0:T(8,128)(2,1)}, bf16[4,128,128]{2,1,0:T(8,128)(2,1)S(1)}, bf16[4,32,128]{2,1,0:T(8,128)(2,1)S(1)}) custom-call(s32[5]{0:T(128)S(1)} %stack.88.ids, bf16[4,288,128]{2,1,0:T(8,128)(2,1)S(1)} %get-tuple-element.48.mine, bf16[4,288,128]{2,1,0:T(8,128)(2,1)S(1)} %collective-permute-done.4.before, ...), custom_call_target="tpu_custom_call" | custom-call | tf_op jit(solution)/shard_map/pallas_call | solution.py:197
  62.9 4.5 %shard_map.211 = f32[4,256,128]{2,1,0:T(8,128)S(1)} custom-call(s32[5]{0:T(128)S(1)} %stack.88.ids, bf16[8,9,96,128]{3,2,1,0:T(8,128)(2,1)} %get-tuple-element.22.q_in, bf16[8,9,96,128]{3,2,1,0:T(8,128)(2,1)} %get-tuple-element.23.q_back, bf16[2,27,128,128]{3,2,1,0:T(8,128)(2,1)} %bitcast.71), custom_call_target="tpu_custom_call" | custom-call | tf_op jit(solution)/shard_map/pallas_call | solution.py:197
  67.5 3.8 %collective-permute-start.8 = (f32[256,128]{1,0:T(8,128)S(1)}, f32[256,128]{1,0:T(8,128)S(1)}, u32[]{:S(2)}, u32[]{:S(2)}) collective-permute-start(f32[256,128]{1,0:T(8,128)S(1)} %get-tuple-element.44), channel_id=1, source_target_pairs={{0,64},{64,128},{128,192},{192,0},{1,65},{65,129},{129,193},{193,1... | collective-permute-start | bytes 393224 | tf_op jit(solution)/shard_map/ppermute | solution.py:287
  71.2 1.6 collective-permute-start.9
  72.8 1.5 collective-permute-done.8
  74.3 6.2 %collective-permute-done.10 = f32[256,128]{1,0:T(8,128)S(1)} collective-permute-done((f32[256,128]{1,0:T(8,128)S(1)}, f32[256,128]{1,0:T(8,128)S(1)}, u32[]{:S(2)}, u32[]{:S(2)}) %collective-permute-start.10) | collective-permute-done | bytes 131104 | tf_op jit(solution)/shard_map/ppermute | solution.py:287
  80.6 0.1 multiply_convert_fusion
  80.7 0.8 collective-permute-start.12
  81.5 0.7 collective-permute-start.11
  82.3 2.5 %collective-permute-start.13 = (bf16[256,128]{1,0:T(8,128)(2,1)S(1)}, bf16[256,128]{1,0:T(8,128)(2,1)S(1)}, u32[]{:S(2)}, u32[]{:S(2)}) collective-permute-start(bf16[256,128]{1,0:T(8,128)(2,1)S(1)} %get-tuple-element.56), channel_id=1, source_target_pairs={{0,64},{64,128},{128,192},{192,0},{1,65},{65,129},{129,193},{193,1... | collective-permute-start | bytes 196616 | tf_op jit(solution)/shard_map/ppermute | solution.py:298
  84.8 2.0 %collective-permute-done.12 = bf16[256,128]{1,0:T(8,128)(2,1)S(1)} collective-permute-done((bf16[256,128]{1,0:T(8,128)(2,1)S(1)}, bf16[256,128]{1,0:T(8,128)(2,1)S(1)}, u32[]{:S(2)}, u32[]{:S(2)}) %collective-permute-start.12) | collective-permute-done | bytes 65568 | tf_op jit(solution)/shard_map/ppermute | solution.py:298
  86.8 0.7 collective-permute-done.11
  87.5 0.4 collective-permute-start.15
  87.8 1.8 %collective-permute-start.14 = (bf16[4,256,128]{2,1,0:T(8,128)(2,1)S(1)}, bf16[4,256,128]{2,1,0:T(8,128)(2,1)S(1)}, u32[]{:S(2)}, u32[]{:S(2)}) collective-permute-start(bf16[4,256,128]{2,1,0:T(8,128)(2,1)S(1)} %get-tuple-element.50.mine), channel_id=1, source_target_pairs={{0,8},{8,16},{16,24},{24,32},{32,40},{40,48},{48,56},{56,0},{1,9},... | collective-permute-start | bytes 786440 | tf_op jit(solution)/shard_map/ppermute | solution.py:222
  89.6 3.9 %shard_map.212 = (f32[8,27,8,128]{3,2,1,0:T(8,128)S(1)}, f32[8,27,8,128]{3,2,1,0:T(8,128)}) custom-call(s32[5]{0:T(128)S(1)} %stack.88.ids, bf16[4,256,128]{2,1,0:T(8,128)(2,1)S(1)} %get-tuple-element.50.mine, bf16[8,9,96,128]{3,2,1,0:T(8,128)(2,1)} %get-tuple-element.22.q_in), custom_call_target="tpu_custom_call" | custom-call | tf_op jit(solution)/shard_map/pallas_call | solution.py:197
  93.5 0.4 collective-permute-done.15.after
  93.9 1.5 collective-permute-done.14.before
  95.5 0.9 pad_maximum_fusion.1
  96.3 0.1 add.67
  96.4 0.9 slice.97
  97.4 1.1 collective-permute-done.16.other
  98.4 0.8 copy-done.6
  99.2 7.3 %shard_map.213 = (f32[8,27,8,128]{3,2,1,0:T(8,128)}, f32[8,27,8,128]{3,2,1,0:T(8,128)}, bf16[8,9,96,128]{3,2,1,0:T(8,128)(2,1)}) custom-call(s32[5]{0:T(128)S(1)} %stack.88.ids, bf16[4,256,128]{2,1,0:T(8,128)(2,1)S(1)} %get-tuple-element.50.mine, bf16[4,256,128]{2,1,0:T(8,128)(2,1)S(1)} %collective-permute-done.14.before, ...), custom_call_target="tpu_custom_call" | custom-call | tf_op jit(solution)/shard_map/pallas_call | solution.py:197
  106.5 0.1 collective-permute-start.18
  106.7 2.4 %collective-permute-done.18 = f32[8,27,8,128]{3,2,1,0:T(8,128)S(1)} collective-permute-done((f32[8,27,8,128]{3,2,1,0:T(8,128)}, f32[8,27,8,128]{3,2,1,0:T(8,128)S(1)}, u32[]{:S(2)}, u32[]{:S(2)}) %collective-permute-start.18) | collective-permute-done | bytes 884768 | tf_op jit(solution)/shard_map/ppermute | solution.py:305
  109.2 1.3 add_convert_fusion
  110.5 0.8 maximum_bitcast_fusion
  111.3 3.5 %all-to-all-start = ((bf16[8,240,128]{2,1,0:T(8,128)(2,1)}), bf16[8,240,128]{2,1,0:T(8,128)(2,1)S(1)}, u32[]{:S(2)}, u32[]{:S(2)}) async-start(bf16[8,240,128]{2,1,0:T(8,128)(2,1)} %maximum_bitcast_fusion), calls=%async_computation | async-start | bytes 983040 | tf_op jit(solution)/shard_map/all_to_all | solution.py:327
  114.8 8.2 %shard_map.214 = f32[4,256,128]{2,1,0:T(8,128)} custom-call(s32[5]{0:T(128)S(1)} %stack.88.ids, bf16[4,256,128]{2,1,0:T(8,128)(2,1)S(1)} %get-tuple-element.50.mine, bf16[4,256,128]{2,1,0:T(8,128)(2,1)S(1)} %collective-permute-done.14.before, bf16[4,256,128]{2,1,0:T(8,128)(2,1)S(1)} %collective-permute-done.15.after, bf16[2,4,256,128]{3,2,1,0:T(8,128)(2,1)} %copy-done.6, ...), custom_call_target="tpu_custom_call" | custom-call | tf_op jit(solution)/shard_map/pallas_call | solution.py:197
  123.0 1.1 slice_bitcast_fusion
  124.2 1.1 collective-permute-start.22
  125.3 2.0 %collective-permute-start.21 = (f32[256,128]{1,0:T(8,128)S(1)}, f32[256,128]{1,0:T(8,128)S(1)}, u32[]{:S(2)}, u32[]{:S(2)}) collective-permute-start(f32[256,128]{1,0:T(8,128)S(1)} %get-tuple-element.41), channel_id=1, source_target_pairs={{0,128},{1,192},{2,0},{3,64},{64,129},{65,193},{66,1},{67,65},{128... | collective-permute-start | bytes 393224 | tf_op jit(solution)/shard_map/ppermute | solution.py:213
  127.3 4.6 %collective-permute-start.20 = (f32[256,128]{1,0:T(8,128)S(1)}, f32[256,128]{1,0:T(8,128)S(1)}, u32[]{:S(2)}, u32[]{:S(2)}) collective-permute-start(f32[256,128]{1,0:T(8,128)S(1)} %get-tuple-element.42), channel_id=1, source_target_pairs={{0,64},{1,128},{2,192},{3,0},{64,65},{65,129},{66,193},{67,1},{128... | collective-permute-start | bytes 393224 | tf_op jit(solution)/shard_map/ppermute | solution.py:213
  131.9 1.0 collective-permute-start.19
  132.8 2.1 %all-to-all-done = bf16[8,240,128]{2,1,0:T(8,128)(2,1)S(1)} async-done(((bf16[8,240,128]{2,1,0:T(8,128)(2,1)}), bf16[8,240,128]{2,1,0:T(8,128)(2,1)S(1)}, u32[]{:S(2)}, u32[]{:S(2)}) %all-to-all-start) | async-done | bytes 491552 | tf_op jit(solution)/shard_map/all_to_all | solution.py:327
  134.9 0.1 convert_reduce_fusion
  135.0 2.4 %collective-permute-start.23 = (f32[27,8,128]{2,1,0:T(8,128)S(1)}, f32[27,8,128]{2,1,0:T(8,128)S(1)}, u32[]{:S(2)}, u32[]{:S(2)}) collective-permute-start(f32[27,8,128]{2,1,0:T(8,128)S(1)} %slice_bitcast_fusion.8), channel_id=1, source_target_pairs={{0,65},{1,64},{2,128},{3,192},{64,1},{65,130},{66,129},{67,193},{1... | collective-permute-start | bytes 331784 | tf_op jit(solution)/shard_map/ppermute | solution.py:213
  137.4 6.4 %reduce-scatter.2.cloned.1.call-done = f32[1,24,8,128]{3,2,1,0:T(8,128)} async-done(((f32[8,24,8,128]{3,2,1,0:T(8,128)}), f32[1,24,8,128]{3,2,1,0:T(8,128)}) %reduce-scatter.2.cloned.1.call-update) | async-done | bytes 98320 | tf_op jit(solution)/shard_map/reduce_scatter | solution.py:309
  143.8 1.5 maximum_bitcast_fusion.1
  145.3 0.9 collective-permute-done.23
  146.2 1.0 add_add_fusion
  147.2 0.7 fusion.3
  147.9 0.7 fusion.32
  (46 shorter events, 0.4 us)
Async XLA Ops:
  7.2 55.8 %all-gather.2.cloned.1.call-start = ((), (), s32[]{:S(2)}) async-start(), calls=%async_computation.2 | async-start | bytes 1880064 | tf_op jit(solution)/shard_map/all_gather | solution.py:239
  7.2 8.4 %collective-permute-start.7 = (bf16[8,27,128]{2,0,1:T(8,128)(2,1)}, bf16[8,27,128]{2,0,1:T(8,128)(2,1)S(1)}, u32[]{:S(2)}, u32[]{:S(2)}) collective-permute-start(bf16[8,27,128]{2,0,1:T(8,128)(2,1)} %param.23), channel_id=1, source_target_pairs={{0,65},{1,64},{2,128},{3,192},{64,1},{65,130},{66,129},{67,193},{1... | collective-permute-start | bytes 165896 | tf_op jit(solution)/shard_map/ppermute | solution.py:213
  17.1 126.7 %reduce-scatter.2.cloned.1.call-start = ((), (), s32[]{:S(2)}) async-start(), calls=%async_computation.3 | async-start | bytes 884736 | tf_op jit(solution)/shard_map/reduce_scatter | solution.py:309
  19.4 36.1 %copy-start = (bf16[864,224]{1,0:T(8,128)(2,1)S(1)}, bf16[864,224]{1,0:T(8,128)(2,1)}, u32[]{:S(2)}) copy-start(bf16[864,224]{1,0:T(8,128)(2,1)} %constant.72.clone.spread) | copy-start | bytes 1161220
  19.4 36.1 %copy-start.1 = (bf16[32,2048]{1,0:T(8,128)(2,1)S(1)}, bf16[32,2048]{1,0:T(8,128)(2,1)}, u32[]{:S(2)}) copy-start(bf16[32,2048]{1,0:T(8,128)(2,1)} %constant.73.clone.lanes) | copy-start | bytes 393220
  19.4 36.1 %copy-start.2 = (f32[224,128]{1,0:T(8,128)S(1)}, f32[224,128]{1,0:T(8,128)}, u32[]{:S(2)}) copy-start(f32[224,128]{1,0:T(8,128)} %constant.71.clone.local) | copy-start | bytes 344068
  19.4 36.1 %copy-start.3 = (bf16[224,32]{1,0:T(8,128)(2,1)S(1)}, bf16[224,32]{1,0:T(8,128)(2,1)}, u32[]{:S(2)}) copy-start(bf16[224,32]{1,0:T(8,128)(2,1)} %constant.70.clone.pick_back) | copy-start | bytes 43012
  19.5 36.1 %copy-start.4 = (bf16[224,32]{1,0:T(8,128)(2,1)S(1)}, bf16[224,32]{1,0:T(8,128)(2,1)}, u32[]{:S(2)}) copy-start(bf16[224,32]{1,0:T(8,128)(2,1)} %constant.69.clone.pick) | copy-start | bytes 43012
  19.5 36.1 %copy-start.5 = (bf16[16,128]{1,0:T(8,128)(2,1)S(1)}, bf16[16,128]{1,0:T(8,128)(2,1)}, u32[]{:S(2)}) copy-start(bf16[16,128]{1,0:T(8,128)(2,1)} %constant.74.clone.sources) | copy-start | bytes 12292
  20.4 13.9 %collective-permute-start = (bf16[288,128]{1,0:T(8,128)(2,1)S(1)}, bf16[288,128]{1,0:T(8,128)(2,1)S(1)}, u32[]{:S(2)}, u32[]{:S(2)}) collective-permute-start(bf16[288,128]{1,0:T(8,128)(2,1)S(1)} %pad_maximum_fusion.5), channel_id=1, source_target_pairs={{0,65},{1,64},{2,128},{3,192},{64,1},{65,130},{66,129},{67,193},{1... | collective-permute-start | bytes 221192 | tf_op jit(solution)/shard_map/ppermute | solution.py:213
  23.5 10.9 %collective-permute-start.2 = (bf16[288,128]{1,0:T(8,128)(2,1)S(1)}, bf16[288,128]{1,0:T(8,128)(2,1)S(1)}, u32[]{:S(2)}, u32[]{:S(2)}) collective-permute-start(bf16[288,128]{1,0:T(8,128)(2,1)S(1)} %pad_maximum_fusion.5), channel_id=1, source_target_pairs={{0,2},{1,66},{2,130},{3,194},{64,3},{65,67},{66,131},{67,195},{128... | collective-permute-start | bytes 221192 | tf_op jit(solution)/shard_map/ppermute | solution.py:213
  23.5 10.9 %collective-permute-start.1 = (bf16[288,128]{1,0:T(8,128)(2,1)S(1)}, bf16[288,128]{1,0:T(8,128)(2,1)S(1)}, u32[]{:S(2)}, u32[]{:S(2)}) collective-permute-start(bf16[288,128]{1,0:T(8,128)(2,1)S(1)} %pad_maximum_fusion.5), channel_id=1, source_target_pairs={{0,3},{1,67},{2,131},{3,195},{64,0},{65,64},{66,128},{67,192},{128... | collective-permute-start | bytes 221192 | tf_op jit(solution)/shard_map/ppermute | solution.py:213
  26.6 8.3 %collective-permute-start.3 = (bf16[288,128]{1,0:T(8,128)(2,1)S(1)}, bf16[288,128]{1,0:T(8,128)(2,1)S(1)}, u32[]{:S(2)}, u32[]{:S(2)}) collective-permute-start(bf16[288,128]{1,0:T(8,128)(2,1)S(1)} %pad_maximum_fusion.5), channel_id=1, source_target_pairs={{0,1},{1,65},{2,129},{3,193},{64,2},{65,66},{66,130},{67,194},{128... | collective-permute-start | bytes 221192 | tf_op jit(solution)/shard_map/ppermute | solution.py:213
  34.9 13.5 %collective-permute-start.5 = (bf16[4,288,128]{2,1,0:T(8,128)(2,1)S(1)}, bf16[4,288,128]{2,1,0:T(8,128)(2,1)S(1)}, u32[]{:S(2)}, u32[]{:S(2)}) collective-permute-start(bf16[4,288,128]{2,1,0:T(8,128)(2,1)S(1)} %get-tuple-element.48.mine), channel_id=1, source_target_pairs={{0,56},{8,0},{16,8},{24,16},{32,24},{40,32},{48,40},{56,48},{1,57}... | collective-permute-start | bytes 884744 | tf_op jit(solution)/shard_map/ppermute | solution.py:223
  40.9 11.6 %collective-permute-start.4 = (bf16[4,288,128]{2,1,0:T(8,128)(2,1)S(1)}, bf16[4,288,128]{2,1,0:T(8,128)(2,1)S(1)}, u32[]{:S(2)}, u32[]{:S(2)}) collective-permute-start(bf16[4,288,128]{2,1,0:T(8,128)(2,1)S(1)} %get-tuple-element.48.mine), channel_id=1, source_target_pairs={{0,8},{8,16},{16,24},{24,32},{32,40},{40,48},{48,56},{56,0},{1,9},... | collective-permute-start | bytes 884744 | tf_op jit(solution)/shard_map/ppermute | solution.py:222
  52.6 2.1 %collective-permute-start.6 = (bf16[2,4,288,128]{3,2,1,0:T(8,128)(2,1)S(1)}, bf16[2,4,288,128]{3,2,1,0:T(8,128)(2,1)S(1)}, u32[]{:S(2)}, u32[]{:S(2)}) collective-permute-start(bf16[2,4,288,128]{3,2,1,0:T(8,128)(2,1)S(1)} %pad_maximum_fusion), channel_id=1, source_target_pairs={{0,4},{4,0},{1,5},{5,1},{2,6},{6,2},{3,7},{7,3},{8,12},{12,8},{9,1... | collective-permute-start | bytes 1769480 | tf_op jit(solution)/shard_map/ppermute | solution.py:225
  54.7 0.8 copy-start.7
  67.5 6.8 %collective-permute-start.8 = (f32[256,128]{1,0:T(8,128)S(1)}, f32[256,128]{1,0:T(8,128)S(1)}, u32[]{:S(2)}, u32[]{:S(2)}) collective-permute-start(f32[256,128]{1,0:T(8,128)S(1)} %get-tuple-element.44), channel_id=1, source_target_pairs={{0,64},{64,128},{128,192},{192,0},{1,65},{65,129},{129,193},{193,1... | collective-permute-start | bytes 393224 | tf_op jit(solution)/shard_map/ppermute | solution.py:287
  71.2 9.3 %collective-permute-start.10 = (f32[256,128]{1,0:T(8,128)S(1)}, f32[256,128]{1,0:T(8,128)S(1)}, u32[]{:S(2)}, u32[]{:S(2)}) collective-permute-start(f32[256,128]{1,0:T(8,128)S(1)} %get-tuple-element.45), channel_id=1, source_target_pairs={{0,192},{64,0},{128,64},{192,128},{1,193},{65,1},{129,65},{193,129... | collective-permute-start | bytes 393224 | tf_op jit(solution)/shard_map/ppermute | solution.py:287
  71.2 9.3 %collective-permute-start.9 = (f32[256,128]{1,0:T(8,128)S(1)}, f32[256,128]{1,0:T(8,128)S(1)}, u32[]{:S(2)}, u32[]{:S(2)}) collective-permute-start(f32[256,128]{1,0:T(8,128)S(1)} %get-tuple-element.46), channel_id=1, source_target_pairs={{0,128},{64,192},{128,0},{192,64},{1,129},{65,193},{129,1},{193,65... | collective-permute-start | bytes 393224 | tf_op jit(solution)/shard_map/ppermute | solution.py:287
  80.7 6.1 %collective-permute-start.12 = (bf16[256,128]{1,0:T(8,128)(2,1)S(1)}, bf16[256,128]{1,0:T(8,128)(2,1)S(1)}, u32[]{:S(2)}, u32[]{:S(2)}) collective-permute-start(bf16[256,128]{1,0:T(8,128)(2,1)S(1)} %get-tuple-element.56), channel_id=1, source_target_pairs={{0,128},{64,192},{128,0},{192,64},{1,129},{65,193},{129,1},{193,65... | collective-permute-start | bytes 196616 | tf_op jit(solution)/shard_map/ppermute | solution.py:298
  81.5 5.9 %collective-permute-start.11 = (bf16[256,128]{1,0:T(8,128)(2,1)S(1)}, bf16[256,128]{1,0:T(8,128)(2,1)S(1)}, u32[]{:S(2)}, u32[]{:S(2)}) collective-permute-start(bf16[256,128]{1,0:T(8,128)(2,1)S(1)} %get-tuple-element.56), channel_id=1, source_target_pairs={{0,192},{64,0},{128,64},{192,128},{1,193},{65,1},{129,65},{193,129... | collective-permute-start | bytes 196616 | tf_op jit(solution)/shard_map/ppermute | solution.py:298
  82.3 5.2 %collective-permute-start.13 = (bf16[256,128]{1,0:T(8,128)(2,1)S(1)}, bf16[256,128]{1,0:T(8,128)(2,1)S(1)}, u32[]{:S(2)}, u32[]{:S(2)}) collective-permute-start(bf16[256,128]{1,0:T(8,128)(2,1)S(1)} %get-tuple-element.56), channel_id=1, source_target_pairs={{0,64},{64,128},{128,192},{192,0},{1,65},{65,129},{129,193},{193,1... | collective-permute-start | bytes 196616 | tf_op jit(solution)/shard_map/ppermute | solution.py:298
  87.5 6.5 %collective-permute-start.15 = (bf16[4,256,128]{2,1,0:T(8,128)(2,1)S(1)}, bf16[4,256,128]{2,1,0:T(8,128)(2,1)S(1)}, u32[]{:S(2)}, u32[]{:S(2)}) collective-permute-start(bf16[4,256,128]{2,1,0:T(8,128)(2,1)S(1)} %get-tuple-element.50.mine), channel_id=1, source_target_pairs={{0,56},{8,0},{16,8},{24,16},{32,24},{40,32},{48,40},{56,48},{1,57}... | collective-permute-start | bytes 786440 | tf_op jit(solution)/shard_map/ppermute | solution.py:223
  87.8 7.6 %collective-permute-start.14 = (bf16[4,256,128]{2,1,0:T(8,128)(2,1)S(1)}, bf16[4,256,128]{2,1,0:T(8,128)(2,1)S(1)}, u32[]{:S(2)}, u32[]{:S(2)}) collective-permute-start(bf16[4,256,128]{2,1,0:T(8,128)(2,1)S(1)} %get-tuple-element.50.mine), channel_id=1, source_target_pairs={{0,8},{8,16},{16,24},{24,32},{32,40},{40,48},{48,56},{56,0},{1,9},... | collective-permute-start | bytes 786440 | tf_op jit(solution)/shard_map/ppermute | solution.py:222
  93.5 2.8 %collective-permute-start.17 = (f32[8,27,8,128]{3,2,1,0:T(8,128)}, f32[8,27,8,128]{3,2,1,0:T(8,128)S(1)}, u32[]{:S(2)}, u32[]{:S(2)}) collective-permute-start(f32[8,27,8,128]{3,2,1,0:T(8,128)} %get-tuple-element.25), channel_id=1, source_target_pairs={{0,4},{4,0},{1,5},{5,1},{2,6},{6,2},{3,7},{7,3},{8,12},{12,8},{9,1... | collective-permute-start | bytes 2654216 | tf_op jit(solution)/shard_map/ppermute | solution.py:305
  96.3 2.1 %collective-permute-start.16 = (bf16[2,4,256,128]{3,2,1,0:T(8,128)(2,1)}, bf16[2,4,256,128]{3,2,1,0:T(8,128)(2,1)S(1)}, u32[]{:S(2)}, u32[]{:S(2)}) collective-permute-start(bf16[2,4,256,128]{3,2,1,0:T(8,128)(2,1)} %pad_maximum_fusion.1), channel_id=1, source_target_pairs={{0,4},{4,0},{1,5},{5,1},{2,6},{6,2},{3,7},{7,3},{8,12},{12,8},{9,1... | collective-permute-start | bytes 1572872 | tf_op jit(solution)/shard_map/ppermute | solution.py:225
  98.4 0.8 copy-start.6
  106.5 2.6 %collective-permute-start.18 = (f32[8,27,8,128]{3,2,1,0:T(8,128)}, f32[8,27,8,128]{3,2,1,0:T(8,128)S(1)}, u32[]{:S(2)}, u32[]{:S(2)}) collective-permute-start(f32[8,27,8,128]{3,2,1,0:T(8,128)} %get-tuple-element.33), channel_id=1, source_target_pairs={{0,4},{4,0},{1,5},{5,1},{2,6},{6,2},{3,7},{7,3},{8,12},{12,8},{9,1... | collective-permute-start | bytes 2654216 | tf_op jit(solution)/shard_map/ppermute | solution.py:305
  111.3 23.6 %all-to-all-start = ((bf16[8,240,128]{2,1,0:T(8,128)(2,1)}), bf16[8,240,128]{2,1,0:T(8,128)(2,1)S(1)}, u32[]{:S(2)}, u32[]{:S(2)}) async-start(bf16[8,240,128]{2,1,0:T(8,128)(2,1)} %maximum_bitcast_fusion), calls=%async_computation | async-start | bytes 983040 | tf_op jit(solution)/shard_map/all_to_all | solution.py:327
  124.2 22.0 %collective-permute-start.22 = (f32[256,128]{1,0:T(8,128)S(1)}, f32[256,128]{1,0:T(8,128)S(1)}, u32[]{:S(2)}, u32[]{:S(2)}) collective-permute-start(f32[256,128]{1,0:T(8,128)S(1)} %get-tuple-element.40), channel_id=1, source_target_pairs={{0,192},{1,0},{2,64},{3,128},{64,193},{65,1},{66,65},{67,129},{128... | collective-permute-start | bytes 393224 | tf_op jit(solution)/shard_map/ppermute | solution.py:213
  125.3 21.0 %collective-permute-start.21 = (f32[256,128]{1,0:T(8,128)S(1)}, f32[256,128]{1,0:T(8,128)S(1)}, u32[]{:S(2)}, u32[]{:S(2)}) collective-permute-start(f32[256,128]{1,0:T(8,128)S(1)} %get-tuple-element.41), channel_id=1, source_target_pairs={{0,128},{1,192},{2,0},{3,64},{64,129},{65,193},{66,1},{67,65},{128... | collective-permute-start | bytes 393224 | tf_op jit(solution)/shard_map/ppermute | solution.py:213
  127.3 18.9 %collective-permute-start.20 = (f32[256,128]{1,0:T(8,128)S(1)}, f32[256,128]{1,0:T(8,128)S(1)}, u32[]{:S(2)}, u32[]{:S(2)}) collective-permute-start(f32[256,128]{1,0:T(8,128)S(1)} %get-tuple-element.42), channel_id=1, source_target_pairs={{0,64},{1,128},{2,192},{3,0},{64,65},{65,129},{66,193},{67,1},{128... | collective-permute-start | bytes 393224 | tf_op jit(solution)/shard_map/ppermute | solution.py:213
  131.9 14.4 %collective-permute-start.19 = (f32[256,128]{1,0:T(8,128)S(1)}, f32[256,128]{1,0:T(8,128)S(1)}, u32[]{:S(2)}, u32[]{:S(2)}) collective-permute-start(f32[256,128]{1,0:T(8,128)S(1)} %get-tuple-element.43), channel_id=1, source_target_pairs={{0,65},{1,64},{2,128},{3,192},{64,1},{65,130},{66,129},{67,193},{1... | collective-permute-start | bytes 393224 | tf_op jit(solution)/shard_map/ppermute | solution.py:213
  135.0 11.2 %collective-permute-start.23 = (f32[27,8,128]{2,1,0:T(8,128)S(1)}, f32[27,8,128]{2,1,0:T(8,128)S(1)}, u32[]{:S(2)}, u32[]{:S(2)}) collective-permute-start(f32[27,8,128]{2,1,0:T(8,128)S(1)} %slice_bitcast_fusion.8), channel_id=1, source_target_pairs={{0,65},{1,64},{2,128},{3,192},{64,1},{65,130},{66,129},{67,193},{1... | collective-permute-start | bytes 331784 | tf_op jit(solution)/shard_map/ppermute | solution.py:213
Sparse Core Ops, SparseCore 0:
  17.2 43.0 all-gather.1
  106.9 36.8 reduce-scatter.1

commit v5 on v4

--- a/solution.py
+++ b/solution.py
@@ -10,7 +10,6 @@
 STEPS = (1, 2, -1, -2)
 SPACE = ("x", "z", "core")
 CELLS = 224
-EARLY = 24
 BF = jnp.bfloat16
 F32 = jnp.float32
 
@@ -305,9 +304,8 @@
         return keep + lax.ppermute(send, "core", [(0, 1), (1, 0)])
 
     first_mine = both_cores(keep1, send1)
-    first_early = first_mine[:, :EARLY]
-    first_sum = lax.psum_scatter(first_early, "z", scatter_dimension=0, tiled=True).reshape(EARLY, 8, 128)
-    before, after, other, _ = lax.optimization_barrier((*spread_out(along), first_early))
+    first_sum = lax.psum_scatter(first_mine, "z", scatter_dimension=0, tiled=True).reshape(27, 8, 128)
+    before, after, other, _ = lax.optimization_barrier((*spread_out(along), first_mine))
     keep2, send2, q_hidden = call(
         weigh_second,
         [pieces, pieces, columns],
@@ -321,8 +319,7 @@
         own,
         *consts,
     )
-    second_mine = jnp.concatenate([both_cores(keep2, send2).astype(BF), first_mine[:, EARLY:].astype(BF)], 1)
-    second_mine = second_mine.reshape(8, -1, 128)
+    second_mine = both_cores(keep2, send2).astype(BF).reshape(8, 216, 128)
     q_hidden, second_mine = lax.optimization_barrier((q_hidden, second_mine))
     moved = lax.all_to_all(second_mine, "z", 0, 0, tiled=True)
     (reduced,) = call(
@@ -340,10 +337,10 @@
         *consts,
     )
     parts = [turn_over(reduced[r], lambda a, b: (b + r, a)) for r in range(4)]
-    sums = jnp.sum(moved.astype(F32), axis=0).reshape(-1, 8, 128)
-    second_sum = settled(*turn_over(sums[:27], lambda a, b: (b, a)))
-    first_sum = jnp.concatenate([first_sum, sums[27:]], 0)
+    second_sum = jnp.sum(moved.astype(F32), axis=0).reshape(27, 8, 128)
+    turned_sum = settled(*turn_over(second_sum, lambda a, b: (b, a)))
     *came, _ = lax.optimization_barrier((*(part[1] for part in parts), second_sum))
+    second_sum = turned_sum
     total = settled(parts[0][0], came[0]) + came[1] + came[2] + came[3]
     output = (active * total[0:128]).astype(BF)
     features_grad = (active * total[128:256]).astype(BF)

time: 158 us -> 153 us (0.968); the launches traced: 155 us -> 153 us
  waiting for transfers between devices: 51.8 us -> 49.4 us
  starting transfers between devices: 41.9 us -> 44.1 us
    reduce_scatter x1 -> x0, waiting for transfers between devices: 6.4 us -> none  [on_device(): lax.psum_scatter(first_early, 'z', scatter_dimension=0, tiled=True)]
    ppermute x10, waiting for transfers between devices: 13.9 us -> 20.3 us  [turn_over(): lax.ppermute(value, ('x', 'chan'), [(p[0] * 4 + p[1], q[0] * 4 + q[1]) fo...]
    ppermute x10, starting transfers between devices: 20.7 us -> 22.8 us  [turn_over(): lax.ppermute(value, ('x', 'chan'), [(p[0] * 4 + p[1], q[0] * 4 + q[1]) fo...]
    all_to_all x1, waiting for transfers between devices: 2.09 us -> 0.02 us  [on_device(): moved = lax.all_to_all(second_mine, 'z', 0, 0, tiled=True)]
  transfers between devices with their start and end apart: 27 -> 27, of which waited for: 17 -> 18; matrix products, arithmetic and copies ran while one was open for 7% -> 7% of each run, Pallas kernels for 13% -> 13%
where the time goes in v5:
time: 153 us
  waiting for transfers between devices  49.4 us (32%)
  starting transfers between devices  44.1 us (29%)
  Pallas kernels  31.4 us (21%)
  between operations  14.3 us (9%)
  other arithmetic  9.8 us (6%)
  local copies, waits for them, and re-layouts  3.69 us (2%)
    pallas_call x5, Pallas kernels, call(): pl.pallas_call(kernel, out_shape=outs, in_specs=[smem if value.dtype == j...  31.4 us
    ppermute x10, starting transfers between devices, turn_over(): lax.ppermute(value, ('x', 'chan'), [(p[0] * 4 + p[1], q[0] * 4 + q[1]) fo...  22.8 us
    ppermute x10, waiting for transfers between devices, turn_over(): lax.ppermute(value, ('x', 'chan'), [(p[0] * 4 + p[1], q[0] * 4 + q[1]) fo...  20.3 us
    ppermute x2, waiting for transfers between devices, spread_out(): after = lax.ppermute(mine, 'z', [(i, (i - 1) % 8) for i in range(8)])  7.93 us
    ppermute x3, waiting for transfers between devices, on_device(): lax.ppermute(partial[r], 'x', [(a, (a + r) % 4) for a in range(4)])  7.73 us
    ppermute x2, starting transfers between devices, spread_out(): after = lax.ppermute(mine, 'z', [(i, (i - 1) % 8) for i in range(8)])  6.28 us
    ppermute x2, waiting for transfers between devices, spread_out(): before = lax.ppermute(mine, 'z', [(i, (i + 1) % 8) for i in range(8)])  5.56 us
    ppermute x3, starting transfers between devices, on_device(): lax.ppermute(partial[r], 'x', [(a, (a + r) % 4) for a in range(4)])  5.3 us
  transfers between devices with their start and end apart: 27, of which 18 were waited for; matrix products, arithmetic and copies ran while one was open for 7% of the time, Pallas kernels for 13%

profile of v5, /device:TPU:6, one launch (start us, length us, event | category | flops | bytes accessed | tf_op | source)
XLA Modules:
  0.0 152.7 jit_solution(4176992746883455278)
XLA Ops:
  7.2 3.0 %collective-permute-start.7 = (bf16[8,27,128]{2,0,1:T(8,128)(2,1)}, bf16[8,27,128]{2,0,1:T(8,128)(2,1)S(1)}, u32[]{:S(2)}, u32[]{:S(2)}) collective-permute-start(bf16[8,27,128]{2,0,1:T(8,128)(2,1)} %param.23), channel_id=1, source_target_pairs={{0,65},{1,64},{2,128},{3,192},{64,1},{65,130},{66,129},{67,193},{1... | collective-permute-start | bytes 165896 | tf_op jit(solution)/shard_map/ppermute | solution.py:212
  10.2 5.4 %collective-permute-done.7 = bf16[8,27,128]{2,0,1:T(8,128)(2,1)S(1)} collective-permute-done((bf16[8,27,128]{2,0,1:T(8,128)(2,1)}, bf16[8,27,128]{2,0,1:T(8,128)(2,1)S(1)}, u32[]{:S(2)}, u32[]{:S(2)}) %collective-permute-start.7) | collective-permute-done | bytes 55328 | tf_op jit(solution)/shard_map/ppermute | solution.py:212
  15.6 1.5 pad_maximum_fusion.4
  17.1 0.0 reduce-scatter.4.cloned.1.call-start
  17.1 0.7 convert_element_type.53
  17.8 0.8 fusion.27
  18.6 0.8 fusion.22
  19.5 0.9 multiply_convert_fusion.1
  20.4 3.0 %collective-permute-start = (bf16[288,128]{1,0:T(8,128)(2,1)S(1)}, bf16[288,128]{1,0:T(8,128)(2,1)S(1)}, u32[]{:S(2)}, u32[]{:S(2)}) collective-permute-start(bf16[288,128]{1,0:T(8,128)(2,1)S(1)} %pad_maximum_fusion.5), channel_id=1, source_target_pairs={{0,65},{1,64},{2,128},{3,192},{64,1},{65,130},{66,129},{67,193},{1... | collective-permute-start | bytes 221192 | tf_op jit(solution)/shard_map/ppermute | solution.py:212
  23.5 3.1 %collective-permute-start.1 = (bf16[288,128]{1,0:T(8,128)(2,1)S(1)}, bf16[288,128]{1,0:T(8,128)(2,1)S(1)}, u32[]{:S(2)}, u32[]{:S(2)}) collective-permute-start(bf16[288,128]{1,0:T(8,128)(2,1)S(1)} %pad_maximum_fusion.5), channel_id=1, source_target_pairs={{0,3},{1,67},{2,131},{3,195},{64,0},{65,64},{66,128},{67,192},{128... | collective-permute-start | bytes 221192 | tf_op jit(solution)/shard_map/ppermute | solution.py:212
  26.6 0.6 collective-permute-start.3
  27.1 7.2 %collective-permute-done = bf16[288,128]{1,0:T(8,128)(2,1)S(1)} collective-permute-done((bf16[288,128]{1,0:T(8,128)(2,1)S(1)}, bf16[288,128]{1,0:T(8,128)(2,1)S(1)}, u32[]{:S(2)}, u32[]{:S(2)}) %collective-permute-start) | collective-permute-done | bytes 73760 | tf_op jit(solution)/shard_map/ppermute | solution.py:212
  34.4 0.5 collective-permute-done.3
  34.9 0.1 fusion.31
  34.9 5.9 %collective-permute-start.5 = (bf16[4,288,128]{2,1,0:T(8,128)(2,1)S(1)}, bf16[4,288,128]{2,1,0:T(8,128)(2,1)S(1)}, u32[]{:S(2)}, u32[]{:S(2)}) collective-permute-start(bf16[4,288,128]{2,1,0:T(8,128)(2,1)S(1)} %get-tuple-element.48.mine), channel_id=1, source_target_pairs={{0,56},{8,0},{16,8},{24,16},{32,24},{40,32},{48,40},{56,48},{1,57}... | collective-permute-start | bytes 884744 | tf_op jit(solution)/shard_map/ppermute | solution.py:222
  40.9 7.5 %collective-permute-done.5.after = bf16[4,288,128]{2,1,0:T(8,128)(2,1)S(1)} collective-permute-done((bf16[4,288,128]{2,1,0:T(8,128)(2,1)S(1)}, bf16[4,288,128]{2,1,0:T(8,128)(2,1)S(1)}, u32[]{:S(2)}, u32[]{:S(2)}) %collective-permute-start.5) | collective-permute-done | bytes 294944 | tf_op jit(solution)/shard_map/ppermute | solution.py:222
  48.4 4.1 %collective-permute-done.4.before = bf16[4,288,128]{2,1,0:T(8,128)(2,1)S(1)} collective-permute-done((bf16[4,288,128]{2,1,0:T(8,128)(2,1)S(1)}, bf16[4,288,128]{2,1,0:T(8,128)(2,1)S(1)}, u32[]{:S(2)}, u32[]{:S(2)}) %collective-permute-start.4) | collective-permute-done | bytes 294944 | tf_op jit(solution)/shard_map/ppermute | solution.py:221
  52.5 0.1 pad_maximum_fusion
  52.6 0.1 collective-permute-start.6
  52.7 0.1 stack.88.ids
  52.8 1.9 %collective-permute-done.6.other = bf16[2,4,288,128]{3,2,1,0:T(8,128)(2,1)S(1)} collective-permute-done((bf16[2,4,288,128]{3,2,1,0:T(8,128)(2,1)S(1)}, bf16[2,4,288,128]{3,2,1,0:T(8,128)(2,1)S(1)}, u32[]{:S(2)}, u32[]{:S(2)}) %collective-permute-start.6) | collective-permute-done | bytes 589856 | tf_op jit(solution)/shard_map/ppermute | solution.py:224
  54.7 0.8 copy-done.7
  55.5 7.4 %shard_map.210 = (bf16[8,9,96,128]{3,2,1,0:T(8,128)(2,1)}, bf16[8,9,96,128]{3,2,1,0:T(8,128)(2,1)}, bf16[4,128,128]{2,1,0:T(8,128)(2,1)S(1)}, bf16[4,32,128]{2,1,0:T(8,128)(2,1)S(1)}) custom-call(s32[5]{0:T(128)S(1)} %stack.88.ids, bf16[4,288,128]{2,1,0:T(8,128)(2,1)S(1)} %get-tuple-element.48.mine, bf16[4,288,128]{2,1,0:T(8,128)(2,1)S(1)} %collective-permute-done.4.before, ...), custom_call_target="tpu_custom_call" | custom-call | tf_op jit(solution)/shard_map/pallas_call | solution.py:196
  62.9 4.5 %shard_map.211 = f32[4,256,128]{2,1,0:T(8,128)S(1)} custom-call(s32[5]{0:T(128)S(1)} %stack.88.ids, bf16[8,9,96,128]{3,2,1,0:T(8,128)(2,1)} %get-tuple-element.22.q_in, bf16[8,9,96,128]{3,2,1,0:T(8,128)(2,1)} %get-tuple-element.23.q_back, bf16[2,27,128,128]{3,2,1,0:T(8,128)(2,1)} %bitcast.66), custom_call_target="tpu_custom_call" | custom-call | tf_op jit(solution)/shard_map/pallas_call | solution.py:196
  67.5 3.8 %collective-permute-start.8 = (f32[256,128]{1,0:T(8,128)S(1)}, f32[256,128]{1,0:T(8,128)S(1)}, u32[]{:S(2)}, u32[]{:S(2)}) collective-permute-start(f32[256,128]{1,0:T(8,128)S(1)} %get-tuple-element.44), channel_id=1, source_target_pairs={{0,64},{64,128},{128,192},{192,0},{1,65},{65,129},{129,193},{193,1... | collective-permute-start | bytes 393224 | tf_op jit(solution)/shard_map/ppermute | solution.py:286
  71.2 1.6 %collective-permute-start.9 = (f32[256,128]{1,0:T(8,128)S(1)}, f32[256,128]{1,0:T(8,128)S(1)}, u32[]{:S(2)}, u32[]{:S(2)}) collective-permute-start(f32[256,128]{1,0:T(8,128)S(1)} %get-tuple-element.46), channel_id=1, source_target_pairs={{0,128},{64,192},{128,0},{192,64},{1,129},{65,193},{129,1},{193,65... | collective-permute-start | bytes 393224 | tf_op jit(solution)/shard_map/ppermute | solution.py:286
  72.8 1.5 collective-permute-done.8
  74.3 6.2 %collective-permute-done.10 = f32[256,128]{1,0:T(8,128)S(1)} collective-permute-done((f32[256,128]{1,0:T(8,128)S(1)}, f32[256,128]{1,0:T(8,128)S(1)}, u32[]{:S(2)}, u32[]{:S(2)}) %collective-permute-start.10) | collective-permute-done | bytes 131104 | tf_op jit(solution)/shard_map/ppermute | solution.py:286
  80.6 0.1 multiply_convert_fusion
  80.7 0.8 collective-permute-start.12
  81.5 0.7 collective-permute-start.11
  82.3 2.5 %collective-permute-start.13 = (bf16[256,128]{1,0:T(8,128)(2,1)S(1)}, bf16[256,128]{1,0:T(8,128)(2,1)S(1)}, u32[]{:S(2)}, u32[]{:S(2)}) collective-permute-start(bf16[256,128]{1,0:T(8,128)(2,1)S(1)} %get-tuple-element.56), channel_id=1, source_target_pairs={{0,64},{64,128},{128,192},{192,0},{1,65},{65,129},{129,193},{193,1... | collective-permute-start | bytes 196616 | tf_op jit(solution)/shard_map/ppermute | solution.py:297
  84.8 2.0 %collective-permute-done.12 = bf16[256,128]{1,0:T(8,128)(2,1)S(1)} collective-permute-done((bf16[256,128]{1,0:T(8,128)(2,1)S(1)}, bf16[256,128]{1,0:T(8,128)(2,1)S(1)}, u32[]{:S(2)}, u32[]{:S(2)}) %collective-permute-start.12) | collective-permute-done | bytes 65568 | tf_op jit(solution)/shard_map/ppermute | solution.py:297
  86.8 0.7 collective-permute-done.11
  87.5 0.4 collective-permute-start.15
  87.8 1.8 %collective-permute-start.14 = (bf16[4,256,128]{2,1,0:T(8,128)(2,1)S(1)}, bf16[4,256,128]{2,1,0:T(8,128)(2,1)S(1)}, u32[]{:S(2)}, u32[]{:S(2)}) collective-permute-start(bf16[4,256,128]{2,1,0:T(8,128)(2,1)S(1)} %get-tuple-element.50.mine), channel_id=1, source_target_pairs={{0,8},{8,16},{16,24},{24,32},{32,40},{40,48},{48,56},{56,0},{1,9},... | collective-permute-start | bytes 786440 | tf_op jit(solution)/shard_map/ppermute | solution.py:221
  89.6 3.9 %shard_map.212 = (f32[8,27,8,128]{3,2,1,0:T(8,128)S(1)}, f32[8,27,8,128]{3,2,1,0:T(8,128)}) custom-call(s32[5]{0:T(128)S(1)} %stack.88.ids, bf16[4,256,128]{2,1,0:T(8,128)(2,1)S(1)} %get-tuple-element.50.mine, bf16[8,9,96,128]{3,2,1,0:T(8,128)(2,1)} %get-tuple-element.22.q_in), custom_call_target="tpu_custom_call" | custom-call | tf_op jit(solution)/shard_map/pallas_call | solution.py:196
  93.5 0.4 collective-permute-done.15.after
  93.9 1.5 collective-permute-done.14.before
  95.5 0.1 pad_maximum_fusion.1
  95.5 0.1 collective-permute-start.16
  95.6 0.6 collective-permute-done.17
  96.2 1.0 add.67
  97.2 0.3 collective-permute-done.16.other
  97.5 0.8 copy-done.6
  98.3 7.3 %shard_map.213 = (f32[8,27,8,128]{3,2,1,0:T(8,128)}, f32[8,27,8,128]{3,2,1,0:T(8,128)}, bf16[8,9,96,128]{3,2,1,0:T(8,128)(2,1)}) custom-call(s32[5]{0:T(128)S(1)} %stack.88.ids, bf16[4,256,128]{2,1,0:T(8,128)(2,1)S(1)} %get-tuple-element.50.mine, bf16[4,256,128]{2,1,0:T(8,128)(2,1)S(1)} %collective-permute-done.14.before, ...), custom_call_target="tpu_custom_call" | custom-call | tf_op jit(solution)/shard_map/pallas_call | solution.py:196
  105.6 0.1 collective-permute-start.18
  105.8 2.5 %collective-permute-done.18 = f32[8,27,8,128]{3,2,1,0:T(8,128)S(1)} collective-permute-done((f32[8,27,8,128]{3,2,1,0:T(8,128)}, f32[8,27,8,128]{3,2,1,0:T(8,128)S(1)}, u32[]{:S(2)}, u32[]{:S(2)}) %collective-permute-start.18) | collective-permute-done | bytes 884768 | tf_op jit(solution)/shard_map/ppermute | solution.py:304
  108.2 2.1 %fusion = bf16[8,216,128]{2,1,0:T(8,128)(2,1)} fusion(f32[8,27,8,128]{3,2,1,0:T(8,128)} %get-tuple-element.32, f32[8,27,8,128]{3,2,1,0:T(8,128)S(1)} %collective-permute-done.18), kind=kLoop, calls=%fused_computation.4 | loop fusion | flops 442368 | bytes 2211840 | tf_op jit(solution)/shard_map/reshape | solution.py:322
  110.3 3.5 %all-to-all-start = ((bf16[8,216,128]{2,1,0:T(8,128)(2,1)}), bf16[8,216,128]{2,1,0:T(8,128)(2,1)S(1)}, u32[]{:S(2)}, u32[]{:S(2)}) async-start(bf16[8,216,128]{2,1,0:T(8,128)(2,1)} %fusion), calls=%async_computation | async-start | bytes 884736 | tf_op jit(solution)/shard_map/all_to_all | solution.py:324
  113.8 8.2 %shard_map.214 = f32[4,256,128]{2,1,0:T(8,128)} custom-call(s32[5]{0:T(128)S(1)} %stack.88.ids, bf16[4,256,128]{2,1,0:T(8,128)(2,1)S(1)} %get-tuple-element.50.mine, bf16[4,256,128]{2,1,0:T(8,128)(2,1)S(1)} %collective-permute-done.14.before, bf16[4,256,128]{2,1,0:T(8,128)(2,1)S(1)} %collective-permute-done.15.after, bf16[2,4,256,128]{3,2,1,0:T(8,128)(2,1)} %copy-done.6, ...), custom_call_target="tpu_custom_call" | custom-call | tf_op jit(solution)/shard_map/pallas_call | solution.py:196
  122.0 1.1 slice_bitcast_fusion
  123.1 1.1 collective-permute-start.22
  124.2 2.0 %collective-permute-start.21 = (f32[256,128]{1,0:T(8,128)S(1)}, f32[256,128]{1,0:T(8,128)S(1)}, u32[]{:S(2)}, u32[]{:S(2)}) collective-permute-start(f32[256,128]{1,0:T(8,128)S(1)} %get-tuple-element.41), channel_id=1, source_target_pairs={{0,128},{1,192},{2,0},{3,64},{64,129},{65,193},{66,1},{67,65},{128... | collective-permute-start | bytes 393224 | tf_op jit(solution)/shard_map/ppermute | solution.py:212
  126.3 4.6 %collective-permute-start.20 = (f32[256,128]{1,0:T(8,128)S(1)}, f32[256,128]{1,0:T(8,128)S(1)}, u32[]{:S(2)}, u32[]{:S(2)}) collective-permute-start(f32[256,128]{1,0:T(8,128)S(1)} %get-tuple-element.42), channel_id=1, source_target_pairs={{0,64},{1,128},{2,192},{3,0},{64,65},{65,129},{66,193},{67,1},{128... | collective-permute-start | bytes 393224 | tf_op jit(solution)/shard_map/ppermute | solution.py:212
  130.8 1.0 collective-permute-start.19
  131.8 0.1 convert_reduce_fusion
  131.9 4.4 %collective-permute-start.23 = (f32[27,8,128]{2,1,0:T(8,128)S(1)}, f32[27,8,128]{2,1,0:T(8,128)S(1)}, u32[]{:S(2)}, u32[]{:S(2)}) collective-permute-start(f32[27,8,128]{2,1,0:T(8,128)S(1)} %bitcast.68), channel_id=1, source_target_pairs={{0,65},{1,64},{2,128},{3,192},{64,1},{65,130},{66,129},{67,193},{1... | collective-permute-start | bytes 331784 | tf_op jit(solution)/shard_map/ppermute | solution.py:212
  136.3 2.4 %collective-permute-done.20 = f32[256,128]{1,0:T(8,128)S(1)} collective-permute-done((f32[256,128]{1,0:T(8,128)S(1)}, f32[256,128]{1,0:T(8,128)S(1)}, u32[]{:S(2)}, u32[]{:S(2)}) %collective-permute-start.20) | collective-permute-done | bytes 131104 | tf_op jit(solution)/shard_map/ppermute | solution.py:212
  138.7 4.6 %collective-permute-done.19 = f32[256,128]{1,0:T(8,128)S(1)} collective-permute-done((f32[256,128]{1,0:T(8,128)S(1)}, f32[256,128]{1,0:T(8,128)S(1)}, u32[]{:S(2)}, u32[]{:S(2)}) %collective-permute-start.19) | collective-permute-done | bytes 131104 | tf_op jit(solution)/shard_map/ppermute | solution.py:212
  143.4 0.9 add_add_fusion
  144.3 0.7 fusion.4
  145.0 0.2 collective-permute-done.23
  145.2 0.7 select_bitcast_fusion.2
  (40 shorter events, 0.4 us)
Async XLA Ops:
  7.2 55.8 %all-gather.2.cloned.1.call-start = ((), (), s32[]{:S(2)}) async-start(), calls=%async_computation.2 | async-start | bytes 1880064 | tf_op jit(solution)/shard_map/all_gather | solution.py:238
  7.2 8.4 %collective-permute-start.7 = (bf16[8,27,128]{2,0,1:T(8,128)(2,1)}, bf16[8,27,128]{2,0,1:T(8,128)(2,1)S(1)}, u32[]{:S(2)}, u32[]{:S(2)}) collective-permute-start(bf16[8,27,128]{2,0,1:T(8,128)(2,1)} %param.23), channel_id=1, source_target_pairs={{0,65},{1,64},{2,128},{3,192},{64,1},{65,130},{66,129},{67,193},{1... | collective-permute-start | bytes 165896 | tf_op jit(solution)/shard_map/ppermute | solution.py:212
  17.1 128.8 %reduce-scatter.4.cloned.1.call-start = ((), (), s32[]{:S(2)}) async-start(), calls=%async_computation.3 | async-start | bytes 995328
  19.4 36.1 %copy-start = (bf16[864,224]{1,0:T(8,128)(2,1)S(1)}, bf16[864,224]{1,0:T(8,128)(2,1)}, u32[]{:S(2)}) copy-start(bf16[864,224]{1,0:T(8,128)(2,1)} %constant.72.clone.spread) | copy-start | bytes 1161220
  19.4 36.1 %copy-start.1 = (bf16[32,2048]{1,0:T(8,128)(2,1)S(1)}, bf16[32,2048]{1,0:T(8,128)(2,1)}, u32[]{:S(2)}) copy-start(bf16[32,2048]{1,0:T(8,128)(2,1)} %constant.73.clone.lanes) | copy-start | bytes 393220
  19.4 36.1 %copy-start.2 = (f32[224,128]{1,0:T(8,128)S(1)}, f32[224,128]{1,0:T(8,128)}, u32[]{:S(2)}) copy-start(f32[224,128]{1,0:T(8,128)} %constant.71.clone.local) | copy-start | bytes 344068
  19.4 36.1 %copy-start.3 = (bf16[224,32]{1,0:T(8,128)(2,1)S(1)}, bf16[224,32]{1,0:T(8,128)(2,1)}, u32[]{:S(2)}) copy-start(bf16[224,32]{1,0:T(8,128)(2,1)} %constant.70.clone.pick_back) | copy-start | bytes 43012
  19.5 36.1 %copy-start.4 = (bf16[224,32]{1,0:T(8,128)(2,1)S(1)}, bf16[224,32]{1,0:T(8,128)(2,1)}, u32[]{:S(2)}) copy-start(bf16[224,32]{1,0:T(8,128)(2,1)} %constant.69.clone.pick) | copy-start | bytes 43012
  19.5 36.1 %copy-start.5 = (bf16[16,128]{1,0:T(8,128)(2,1)S(1)}, bf16[16,128]{1,0:T(8,128)(2,1)}, u32[]{:S(2)}) copy-start(bf16[16,128]{1,0:T(8,128)(2,1)} %constant.74.clone.sources) | copy-start | bytes 12292
  20.4 13.9 %collective-permute-start = (bf16[288,128]{1,0:T(8,128)(2,1)S(1)}, bf16[288,128]{1,0:T(8,128)(2,1)S(1)}, u32[]{:S(2)}, u32[]{:S(2)}) collective-permute-start(bf16[288,128]{1,0:T(8,128)(2,1)S(1)} %pad_maximum_fusion.5), channel_id=1, source_target_pairs={{0,65},{1,64},{2,128},{3,192},{64,1},{65,130},{66,129},{67,193},{1... | collective-permute-start | bytes 221192 | tf_op jit(solution)/shard_map/ppermute | solution.py:212
  23.5 10.9 %collective-permute-start.2 = (bf16[288,128]{1,0:T(8,128)(2,1)S(1)}, bf16[288,128]{1,0:T(8,128)(2,1)S(1)}, u32[]{:S(2)}, u32[]{:S(2)}) collective-permute-start(bf16[288,128]{1,0:T(8,128)(2,1)S(1)} %pad_maximum_fusion.5), channel_id=1, source_target_pairs={{0,2},{1,66},{2,130},{3,194},{64,3},{65,67},{66,131},{67,195},{128... | collective-permute-start | bytes 221192 | tf_op jit(solution)/shard_map/ppermute | solution.py:212
  23.5 10.9 %collective-permute-start.1 = (bf16[288,128]{1,0:T(8,128)(2,1)S(1)}, bf16[288,128]{1,0:T(8,128)(2,1)S(1)}, u32[]{:S(2)}, u32[]{:S(2)}) collective-permute-start(bf16[288,128]{1,0:T(8,128)(2,1)S(1)} %pad_maximum_fusion.5), channel_id=1, source_target_pairs={{0,3},{1,67},{2,131},{3,195},{64,0},{65,64},{66,128},{67,192},{128... | collective-permute-start | bytes 221192 | tf_op jit(solution)/shard_map/ppermute | solution.py:212
  26.6 8.3 %collective-permute-start.3 = (bf16[288,128]{1,0:T(8,128)(2,1)S(1)}, bf16[288,128]{1,0:T(8,128)(2,1)S(1)}, u32[]{:S(2)}, u32[]{:S(2)}) collective-permute-start(bf16[288,128]{1,0:T(8,128)(2,1)S(1)} %pad_maximum_fusion.5), channel_id=1, source_target_pairs={{0,1},{1,65},{2,129},{3,193},{64,2},{65,66},{66,130},{67,194},{128... | collective-permute-start | bytes 221192 | tf_op jit(solution)/shard_map/ppermute | solution.py:212
  34.9 13.5 %collective-permute-start.5 = (bf16[4,288,128]{2,1,0:T(8,128)(2,1)S(1)}, bf16[4,288,128]{2,1,0:T(8,128)(2,1)S(1)}, u32[]{:S(2)}, u32[]{:S(2)}) collective-permute-start(bf16[4,288,128]{2,1,0:T(8,128)(2,1)S(1)} %get-tuple-element.48.mine), channel_id=1, source_target_pairs={{0,56},{8,0},{16,8},{24,16},{32,24},{40,32},{48,40},{56,48},{1,57}... | collective-permute-start | bytes 884744 | tf_op jit(solution)/shard_map/ppermute | solution.py:222
  40.9 11.6 %collective-permute-start.4 = (bf16[4,288,128]{2,1,0:T(8,128)(2,1)S(1)}, bf16[4,288,128]{2,1,0:T(8,128)(2,1)S(1)}, u32[]{:S(2)}, u32[]{:S(2)}) collective-permute-start(bf16[4,288,128]{2,1,0:T(8,128)(2,1)S(1)} %get-tuple-element.48.mine), channel_id=1, source_target_pairs={{0,8},{8,16},{16,24},{24,32},{32,40},{40,48},{48,56},{56,0},{1,9},... | collective-permute-start | bytes 884744 | tf_op jit(solution)/shard_map/ppermute | solution.py:221
  52.6 2.1 %collective-permute-start.6 = (bf16[2,4,288,128]{3,2,1,0:T(8,128)(2,1)S(1)}, bf16[2,4,288,128]{3,2,1,0:T(8,128)(2,1)S(1)}, u32[]{:S(2)}, u32[]{:S(2)}) collective-permute-start(bf16[2,4,288,128]{3,2,1,0:T(8,128)(2,1)S(1)} %pad_maximum_fusion), channel_id=1, source_target_pairs={{0,4},{4,0},{1,5},{5,1},{2,6},{6,2},{3,7},{7,3},{8,12},{12,8},{9,1... | collective-permute-start | bytes 1769480 | tf_op jit(solution)/shard_map/ppermute | solution.py:224
  54.7 0.8 copy-start.7
  67.5 6.8 %collective-permute-start.8 = (f32[256,128]{1,0:T(8,128)S(1)}, f32[256,128]{1,0:T(8,128)S(1)}, u32[]{:S(2)}, u32[]{:S(2)}) collective-permute-start(f32[256,128]{1,0:T(8,128)S(1)} %get-tuple-element.44), channel_id=1, source_target_pairs={{0,64},{64,128},{128,192},{192,0},{1,65},{65,129},{129,193},{193,1... | collective-permute-start | bytes 393224 | tf_op jit(solution)/shard_map/ppermute | solution.py:286
  71.2 9.3 %collective-permute-start.10 = (f32[256,128]{1,0:T(8,128)S(1)}, f32[256,128]{1,0:T(8,128)S(1)}, u32[]{:S(2)}, u32[]{:S(2)}) collective-permute-start(f32[256,128]{1,0:T(8,128)S(1)} %get-tuple-element.45), channel_id=1, source_target_pairs={{0,192},{64,0},{128,64},{192,128},{1,193},{65,1},{129,65},{193,129... | collective-permute-start | bytes 393224 | tf_op jit(solution)/shard_map/ppermute | solution.py:286
  71.2 9.3 %collective-permute-start.9 = (f32[256,128]{1,0:T(8,128)S(1)}, f32[256,128]{1,0:T(8,128)S(1)}, u32[]{:S(2)}, u32[]{:S(2)}) collective-permute-start(f32[256,128]{1,0:T(8,128)S(1)} %get-tuple-element.46), channel_id=1, source_target_pairs={{0,128},{64,192},{128,0},{192,64},{1,129},{65,193},{129,1},{193,65... | collective-permute-start | bytes 393224 | tf_op jit(solution)/shard_map/ppermute | solution.py:286
  80.7 6.1 %collective-permute-start.12 = (bf16[256,128]{1,0:T(8,128)(2,1)S(1)}, bf16[256,128]{1,0:T(8,128)(2,1)S(1)}, u32[]{:S(2)}, u32[]{:S(2)}) collective-permute-start(bf16[256,128]{1,0:T(8,128)(2,1)S(1)} %get-tuple-element.56), channel_id=1, source_target_pairs={{0,128},{64,192},{128,0},{192,64},{1,129},{65,193},{129,1},{193,65... | collective-permute-start | bytes 196616 | tf_op jit(solution)/shard_map/ppermute | solution.py:297
  81.5 5.9 %collective-permute-start.11 = (bf16[256,128]{1,0:T(8,128)(2,1)S(1)}, bf16[256,128]{1,0:T(8,128)(2,1)S(1)}, u32[]{:S(2)}, u32[]{:S(2)}) collective-permute-start(bf16[256,128]{1,0:T(8,128)(2,1)S(1)} %get-tuple-element.56), channel_id=1, source_target_pairs={{0,192},{64,0},{128,64},{192,128},{1,193},{65,1},{129,65},{193,129... | collective-permute-start | bytes 196616 | tf_op jit(solution)/shard_map/ppermute | solution.py:297
  82.3 5.2 %collective-permute-start.13 = (bf16[256,128]{1,0:T(8,128)(2,1)S(1)}, bf16[256,128]{1,0:T(8,128)(2,1)S(1)}, u32[]{:S(2)}, u32[]{:S(2)}) collective-permute-start(bf16[256,128]{1,0:T(8,128)(2,1)S(1)} %get-tuple-element.56), channel_id=1, source_target_pairs={{0,64},{64,128},{128,192},{192,0},{1,65},{65,129},{129,193},{193,1... | collective-permute-start | bytes 196616 | tf_op jit(solution)/shard_map/ppermute | solution.py:297
  87.5 6.5 %collective-permute-start.15 = (bf16[4,256,128]{2,1,0:T(8,128)(2,1)S(1)}, bf16[4,256,128]{2,1,0:T(8,128)(2,1)S(1)}, u32[]{:S(2)}, u32[]{:S(2)}) collective-permute-start(bf16[4,256,128]{2,1,0:T(8,128)(2,1)S(1)} %get-tuple-element.50.mine), channel_id=1, source_target_pairs={{0,56},{8,0},{16,8},{24,16},{32,24},{40,32},{48,40},{56,48},{1,57}... | collective-permute-start | bytes 786440 | tf_op jit(solution)/shard_map/ppermute | solution.py:222
  87.8 7.6 %collective-permute-start.14 = (bf16[4,256,128]{2,1,0:T(8,128)(2,1)S(1)}, bf16[4,256,128]{2,1,0:T(8,128)(2,1)S(1)}, u32[]{:S(2)}, u32[]{:S(2)}) collective-permute-start(bf16[4,256,128]{2,1,0:T(8,128)(2,1)S(1)} %get-tuple-element.50.mine), channel_id=1, source_target_pairs={{0,8},{8,16},{16,24},{24,32},{32,40},{40,48},{48,56},{56,0},{1,9},... | collective-permute-start | bytes 786440 | tf_op jit(solution)/shard_map/ppermute | solution.py:221
  93.5 2.6 %collective-permute-start.17 = (f32[8,27,8,128]{3,2,1,0:T(8,128)}, f32[8,27,8,128]{3,2,1,0:T(8,128)S(1)}, u32[]{:S(2)}, u32[]{:S(2)}) collective-permute-start(f32[8,27,8,128]{3,2,1,0:T(8,128)} %get-tuple-element.25), channel_id=1, source_target_pairs={{0,4},{4,0},{1,5},{5,1},{2,6},{6,2},{3,7},{7,3},{8,12},{12,8},{9,1... | collective-permute-start | bytes 2654216 | tf_op jit(solution)/shard_map/ppermute | solution.py:304
  95.5 2.0 %collective-permute-start.16 = (bf16[2,4,256,128]{3,2,1,0:T(8,128)(2,1)S(1)}, bf16[2,4,256,128]{3,2,1,0:T(8,128)(2,1)S(1)}, u32[]{:S(2)}, u32[]{:S(2)}) collective-permute-start(bf16[2,4,256,128]{3,2,1,0:T(8,128)(2,1)S(1)} %pad_maximum_fusion.1), channel_id=1, source_target_pairs={{0,4},{4,0},{1,5},{5,1},{2,6},{6,2},{3,7},{7,3},{8,12},{12,8},{9,1... | collective-permute-start | bytes 1572872 | tf_op jit(solution)/shard_map/ppermute | solution.py:224
  97.5 0.8 copy-start.6
  105.6 2.6 %collective-permute-start.18 = (f32[8,27,8,128]{3,2,1,0:T(8,128)}, f32[8,27,8,128]{3,2,1,0:T(8,128)S(1)}, u32[]{:S(2)}, u32[]{:S(2)}) collective-permute-start(f32[8,27,8,128]{3,2,1,0:T(8,128)} %get-tuple-element.33), channel_id=1, source_target_pairs={{0,4},{4,0},{1,5},{5,1},{2,6},{6,2},{3,7},{7,3},{8,12},{12,8},{9,1... | collective-permute-start | bytes 2654216 | tf_op jit(solution)/shard_map/ppermute | solution.py:304
  110.3 21.5 %all-to-all-start = ((bf16[8,216,128]{2,1,0:T(8,128)(2,1)}), bf16[8,216,128]{2,1,0:T(8,128)(2,1)S(1)}, u32[]{:S(2)}, u32[]{:S(2)}) async-start(bf16[8,216,128]{2,1,0:T(8,128)(2,1)} %fusion), calls=%async_computation | async-start | bytes 884736 | tf_op jit(solution)/shard_map/all_to_all | solution.py:324
  123.1 13.2 %collective-permute-start.22 = (f32[256,128]{1,0:T(8,128)S(1)}, f32[256,128]{1,0:T(8,128)S(1)}, u32[]{:S(2)}, u32[]{:S(2)}) collective-permute-start(f32[256,128]{1,0:T(8,128)S(1)} %get-tuple-element.40), channel_id=1, source_target_pairs={{0,192},{1,0},{2,64},{3,128},{64,193},{65,1},{66,65},{67,129},{128... | collective-permute-start | bytes 393224 | tf_op jit(solution)/shard_map/ppermute | solution.py:212
  124.2 12.1 %collective-permute-start.21 = (f32[256,128]{1,0:T(8,128)S(1)}, f32[256,128]{1,0:T(8,128)S(1)}, u32[]{:S(2)}, u32[]{:S(2)}) collective-permute-start(f32[256,128]{1,0:T(8,128)S(1)} %get-tuple-element.41), channel_id=1, source_target_pairs={{0,128},{1,192},{2,0},{3,64},{64,129},{65,193},{66,1},{67,65},{128... | collective-permute-start | bytes 393224 | tf_op jit(solution)/shard_map/ppermute | solution.py:212
  126.3 12.4 %collective-permute-start.20 = (f32[256,128]{1,0:T(8,128)S(1)}, f32[256,128]{1,0:T(8,128)S(1)}, u32[]{:S(2)}, u32[]{:S(2)}) collective-permute-start(f32[256,128]{1,0:T(8,128)S(1)} %get-tuple-element.42), channel_id=1, source_target_pairs={{0,64},{1,128},{2,192},{3,0},{64,65},{65,129},{66,193},{67,1},{128... | collective-permute-start | bytes 393224 | tf_op jit(solution)/shard_map/ppermute | solution.py:212
  130.8 12.5 %collective-permute-start.19 = (f32[256,128]{1,0:T(8,128)S(1)}, f32[256,128]{1,0:T(8,128)S(1)}, u32[]{:S(2)}, u32[]{:S(2)}) collective-permute-start(f32[256,128]{1,0:T(8,128)S(1)} %get-tuple-element.43), channel_id=1, source_target_pairs={{0,65},{1,64},{2,128},{3,192},{64,1},{65,130},{66,129},{67,193},{1... | collective-permute-start | bytes 393224 | tf_op jit(solution)/shard_map/ppermute | solution.py:212
  131.9 13.3 %collective-permute-start.23 = (f32[27,8,128]{2,1,0:T(8,128)S(1)}, f32[27,8,128]{2,1,0:T(8,128)S(1)}, u32[]{:S(2)}, u32[]{:S(2)}) collective-permute-start(f32[27,8,128]{2,1,0:T(8,128)S(1)} %bitcast.68), channel_id=1, source_target_pairs={{0,65},{1,64},{2,128},{3,192},{64,1},{65,130},{66,129},{67,193},{1... | collective-permute-start | bytes 331784 | tf_op jit(solution)/shard_map/ppermute | solution.py:212
Sparse Core Ops, SparseCore 0:
  17.2 43.0 all-gather.1
  105.9 36.9 reduce-scatter.3

commit v6 on v5

--- a/solution.py
+++ b/solution.py
@@ -158,7 +158,7 @@
     ids, mine, before, after, other, matched, own, pick, pick_back, local, spread, lanes, sources,
     keep, send, q_hidden, scratch,
 ):
-    @pl.loop(0, 4, unroll=2)
+    @pl.loop(0, 4, unroll=4)
     def _(turn):
         at = (ids[0] + turn) & 3
         views = around(ids, mine, before, after, other, turn)

time: 153 us -> 153 us (level)
  no operation moved by 1% of the time
where the time goes in v6:
time: 153 us; the launch traced here: 152 us
  waiting for transfers between devices  49.4 us (32%)
  starting transfers between devices  44.1 us (29%)
  Pallas kernels  30.8 us (20%)
  between operations  14.3 us (9%)
  other arithmetic  9.8 us (6%)
  local copies, waits for them, and re-layouts  3.69 us (2%)
    pallas_call x5, Pallas kernels, call(): pl.pallas_call(kernel, out_shape=outs, in_specs=[smem if value.dtype == j...  30.8 us
    ppermute x10, starting transfers between devices, turn_over(): lax.ppermute(value, ('x', 'chan'), [(p[0] * 4 + p[1], q[0] * 4 + q[1]) fo...  22.8 us
    ppermute x10, waiting for transfers between devices, turn_over(): lax.ppermute(value, ('x', 'chan'), [(p[0] * 4 + p[1], q[0] * 4 + q[1]) fo...  20.2 us
    ppermute x2, waiting for transfers between devices, spread_out(): after = lax.ppermute(mine, 'z', [(i, (i - 1) % 8) for i in range(8)])  7.93 us
    ppermute x3, waiting for transfers between devices, on_device(): lax.ppermute(partial[r], 'x', [(a, (a + r) % 4) for a in range(4)])  7.73 us
    ppermute x2, starting transfers between devices, spread_out(): after = lax.ppermute(mine, 'z', [(i, (i - 1) % 8) for i in range(8)])  6.28 us
    ppermute x2, waiting for transfers between devices, spread_out(): before = lax.ppermute(mine, 'z', [(i, (i + 1) % 8) for i in range(8)])  5.56 us
    ppermute x3, starting transfers between devices, on_device(): lax.ppermute(partial[r], 'x', [(a, (a + r) % 4) for a in range(4)])  5.3 us
  transfers between devices with their start and end apart: 27, of which 18 were waited for; matrix products, arithmetic and copies ran while one was open for 7% of the time, Pallas kernels for 13%

profile of v6, /device:TPU:6, one launch (start us, length us, event | category | flops | bytes accessed | tf_op | source)
XLA Modules:
  0.0 152.1 jit_solution(4028043401747621091)
XLA Ops:
  7.2 3.0 %collective-permute-start.7 = (bf16[8,27,128]{2,0,1:T(8,128)(2,1)}, bf16[8,27,128]{2,0,1:T(8,128)(2,1)S(1)}, u32[]{:S(2)}, u32[]{:S(2)}) collective-permute-start(bf16[8,27,128]{2,0,1:T(8,128)(2,1)} %param.23), channel_id=1, source_target_pairs={{0,65},{1,64},{2,128},{3,192},{64,1},{65,130},{66,129},{67,193},{1... | collective-permute-start | bytes 165896 | tf_op jit(solution)/shard_map/ppermute | solution.py:212
  10.2 5.4 %collective-permute-done.7 = bf16[8,27,128]{2,0,1:T(8,128)(2,1)S(1)} collective-permute-done((bf16[8,27,128]{2,0,1:T(8,128)(2,1)}, bf16[8,27,128]{2,0,1:T(8,128)(2,1)S(1)}, u32[]{:S(2)}, u32[]{:S(2)}) %collective-permute-start.7) | collective-permute-done | bytes 55328 | tf_op jit(solution)/shard_map/ppermute | solution.py:212
  15.6 1.5 pad_maximum_fusion.4
  17.1 0.0 reduce-scatter.4.cloned.1.call-start
  17.1 0.7 convert_element_type.53
  17.8 0.8 fusion.27
  18.6 0.8 fusion.22
  19.5 0.9 multiply_convert_fusion.1
  20.4 3.0 %collective-permute-start = (bf16[288,128]{1,0:T(8,128)(2,1)S(1)}, bf16[288,128]{1,0:T(8,128)(2,1)S(1)}, u32[]{:S(2)}, u32[]{:S(2)}) collective-permute-start(bf16[288,128]{1,0:T(8,128)(2,1)S(1)} %pad_maximum_fusion.5), channel_id=1, source_target_pairs={{0,65},{1,64},{2,128},{3,192},{64,1},{65,130},{66,129},{67,193},{1... | collective-permute-start | bytes 221192 | tf_op jit(solution)/shard_map/ppermute | solution.py:212
  23.5 3.1 %collective-permute-start.1 = (bf16[288,128]{1,0:T(8,128)(2,1)S(1)}, bf16[288,128]{1,0:T(8,128)(2,1)S(1)}, u32[]{:S(2)}, u32[]{:S(2)}) collective-permute-start(bf16[288,128]{1,0:T(8,128)(2,1)S(1)} %pad_maximum_fusion.5), channel_id=1, source_target_pairs={{0,3},{1,67},{2,131},{3,195},{64,0},{65,64},{66,128},{67,192},{128... | collective-permute-start | bytes 221192 | tf_op jit(solution)/shard_map/ppermute | solution.py:212
  26.6 0.6 collective-permute-start.3
  27.1 7.2 %collective-permute-done = bf16[288,128]{1,0:T(8,128)(2,1)S(1)} collective-permute-done((bf16[288,128]{1,0:T(8,128)(2,1)S(1)}, bf16[288,128]{1,0:T(8,128)(2,1)S(1)}, u32[]{:S(2)}, u32[]{:S(2)}) %collective-permute-start) | collective-permute-done | bytes 73760 | tf_op jit(solution)/shard_map/ppermute | solution.py:212
  34.4 0.5 collective-permute-done.3
  34.9 0.1 fusion.31
  34.9 5.9 %collective-permute-start.5 = (bf16[4,288,128]{2,1,0:T(8,128)(2,1)S(1)}, bf16[4,288,128]{2,1,0:T(8,128)(2,1)S(1)}, u32[]{:S(2)}, u32[]{:S(2)}) collective-permute-start(bf16[4,288,128]{2,1,0:T(8,128)(2,1)S(1)} %get-tuple-element.48.mine), channel_id=1, source_target_pairs={{0,56},{8,0},{16,8},{24,16},{32,24},{40,32},{48,40},{56,48},{1,57}... | collective-permute-start | bytes 884744 | tf_op jit(solution)/shard_map/ppermute | solution.py:222
  40.9 7.5 %collective-permute-done.5.after = bf16[4,288,128]{2,1,0:T(8,128)(2,1)S(1)} collective-permute-done((bf16[4,288,128]{2,1,0:T(8,128)(2,1)S(1)}, bf16[4,288,128]{2,1,0:T(8,128)(2,1)S(1)}, u32[]{:S(2)}, u32[]{:S(2)}) %collective-permute-start.5) | collective-permute-done | bytes 294944 | tf_op jit(solution)/shard_map/ppermute | solution.py:222
  48.4 4.1 %collective-permute-done.4.before = bf16[4,288,128]{2,1,0:T(8,128)(2,1)S(1)} collective-permute-done((bf16[4,288,128]{2,1,0:T(8,128)(2,1)S(1)}, bf16[4,288,128]{2,1,0:T(8,128)(2,1)S(1)}, u32[]{:S(2)}, u32[]{:S(2)}) %collective-permute-start.4) | collective-permute-done | bytes 294944 | tf_op jit(solution)/shard_map/ppermute | solution.py:221
  52.5 0.1 pad_maximum_fusion
  52.6 0.1 collective-permute-start.6
  52.7 0.1 stack.88.ids
  52.8 1.9 %collective-permute-done.6.other = bf16[2,4,288,128]{3,2,1,0:T(8,128)(2,1)S(1)} collective-permute-done((bf16[2,4,288,128]{3,2,1,0:T(8,128)(2,1)S(1)}, bf16[2,4,288,128]{3,2,1,0:T(8,128)(2,1)S(1)}, u32[]{:S(2)}, u32[]{:S(2)}) %collective-permute-start.6) | collective-permute-done | bytes 589856 | tf_op jit(solution)/shard_map/ppermute | solution.py:224
  54.7 0.8 copy-done.7
  55.5 7.4 %shard_map.210 = (bf16[8,9,96,128]{3,2,1,0:T(8,128)(2,1)}, bf16[8,9,96,128]{3,2,1,0:T(8,128)(2,1)}, bf16[4,128,128]{2,1,0:T(8,128)(2,1)S(1)}, bf16[4,32,128]{2,1,0:T(8,128)(2,1)S(1)}) custom-call(s32[5]{0:T(128)S(1)} %stack.88.ids, bf16[4,288,128]{2,1,0:T(8,128)(2,1)S(1)} %get-tuple-element.48.mine, bf16[4,288,128]{2,1,0:T(8,128)(2,1)S(1)} %collective-permute-done.4.before, ...), custom_call_target="tpu_custom_call" | custom-call | tf_op jit(solution)/shard_map/pallas_call | solution.py:196
  62.9 4.5 %shard_map.211 = f32[4,256,128]{2,1,0:T(8,128)S(1)} custom-call(s32[5]{0:T(128)S(1)} %stack.88.ids, bf16[8,9,96,128]{3,2,1,0:T(8,128)(2,1)} %get-tuple-element.22.q_in, bf16[8,9,96,128]{3,2,1,0:T(8,128)(2,1)} %get-tuple-element.23.q_back, bf16[2,27,128,128]{3,2,1,0:T(8,128)(2,1)} %bitcast.66), custom_call_target="tpu_custom_call" | custom-call | tf_op jit(solution)/shard_map/pallas_call | solution.py:196
  67.5 3.8 %collective-permute-start.8 = (f32[256,128]{1,0:T(8,128)S(1)}, f32[256,128]{1,0:T(8,128)S(1)}, u32[]{:S(2)}, u32[]{:S(2)}) collective-permute-start(f32[256,128]{1,0:T(8,128)S(1)} %get-tuple-element.44), channel_id=1, source_target_pairs={{0,64},{64,128},{128,192},{192,0},{1,65},{65,129},{129,193},{193,1... | collective-permute-start | bytes 393224 | tf_op jit(solution)/shard_map/ppermute | solution.py:286
  71.2 1.6 %collective-permute-start.9 = (f32[256,128]{1,0:T(8,128)S(1)}, f32[256,128]{1,0:T(8,128)S(1)}, u32[]{:S(2)}, u32[]{:S(2)}) collective-permute-start(f32[256,128]{1,0:T(8,128)S(1)} %get-tuple-element.46), channel_id=1, source_target_pairs={{0,128},{64,192},{128,0},{192,64},{1,129},{65,193},{129,1},{193,65... | collective-permute-start | bytes 393224 | tf_op jit(solution)/shard_map/ppermute | solution.py:286
  72.8 1.5 collective-permute-done.8
  74.3 6.2 %collective-permute-done.10 = f32[256,128]{1,0:T(8,128)S(1)} collective-permute-done((f32[256,128]{1,0:T(8,128)S(1)}, f32[256,128]{1,0:T(8,128)S(1)}, u32[]{:S(2)}, u32[]{:S(2)}) %collective-permute-start.10) | collective-permute-done | bytes 131104 | tf_op jit(solution)/shard_map/ppermute | solution.py:286
  80.6 0.1 multiply_convert_fusion
  80.7 0.8 collective-permute-start.12
  81.5 0.7 collective-permute-start.11
  82.3 2.5 %collective-permute-start.13 = (bf16[256,128]{1,0:T(8,128)(2,1)S(1)}, bf16[256,128]{1,0:T(8,128)(2,1)S(1)}, u32[]{:S(2)}, u32[]{:S(2)}) collective-permute-start(bf16[256,128]{1,0:T(8,128)(2,1)S(1)} %get-tuple-element.56), channel_id=1, source_target_pairs={{0,64},{64,128},{128,192},{192,0},{1,65},{65,129},{129,193},{193,1... | collective-permute-start | bytes 196616 | tf_op jit(solution)/shard_map/ppermute | solution.py:297
  84.8 2.0 %collective-permute-done.12 = bf16[256,128]{1,0:T(8,128)(2,1)S(1)} collective-permute-done((bf16[256,128]{1,0:T(8,128)(2,1)S(1)}, bf16[256,128]{1,0:T(8,128)(2,1)S(1)}, u32[]{:S(2)}, u32[]{:S(2)}) %collective-permute-start.12) | collective-permute-done | bytes 65568 | tf_op jit(solution)/shard_map/ppermute | solution.py:297
  86.8 0.7 collective-permute-done.11
  87.5 0.4 collective-permute-start.15
  87.8 1.8 %collective-permute-start.14 = (bf16[4,256,128]{2,1,0:T(8,128)(2,1)S(1)}, bf16[4,256,128]{2,1,0:T(8,128)(2,1)S(1)}, u32[]{:S(2)}, u32[]{:S(2)}) collective-permute-start(bf16[4,256,128]{2,1,0:T(8,128)(2,1)S(1)} %get-tuple-element.50.mine), channel_id=1, source_target_pairs={{0,8},{8,16},{16,24},{24,32},{32,40},{40,48},{48,56},{56,0},{1,9},... | collective-permute-start | bytes 786440 | tf_op jit(solution)/shard_map/ppermute | solution.py:221
  89.6 3.9 %shard_map.212 = (f32[8,27,8,128]{3,2,1,0:T(8,128)S(1)}, f32[8,27,8,128]{3,2,1,0:T(8,128)}) custom-call(s32[5]{0:T(128)S(1)} %stack.88.ids, bf16[4,256,128]{2,1,0:T(8,128)(2,1)S(1)} %get-tuple-element.50.mine, bf16[8,9,96,128]{3,2,1,0:T(8,128)(2,1)} %get-tuple-element.22.q_in), custom_call_target="tpu_custom_call" | custom-call | tf_op jit(solution)/shard_map/pallas_call | solution.py:196
  93.5 0.4 collective-permute-done.15.after
  93.9 1.5 collective-permute-done.14.before
  95.5 0.1 pad_maximum_fusion.1
  95.5 0.1 collective-permute-start.16
  95.6 0.6 collective-permute-done.17
  96.2 1.0 add.67
  97.2 0.3 collective-permute-done.16.other
  97.5 0.8 copy-done.6
  98.3 6.7 %shard_map.213 = (f32[8,27,8,128]{3,2,1,0:T(8,128)}, f32[8,27,8,128]{3,2,1,0:T(8,128)}, bf16[8,9,96,128]{3,2,1,0:T(8,128)(2,1)}) custom-call(s32[5]{0:T(128)S(1)} %stack.88.ids, bf16[4,256,128]{2,1,0:T(8,128)(2,1)S(1)} %get-tuple-element.50.mine, bf16[4,256,128]{2,1,0:T(8,128)(2,1)S(1)} %collective-permute-done.14.before, ...), custom_call_target="tpu_custom_call" | custom-call | tf_op jit(solution)/shard_map/pallas_call | solution.py:196
  105.0 0.2 collective-permute-start.18
  105.2 2.5 %collective-permute-done.18 = f32[8,27,8,128]{3,2,1,0:T(8,128)S(1)} collective-permute-done((f32[8,27,8,128]{3,2,1,0:T(8,128)}, f32[8,27,8,128]{3,2,1,0:T(8,128)S(1)}, u32[]{:S(2)}, u32[]{:S(2)}) %collective-permute-start.18) | collective-permute-done | bytes 884768 | tf_op jit(solution)/shard_map/ppermute | solution.py:304
  107.7 2.1 %fusion = bf16[8,216,128]{2,1,0:T(8,128)(2,1)} fusion(f32[8,27,8,128]{3,2,1,0:T(8,128)} %get-tuple-element.32, f32[8,27,8,128]{3,2,1,0:T(8,128)S(1)} %collective-permute-done.18), kind=kLoop, calls=%fused_computation.4 | loop fusion | flops 442368 | bytes 2211840 | tf_op jit(solution)/shard_map/reshape | solution.py:322
  109.7 3.5 %all-to-all-start = ((bf16[8,216,128]{2,1,0:T(8,128)(2,1)}), bf16[8,216,128]{2,1,0:T(8,128)(2,1)S(1)}, u32[]{:S(2)}, u32[]{:S(2)}) async-start(bf16[8,216,128]{2,1,0:T(8,128)(2,1)} %fusion), calls=%async_computation | async-start | bytes 884736 | tf_op jit(solution)/shard_map/all_to_all | solution.py:324
  113.2 8.2 %shard_map.214 = f32[4,256,128]{2,1,0:T(8,128)} custom-call(s32[5]{0:T(128)S(1)} %stack.88.ids, bf16[4,256,128]{2,1,0:T(8,128)(2,1)S(1)} %get-tuple-element.50.mine, bf16[4,256,128]{2,1,0:T(8,128)(2,1)S(1)} %collective-permute-done.14.before, bf16[4,256,128]{2,1,0:T(8,128)(2,1)S(1)} %collective-permute-done.15.after, bf16[2,4,256,128]{3,2,1,0:T(8,128)(2,1)} %copy-done.6, ...), custom_call_target="tpu_custom_call" | custom-call | tf_op jit(solution)/shard_map/pallas_call | solution.py:196
  121.4 1.1 slice_bitcast_fusion
  122.6 1.1 collective-permute-start.22
  123.7 2.0 %collective-permute-start.21 = (f32[256,128]{1,0:T(8,128)S(1)}, f32[256,128]{1,0:T(8,128)S(1)}, u32[]{:S(2)}, u32[]{:S(2)}) collective-permute-start(f32[256,128]{1,0:T(8,128)S(1)} %get-tuple-element.41), channel_id=1, source_target_pairs={{0,128},{1,192},{2,0},{3,64},{64,129},{65,193},{66,1},{67,65},{128... | collective-permute-start | bytes 393224 | tf_op jit(solution)/shard_map/ppermute | solution.py:212
  125.7 4.6 %collective-permute-start.20 = (f32[256,128]{1,0:T(8,128)S(1)}, f32[256,128]{1,0:T(8,128)S(1)}, u32[]{:S(2)}, u32[]{:S(2)}) collective-permute-start(f32[256,128]{1,0:T(8,128)S(1)} %get-tuple-element.42), channel_id=1, source_target_pairs={{0,64},{1,128},{2,192},{3,0},{64,65},{65,129},{66,193},{67,1},{128... | collective-permute-start | bytes 393224 | tf_op jit(solution)/shard_map/ppermute | solution.py:212
  130.3 1.0 collective-permute-start.19
  131.3 0.1 convert_reduce_fusion
  131.3 4.5 %collective-permute-start.23 = (f32[27,8,128]{2,1,0:T(8,128)S(1)}, f32[27,8,128]{2,1,0:T(8,128)S(1)}, u32[]{:S(2)}, u32[]{:S(2)}) collective-permute-start(f32[27,8,128]{2,1,0:T(8,128)S(1)} %bitcast.68), channel_id=1, source_target_pairs={{0,65},{1,64},{2,128},{3,192},{64,1},{65,130},{66,129},{67,193},{1... | collective-permute-start | bytes 331784 | tf_op jit(solution)/shard_map/ppermute | solution.py:212
  135.8 2.4 %collective-permute-done.20 = f32[256,128]{1,0:T(8,128)S(1)} collective-permute-done((f32[256,128]{1,0:T(8,128)S(1)}, f32[256,128]{1,0:T(8,128)S(1)}, u32[]{:S(2)}, u32[]{:S(2)}) %collective-permute-start.20) | collective-permute-done | bytes 131104 | tf_op jit(solution)/shard_map/ppermute | solution.py:212
  138.1 4.7 %collective-permute-done.19 = f32[256,128]{1,0:T(8,128)S(1)} collective-permute-done((f32[256,128]{1,0:T(8,128)S(1)}, f32[256,128]{1,0:T(8,128)S(1)}, u32[]{:S(2)}, u32[]{:S(2)}) %collective-permute-start.19) | collective-permute-done | bytes 131104 | tf_op jit(solution)/shard_map/ppermute | solution.py:212
  142.8 0.9 add_add_fusion
  143.7 0.7 fusion.4
  144.5 0.1 collective-permute-done.23
  144.6 0.7 select_bitcast_fusion.2
  (40 shorter events, 0.4 us)
Async XLA Ops:
  7.2 55.8 %all-gather.2.cloned.1.call-start = ((), (), s32[]{:S(2)}) async-start(), calls=%async_computation.2 | async-start | bytes 1880064 | tf_op jit(solution)/shard_map/all_gather | solution.py:238
  7.2 8.4 %collective-permute-start.7 = (bf16[8,27,128]{2,0,1:T(8,128)(2,1)}, bf16[8,27,128]{2,0,1:T(8,128)(2,1)S(1)}, u32[]{:S(2)}, u32[]{:S(2)}) collective-permute-start(bf16[8,27,128]{2,0,1:T(8,128)(2,1)} %param.23), channel_id=1, source_target_pairs={{0,65},{1,64},{2,128},{3,192},{64,1},{65,130},{66,129},{67,193},{1... | collective-permute-start | bytes 165896 | tf_op jit(solution)/shard_map/ppermute | solution.py:212
  17.1 128.2 %reduce-scatter.4.cloned.1.call-start = ((), (), s32[]{:S(2)}) async-start(), calls=%async_computation.3 | async-start | bytes 995328
  19.4 36.1 %copy-start = (bf16[864,224]{1,0:T(8,128)(2,1)S(1)}, bf16[864,224]{1,0:T(8,128)(2,1)}, u32[]{:S(2)}) copy-start(bf16[864,224]{1,0:T(8,128)(2,1)} %constant.72.clone.spread) | copy-start | bytes 1161220
  19.4 36.1 %copy-start.1 = (bf16[32,2048]{1,0:T(8,128)(2,1)S(1)}, bf16[32,2048]{1,0:T(8,128)(2,1)}, u32[]{:S(2)}) copy-start(bf16[32,2048]{1,0:T(8,128)(2,1)} %constant.73.clone.lanes) | copy-start | bytes 393220
  19.4 36.1 %copy-start.2 = (f32[224,128]{1,0:T(8,128)S(1)}, f32[224,128]{1,0:T(8,128)}, u32[]{:S(2)}) copy-start(f32[224,128]{1,0:T(8,128)} %constant.71.clone.local) | copy-start | bytes 344068
  19.4 36.1 %copy-start.3 = (bf16[224,32]{1,0:T(8,128)(2,1)S(1)}, bf16[224,32]{1,0:T(8,128)(2,1)}, u32[]{:S(2)}) copy-start(bf16[224,32]{1,0:T(8,128)(2,1)} %constant.70.clone.pick_back) | copy-start | bytes 43012
  19.5 36.1 %copy-start.4 = (bf16[224,32]{1,0:T(8,128)(2,1)S(1)}, bf16[224,32]{1,0:T(8,128)(2,1)}, u32[]{:S(2)}) copy-start(bf16[224,32]{1,0:T(8,128)(2,1)} %constant.69.clone.pick) | copy-start | bytes 43012
  19.5 36.1 %copy-start.5 = (bf16[16,128]{1,0:T(8,128)(2,1)S(1)}, bf16[16,128]{1,0:T(8,128)(2,1)}, u32[]{:S(2)}) copy-start(bf16[16,128]{1,0:T(8,128)(2,1)} %constant.74.clone.sources) | copy-start | bytes 12292
  20.4 13.9 %collective-permute-start = (bf16[288,128]{1,0:T(8,128)(2,1)S(1)}, bf16[288,128]{1,0:T(8,128)(2,1)S(1)}, u32[]{:S(2)}, u32[]{:S(2)}) collective-permute-start(bf16[288,128]{1,0:T(8,128)(2,1)S(1)} %pad_maximum_fusion.5), channel_id=1, source_target_pairs={{0,65},{1,64},{2,128},{3,192},{64,1},{65,130},{66,129},{67,193},{1... | collective-permute-start | bytes 221192 | tf_op jit(solution)/shard_map/ppermute | solution.py:212
  23.5 10.9 %collective-permute-start.2 = (bf16[288,128]{1,0:T(8,128)(2,1)S(1)}, bf16[288,128]{1,0:T(8,128)(2,1)S(1)}, u32[]{:S(2)}, u32[]{:S(2)}) collective-permute-start(bf16[288,128]{1,0:T(8,128)(2,1)S(1)} %pad_maximum_fusion.5), channel_id=1, source_target_pairs={{0,2},{1,66},{2,130},{3,194},{64,3},{65,67},{66,131},{67,195},{128... | collective-permute-start | bytes 221192 | tf_op jit(solution)/shard_map/ppermute | solution.py:212
  23.5 10.9 %collective-permute-start.1 = (bf16[288,128]{1,0:T(8,128)(2,1)S(1)}, bf16[288,128]{1,0:T(8,128)(2,1)S(1)}, u32[]{:S(2)}, u32[]{:S(2)}) collective-permute-start(bf16[288,128]{1,0:T(8,128)(2,1)S(1)} %pad_maximum_fusion.5), channel_id=1, source_target_pairs={{0,3},{1,67},{2,131},{3,195},{64,0},{65,64},{66,128},{67,192},{128... | collective-permute-start | bytes 221192 | tf_op jit(solution)/shard_map/ppermute | solution.py:212
  26.6 8.3 %collective-permute-start.3 = (bf16[288,128]{1,0:T(8,128)(2,1)S(1)}, bf16[288,128]{1,0:T(8,128)(2,1)S(1)}, u32[]{:S(2)}, u32[]{:S(2)}) collective-permute-start(bf16[288,128]{1,0:T(8,128)(2,1)S(1)} %pad_maximum_fusion.5), channel_id=1, source_target_pairs={{0,1},{1,65},{2,129},{3,193},{64,2},{65,66},{66,130},{67,194},{128... | collective-permute-start | bytes 221192 | tf_op jit(solution)/shard_map/ppermute | solution.py:212
  34.9 13.5 %collective-permute-start.5 = (bf16[4,288,128]{2,1,0:T(8,128)(2,1)S(1)}, bf16[4,288,128]{2,1,0:T(8,128)(2,1)S(1)}, u32[]{:S(2)}, u32[]{:S(2)}) collective-permute-start(bf16[4,288,128]{2,1,0:T(8,128)(2,1)S(1)} %get-tuple-element.48.mine), channel_id=1, source_target_pairs={{0,56},{8,0},{16,8},{24,16},{32,24},{40,32},{48,40},{56,48},{1,57}... | collective-permute-start | bytes 884744 | tf_op jit(solution)/shard_map/ppermute | solution.py:222
  40.9 11.6 %collective-permute-start.4 = (bf16[4,288,128]{2,1,0:T(8,128)(2,1)S(1)}, bf16[4,288,128]{2,1,0:T(8,128)(2,1)S(1)}, u32[]{:S(2)}, u32[]{:S(2)}) collective-permute-start(bf16[4,288,128]{2,1,0:T(8,128)(2,1)S(1)} %get-tuple-element.48.mine), channel_id=1, source_target_pairs={{0,8},{8,16},{16,24},{24,32},{32,40},{40,48},{48,56},{56,0},{1,9},... | collective-permute-start | bytes 884744 | tf_op jit(solution)/shard_map/ppermute | solution.py:221
  52.6 2.1 %collective-permute-start.6 = (bf16[2,4,288,128]{3,2,1,0:T(8,128)(2,1)S(1)}, bf16[2,4,288,128]{3,2,1,0:T(8,128)(2,1)S(1)}, u32[]{:S(2)}, u32[]{:S(2)}) collective-permute-start(bf16[2,4,288,128]{3,2,1,0:T(8,128)(2,1)S(1)} %pad_maximum_fusion), channel_id=1, source_target_pairs={{0,4},{4,0},{1,5},{5,1},{2,6},{6,2},{3,7},{7,3},{8,12},{12,8},{9,1... | collective-permute-start | bytes 1769480 | tf_op jit(solution)/shard_map/ppermute | solution.py:224
  54.7 0.8 copy-start.7
  67.5 6.8 %collective-permute-start.8 = (f32[256,128]{1,0:T(8,128)S(1)}, f32[256,128]{1,0:T(8,128)S(1)}, u32[]{:S(2)}, u32[]{:S(2)}) collective-permute-start(f32[256,128]{1,0:T(8,128)S(1)} %get-tuple-element.44), channel_id=1, source_target_pairs={{0,64},{64,128},{128,192},{192,0},{1,65},{65,129},{129,193},{193,1... | collective-permute-start | bytes 393224 | tf_op jit(solution)/shard_map/ppermute | solution.py:286
  71.2 9.3 %collective-permute-start.10 = (f32[256,128]{1,0:T(8,128)S(1)}, f32[256,128]{1,0:T(8,128)S(1)}, u32[]{:S(2)}, u32[]{:S(2)}) collective-permute-start(f32[256,128]{1,0:T(8,128)S(1)} %get-tuple-element.45), channel_id=1, source_target_pairs={{0,192},{64,0},{128,64},{192,128},{1,193},{65,1},{129,65},{193,129... | collective-permute-start | bytes 393224 | tf_op jit(solution)/shard_map/ppermute | solution.py:286
  71.2 9.3 %collective-permute-start.9 = (f32[256,128]{1,0:T(8,128)S(1)}, f32[256,128]{1,0:T(8,128)S(1)}, u32[]{:S(2)}, u32[]{:S(2)}) collective-permute-start(f32[256,128]{1,0:T(8,128)S(1)} %get-tuple-element.46), channel_id=1, source_target_pairs={{0,128},{64,192},{128,0},{192,64},{1,129},{65,193},{129,1},{193,65... | collective-permute-start | bytes 393224 | tf_op jit(solution)/shard_map/ppermute | solution.py:286
  80.7 6.1 %collective-permute-start.12 = (bf16[256,128]{1,0:T(8,128)(2,1)S(1)}, bf16[256,128]{1,0:T(8,128)(2,1)S(1)}, u32[]{:S(2)}, u32[]{:S(2)}) collective-permute-start(bf16[256,128]{1,0:T(8,128)(2,1)S(1)} %get-tuple-element.56), channel_id=1, source_target_pairs={{0,128},{64,192},{128,0},{192,64},{1,129},{65,193},{129,1},{193,65... | collective-permute-start | bytes 196616 | tf_op jit(solution)/shard_map/ppermute | solution.py:297
  81.5 5.9 %collective-permute-start.11 = (bf16[256,128]{1,0:T(8,128)(2,1)S(1)}, bf16[256,128]{1,0:T(8,128)(2,1)S(1)}, u32[]{:S(2)}, u32[]{:S(2)}) collective-permute-start(bf16[256,128]{1,0:T(8,128)(2,1)S(1)} %get-tuple-element.56), channel_id=1, source_target_pairs={{0,192},{64,0},{128,64},{192,128},{1,193},{65,1},{129,65},{193,129... | collective-permute-start | bytes 196616 | tf_op jit(solution)/shard_map/ppermute | solution.py:297
  82.3 5.2 %collective-permute-start.13 = (bf16[256,128]{1,0:T(8,128)(2,1)S(1)}, bf16[256,128]{1,0:T(8,128)(2,1)S(1)}, u32[]{:S(2)}, u32[]{:S(2)}) collective-permute-start(bf16[256,128]{1,0:T(8,128)(2,1)S(1)} %get-tuple-element.56), channel_id=1, source_target_pairs={{0,64},{64,128},{128,192},{192,0},{1,65},{65,129},{129,193},{193,1... | collective-permute-start | bytes 196616 | tf_op jit(solution)/shard_map/ppermute | solution.py:297
  87.5 6.5 %collective-permute-start.15 = (bf16[4,256,128]{2,1,0:T(8,128)(2,1)S(1)}, bf16[4,256,128]{2,1,0:T(8,128)(2,1)S(1)}, u32[]{:S(2)}, u32[]{:S(2)}) collective-permute-start(bf16[4,256,128]{2,1,0:T(8,128)(2,1)S(1)} %get-tuple-element.50.mine), channel_id=1, source_target_pairs={{0,56},{8,0},{16,8},{24,16},{32,24},{40,32},{48,40},{56,48},{1,57}... | collective-permute-start | bytes 786440 | tf_op jit(solution)/shard_map/ppermute | solution.py:222
  87.8 7.6 %collective-permute-start.14 = (bf16[4,256,128]{2,1,0:T(8,128)(2,1)S(1)}, bf16[4,256,128]{2,1,0:T(8,128)(2,1)S(1)}, u32[]{:S(2)}, u32[]{:S(2)}) collective-permute-start(bf16[4,256,128]{2,1,0:T(8,128)(2,1)S(1)} %get-tuple-element.50.mine), channel_id=1, source_target_pairs={{0,8},{8,16},{16,24},{24,32},{32,40},{40,48},{48,56},{56,0},{1,9},... | collective-permute-start | bytes 786440 | tf_op jit(solution)/shard_map/ppermute | solution.py:221
  93.5 2.6 %collective-permute-start.17 = (f32[8,27,8,128]{3,2,1,0:T(8,128)}, f32[8,27,8,128]{3,2,1,0:T(8,128)S(1)}, u32[]{:S(2)}, u32[]{:S(2)}) collective-permute-start(f32[8,27,8,128]{3,2,1,0:T(8,128)} %get-tuple-element.25), channel_id=1, source_target_pairs={{0,4},{4,0},{1,5},{5,1},{2,6},{6,2},{3,7},{7,3},{8,12},{12,8},{9,1... | collective-permute-start | bytes 2654216 | tf_op jit(solution)/shard_map/ppermute | solution.py:304
  95.5 2.0 %collective-permute-start.16 = (bf16[2,4,256,128]{3,2,1,0:T(8,128)(2,1)S(1)}, bf16[2,4,256,128]{3,2,1,0:T(8,128)(2,1)S(1)}, u32[]{:S(2)}, u32[]{:S(2)}) collective-permute-start(bf16[2,4,256,128]{3,2,1,0:T(8,128)(2,1)S(1)} %pad_maximum_fusion.1), channel_id=1, source_target_pairs={{0,4},{4,0},{1,5},{5,1},{2,6},{6,2},{3,7},{7,3},{8,12},{12,8},{9,1... | collective-permute-start | bytes 1572872 | tf_op jit(solution)/shard_map/ppermute | solution.py:224
  97.5 0.8 copy-start.6
  105.0 2.6 %collective-permute-start.18 = (f32[8,27,8,128]{3,2,1,0:T(8,128)}, f32[8,27,8,128]{3,2,1,0:T(8,128)S(1)}, u32[]{:S(2)}, u32[]{:S(2)}) collective-permute-start(f32[8,27,8,128]{3,2,1,0:T(8,128)} %get-tuple-element.33), channel_id=1, source_target_pairs={{0,4},{4,0},{1,5},{5,1},{2,6},{6,2},{3,7},{7,3},{8,12},{12,8},{9,1... | collective-permute-start | bytes 2654216 | tf_op jit(solution)/shard_map/ppermute | solution.py:304
  109.7 21.5 %all-to-all-start = ((bf16[8,216,128]{2,1,0:T(8,128)(2,1)}), bf16[8,216,128]{2,1,0:T(8,128)(2,1)S(1)}, u32[]{:S(2)}, u32[]{:S(2)}) async-start(bf16[8,216,128]{2,1,0:T(8,128)(2,1)} %fusion), calls=%async_computation | async-start | bytes 884736 | tf_op jit(solution)/shard_map/all_to_all | solution.py:324
  122.6 13.2 %collective-permute-start.22 = (f32[256,128]{1,0:T(8,128)S(1)}, f32[256,128]{1,0:T(8,128)S(1)}, u32[]{:S(2)}, u32[]{:S(2)}) collective-permute-start(f32[256,128]{1,0:T(8,128)S(1)} %get-tuple-element.40), channel_id=1, source_target_pairs={{0,192},{1,0},{2,64},{3,128},{64,193},{65,1},{66,65},{67,129},{128... | collective-permute-start | bytes 393224 | tf_op jit(solution)/shard_map/ppermute | solution.py:212
  123.7 12.1 %collective-permute-start.21 = (f32[256,128]{1,0:T(8,128)S(1)}, f32[256,128]{1,0:T(8,128)S(1)}, u32[]{:S(2)}, u32[]{:S(2)}) collective-permute-start(f32[256,128]{1,0:T(8,128)S(1)} %get-tuple-element.41), channel_id=1, source_target_pairs={{0,128},{1,192},{2,0},{3,64},{64,129},{65,193},{66,1},{67,65},{128... | collective-permute-start | bytes 393224 | tf_op jit(solution)/shard_map/ppermute | solution.py:212
  125.7 12.4 %collective-permute-start.20 = (f32[256,128]{1,0:T(8,128)S(1)}, f32[256,128]{1,0:T(8,128)S(1)}, u32[]{:S(2)}, u32[]{:S(2)}) collective-permute-start(f32[256,128]{1,0:T(8,128)S(1)} %get-tuple-element.42), channel_id=1, source_target_pairs={{0,64},{1,128},{2,192},{3,0},{64,65},{65,129},{66,193},{67,1},{128... | collective-permute-start | bytes 393224 | tf_op jit(solution)/shard_map/ppermute | solution.py:212
  130.3 12.5 %collective-permute-start.19 = (f32[256,128]{1,0:T(8,128)S(1)}, f32[256,128]{1,0:T(8,128)S(1)}, u32[]{:S(2)}, u32[]{:S(2)}) collective-permute-start(f32[256,128]{1,0:T(8,128)S(1)} %get-tuple-element.43), channel_id=1, source_target_pairs={{0,65},{1,64},{2,128},{3,192},{64,1},{65,130},{66,129},{67,193},{1... | collective-permute-start | bytes 393224 | tf_op jit(solution)/shard_map/ppermute | solution.py:212
  131.3 13.3 %collective-permute-start.23 = (f32[27,8,128]{2,1,0:T(8,128)S(1)}, f32[27,8,128]{2,1,0:T(8,128)S(1)}, u32[]{:S(2)}, u32[]{:S(2)}) collective-permute-start(f32[27,8,128]{2,1,0:T(8,128)S(1)} %bitcast.68), channel_id=1, source_target_pairs={{0,65},{1,64},{2,128},{3,192},{64,1},{65,130},{66,129},{67,193},{1... | collective-permute-start | bytes 331784 | tf_op jit(solution)/shard_map/ppermute | solution.py:212
Sparse Core Ops, SparseCore 0:
  17.2 43.0 all-gather.1
  105.3 36.8 reduce-scatter.3
